TPU v7x, 512 devices: a whole 4x4x16 slice. The times are simulated.
512 devices in a mesh: seq: 32 (over z, core), head: 16 (over x, y).
Axes of the slice: x: 4, y: 4, z: 16, core: 2. Of those that a mesh axis runs over, the one named last changes fastest.
Arguments:
- tokens: bfloat16 [8192, 4096], P('seq', 'head'), may hold values from -40 to 40
- norm_gain: float32 [4096], replicated, may hold values from 1.5 to 8
- w_qkv: bfloat16 [4096, 3, 2048], P(None, None, 'head'), may hold values from -0.09375 to 0.09375
- w_out: bfloat16 [2048, 4096], P('head'), may hold values from -0.75 to 0.75
- span_order: int32 [64], replicated, may hold values from 0 to 63, each once
- frame_id: int32 [8192], replicated, may hold values from 0 to 63, never falling along the last dimension, each value on 1 to 256 neighbouring positions
- camera_id: int32 [8192], replicated, may hold values from 0 to 5
Outputs:
- mixed: bfloat16 [8192, 4096], P('seq', 'head')
Inputs may be any that keep to these rules, and one draw needn't show every extreme that they name: `span_order`: each of the 64 spans appears once. `frame_id`: never falls along the sequence; every frame has 1 to 256 positions and one has exactly 256.
All inputs are finite; a program needn't handle non-finite values.
Results may differ from a plain program's by a relative error of at most 0.015.
The roundings to bfloat16 on the way count: a program that leaves them out, or rounds other values in their place, can miss the bound.
Values may be sent and summed in bfloat16 or wider, within the bound.
No kernel may reach another device: no remote copies, remote signals or barrier semaphores. Data moves between devices by JAX's collectives and lax.ppermute only.
A program may use at most 64 MiB of HBM per device.

v0:
```python
import math

import jax
import jax.numpy as jnp
from jax import lax
from jax.experimental import pallas as pl
from jax.experimental.pallas import tpu as pltpu
from jax.sharding import PartitionSpec as P


D = 4096
HD = 128
ROWS = 256
SPAN = 128
CORES = 2
BLOCK_Z = 4
GRANT = 16 << 20
MASKED = -1e30
EPSILON = 1e-06
LOG2_E = 1.4426950408889634
SCALE = HD**-0.5 * LOG2_E
PART_ROWS = HD + 16


def project_kernel(x_ref, gain_ref, w_ref, q_ref, kv_ref, inv_ref, acc_ref):
    step = pl.program_id(0)
    blocks = x_ref.shape[0]
    per_step = blocks // pl.num_programs(0)

    @pl.when(step == 0)
    def _():
        total = jnp.zeros((ROWS, x_ref.shape[2]), jnp.float32)
        for j in range(blocks):
            piece = x_ref[j].astype(jnp.float32)
            total = total + piece * piece
        mean = jnp.sum(total, axis=1, keepdims=True) * (1.0 / D)
        inv_ref[...] = jnp.broadcast_to(lax.rsqrt(mean + EPSILON), inv_ref.shape)
        acc_ref[...] = jnp.zeros_like(acc_ref)

    width = x_ref.shape[2]
    inverse = jnp.concatenate([inv_ref[...]] * (width // 128), axis=1)
    sums = acc_ref[...]
    for i in range(per_step):
        piece = x_ref[step * per_step + i].astype(jnp.float32)
        gain = gain_ref[:, i * width : (i + 1) * width]
        normed = (piece * inverse * gain).astype(jnp.bfloat16)
        rows = slice(i * width, (i + 1) * width)
        weights = jnp.concatenate([w_ref[0, rows], w_ref[1, rows], w_ref[2, rows]], axis=1)
        sums = sums + jnp.dot(normed, weights, preferred_element_type=jnp.float32)
    acc_ref[...] = sums

    @pl.when(step == pl.num_programs(0) - 1)
    def _():
        done = sums.astype(jnp.bfloat16)
        q_ref[...] = done[:, :HD]
        for j in range(kv_ref.shape[0]):
            kv_ref[j] = done[:, HD:]


def project(x, gain, w, copies):
    blocks, _, width = x.shape
    steps = 4
    depth = D // steps
    return pl.pallas_call(
        project_kernel,
        grid=(steps,),
        in_specs=[
            pl.BlockSpec((blocks, ROWS, width), lambda s: (0, 0, 0)),
            pl.BlockSpec((1, depth), lambda s: (0, s)),
            pl.BlockSpec((3, depth, HD), lambda s: (0, s, 0)),
        ],
        out_specs=[
            pl.BlockSpec((ROWS, HD), lambda s: (0, 0)),
            pl.BlockSpec((copies, ROWS, 2 * HD), lambda s: (0, 0, 0)),
        ],
        out_shape=[
            jax.ShapeDtypeStruct((ROWS, HD), jnp.bfloat16),
            jax.ShapeDtypeStruct((copies, ROWS, 2 * HD), jnp.bfloat16),
        ],
        scratch_shapes=[
            pltpu.VMEM((ROWS, 128), jnp.float32),
            pltpu.VMEM((ROWS, 3 * HD), jnp.float32),
        ],
        compiler_params=pltpu.CompilerParams(vmem_limit_bytes=GRANT),
        name="project",
    )(x, gain, w)


def attend_kernel(q_ref, qcode_ref, own_ref, other_ref, kcode_ref, out_ref, vt_ref):
    count = own_ref.shape[0]

    @pl.when(pl.program_id(0) == 0)
    def _():
        for part, ref in enumerate((own_ref, other_ref)):
            for j in range(count):
                at = (part * count + j) * ROWS
                vt_ref[:, at : at + ROWS] = jnp.transpose(ref[j][:, HD:])

    qcode = qcode_ref[0]
    qbase = qcode & -8
    queries = q_ref[0]
    scores = []
    for part, ref in enumerate((own_ref, other_ref)):
        for j in range(count):
            at = (part * count + j) * ROWS
            raw = lax.dot_general(
                ref[j][:, :HD],
                queries,
                (((1,), (1,)), ((), ())),
                preferred_element_type=jnp.float32,
            )
            code = kcode_ref[at : at + ROWS, :]
            kcode = jnp.concatenate([code] * (ROWS // 128), axis=1)
            seen = (kcode < qbase) | (kcode == qcode)
            scores.append(jnp.where(seen, raw * SCALE, MASKED))
    scores = jnp.concatenate(scores, axis=0)
    best = jnp.max(scores, axis=0, keepdims=True)
    weights = jnp.exp2(scores - best)
    total = jnp.sum(weights, axis=0, keepdims=True)
    mixed = jnp.dot(vt_ref[...], weights.astype(jnp.bfloat16), preferred_element_type=jnp.float32)
    out_ref[0, :HD] = (mixed / total).astype(jnp.bfloat16)
    level = best + jnp.log2(total)
    high = level.astype(jnp.bfloat16).astype(jnp.float32)
    rest = level - high
    middle = rest.astype(jnp.bfloat16).astype(jnp.float32)
    low = rest - middle
    row = lax.broadcasted_iota(jnp.int32, (16, ROWS), 0)
    stats = jnp.where(row == 0, high, jnp.where(row == 1, middle, jnp.where(row == 2, low, 0.0)))
    out_ref[0, HD:] = stats.astype(jnp.bfloat16)


def attend(q, qcode, own_kv, other_kv, kcode):
    groups = q.shape[0]
    keys = kcode.shape[0]
    return pl.pallas_call(
        attend_kernel,
        grid=(groups,),
        in_specs=[
            pl.BlockSpec((1, ROWS, HD), lambda i: (i, 0, 0)),
            pl.BlockSpec((1, 1, ROWS), lambda i: (i, 0, 0)),
            pl.BlockSpec(own_kv.shape, lambda i: (0, 0, 0)),
            pl.BlockSpec(other_kv.shape, lambda i: (0, 0, 0)),
            pl.BlockSpec((keys, 128), lambda i: (0, 0)),
        ],
        out_specs=pl.BlockSpec((1, PART_ROWS, ROWS), lambda i: (i, 0, 0)),
        out_shape=jax.ShapeDtypeStruct((groups, PART_ROWS, ROWS), jnp.bfloat16),
        scratch_shapes=[pltpu.VMEM((HD, keys), jnp.bfloat16)],
        compiler_params=pltpu.CompilerParams(vmem_limit_bytes=GRANT),
        name="attend",
    )(q, qcode, own_kv, other_kv, kcode)


def combine_kernel(part_ref, out_ref):
    groups = part_ref.shape[0]
    levels = []
    for j in range(groups):
        stats = part_ref[j, HD:].astype(jnp.float32)
        levels.append(stats[0:1] + stats[1:2] + stats[2:3])
    best = levels[0]
    for level in levels[1:]:
        best = jnp.maximum(best, level)
    total = jnp.zeros_like(best)
    mixed = jnp.zeros((HD, ROWS), jnp.float32)
    for j in range(groups):
        share = jnp.exp2(levels[j] - best)
        total = total + share
        mixed = mixed + share * part_ref[j, :HD].astype(jnp.float32)
    attended = jnp.transpose(mixed / total).astype(jnp.bfloat16)
    for j in range(out_ref.shape[0]):
        out_ref[j] = attended


def combine(parts, copies):
    return pl.pallas_call(
        combine_kernel,
        out_shape=jax.ShapeDtypeStruct((copies, ROWS, HD), jnp.bfloat16),
        compiler_params=pltpu.CompilerParams(vmem_limit_bytes=GRANT),
        name="combine",
    )(parts)


def take_kernel(place_ref, w_ref, *out_refs):
    side = len(out_refs)
    width = out_refs[0].shape[2]
    for shift, out_ref in enumerate(out_refs):
        y = lax.rem(place_ref[1] + shift, side)
        for x in range(side):
            at = pl.multiple_of((x * side + y) * width, width)
            out_ref[x] = w_ref[:, pl.ds(at, width)]


def take(place, w, side):
    piece = jax.ShapeDtypeStruct((side, HD, w.shape[1] // side**2), w.dtype)
    return pl.pallas_call(
        take_kernel,
        in_specs=[
            pl.BlockSpec(memory_space=pltpu.SMEM),
            pl.BlockSpec(memory_space=pltpu.VMEM),
        ],
        out_shape=[piece] * side,
        compiler_params=pltpu.CompilerParams(vmem_limit_bytes=GRANT),
        name="take",
    )(place, w)


def turn_kernel(place_ref, *refs):
    side = len(refs) // 2
    for shift, out_ref in enumerate(refs[side:]):
        x = lax.rem(place_ref[0] + shift, side)
        for j in range(side):
            out_ref[j] = refs[j][x]


def turn(place, pieces):
    return pl.pallas_call(
        turn_kernel,
        in_specs=[pl.BlockSpec(memory_space=pltpu.SMEM)]
        + [pl.BlockSpec(memory_space=pltpu.VMEM)] * len(pieces),
        out_shape=[jax.ShapeDtypeStruct(p.shape, p.dtype) for p in pieces],
        compiler_params=pltpu.CompilerParams(vmem_limit_bytes=GRANT),
        name="turn",
    )(place, *pieces)


def output_kernel(place_ref, attended_ref, *refs):
    out_ref = refs[-1]
    side = len(refs) - 1
    total = jnp.zeros(out_ref.shape, jnp.float32)
    for k in range(side):
        for j in range(side):
            x = lax.rem(place_ref[0] + (side - k), side)
            y = lax.rem(place_ref[1] + (side - j), side)
            rows = attended_ref[x * side + y]
            head_out = jnp.dot(rows, refs[k][j], preferred_element_type=jnp.float32)
            total = total + head_out.astype(jnp.bfloat16).astype(jnp.float32)
    out_ref[...] = total.astype(jnp.bfloat16)


def output(place, attended, pieces):
    return pl.pallas_call(
        output_kernel,
        in_specs=[pl.BlockSpec(memory_space=pltpu.SMEM)]
        + [pl.BlockSpec(memory_space=pltpu.VMEM)] * (1 + len(pieces)),
        out_shape=jax.ShapeDtypeStruct((ROWS, pieces[0].shape[2]), jnp.bfloat16),
        compiler_params=pltpu.CompilerParams(vmem_limit_bytes=GRANT),
        name="output",
    )(place, attended, *pieces)


def make_on_device(n_seq, n_head):
    group = CORES * BLOCK_Z
    blocks = n_seq // group
    near = [
        [g * group + b * CORES + c for b in range(BLOCK_Z)] for g in range(blocks) for c in range(CORES)
    ]
    far = [[g * group + i for g in range(blocks)] for i in range(group)]
    swap = [(i, i ^ 1) for i in range(n_seq)]
    keys = CORES * blocks * ROWS

    def codes(span_order, frame_id, camera_id):
        code = (frame_id * 8 + camera_id).reshape(-1, SPAN)[span_order]
        code = code.reshape(blocks, BLOCK_Z, CORES, ROWS)
        place = lax.axis_index("seq")
        core = place % CORES
        query_code = lax.dynamic_index_in_dim(code, place // group, 0, keepdims=False)
        query_code = lax.dynamic_index_in_dim(query_code, core, 1, keepdims=False)
        key_code = lax.dynamic_index_in_dim(code, place // CORES % BLOCK_Z, 1, keepdims=False)
        own = lax.dynamic_index_in_dim(key_code, core, 1, keepdims=False)
        other = lax.dynamic_index_in_dim(key_code, 1 - core, 1, keepdims=False)
        key_code = jnp.concatenate([own, other]).reshape(-1, 1)
        return query_code[:, None, :], jnp.broadcast_to(key_code, (keys, 128))

    side = math.isqrt(n_head)
    along_x = [[(i, (i + k * side) % n_head) for i in range(n_head)] for k in range(side)]
    along_y = [
        [(i, i // side * side + (i + k) % side) for i in range(n_head)] for k in range(side)
    ]

    def on_device(tokens, norm_gain, w_qkv, w_out, span_order, frame_id, camera_id):
        head = lax.axis_index("head")
        place = jnp.stack([head // side, head % side]).astype(jnp.int32)
        copies = jnp.broadcast_to(tokens[None], (n_head,) + tokens.shape)
        gathered = lax.all_to_all(copies, "head", 0, 0)
        query_code, key_code = codes(span_order, frame_id, camera_id)
        taken = take(place, w_out, side)
        gathered, taken, query_code, key_code = lax.optimization_barrier(
            (gathered, taken, query_code, key_code)
        )
        queries, kv = project(gathered, norm_gain.reshape(1, D), w_qkv.transpose(1, 0, 2), blocks)
        all_queries = lax.all_gather(queries, "seq", axis_index_groups=near)
        all_queries, kv, taken = lax.optimization_barrier((all_queries, kv, taken))
        own_kv = lax.all_to_all(kv, "seq", 0, 0, axis_index_groups=far)
        taken = [taken[0]] + [lax.ppermute(taken[k], "head", along_y[k]) for k in range(1, side)]
        turned = turn(place, taken)
        w_columns = [turned[0]] + [
            lax.ppermute(turned[k], "head", along_x[k]) for k in range(1, side)
        ]
        other_kv = lax.ppermute(own_kv, "seq", swap)
        parts = attend(all_queries, query_code, own_kv, other_kv, key_code)
        parts = lax.all_to_all(parts, "seq", 0, 0, axis_index_groups=near)
        attended = combine(parts, n_head)
        all_attended = lax.all_to_all(attended, "head", 0, 0)
        return output(place, all_attended, w_columns)

    return on_device


def solution(mesh):
    placed = (P("seq", "head"), P(), P(None, None, "head"), P("head", None), P(), P(), P())
    return jax.shard_map(
        make_on_device(mesh.shape["seq"], mesh.shape["head"]),
        mesh=mesh,
        in_specs=placed,
        out_specs=P("seq", "head"),
        check_vma=False,
    )
```

profile of v0, /device:TPU:6, one launch (start us, length us, event | category | flops | bytes accessed | tf_op | source)
XLA Modules:
  0.0 173.2 jit_solution(5869932918381962125)
XLA Ops:
  0.0 2.4 %broadcast_in_dim.8 = bf16[16,256,256]{2,1,0:T(8,128)(2,1)} broadcast(bf16[256,256]{1,0:T(8,128)(2,1)} %param.7), dimensions={1,2} | broadcast | bytes 2228224 | tf_op jit(solution)/shard_map/broadcast_in_dim | solution.py:282
  2.4 9.5 %all-to-all-start = ((bf16[16,256,256]{2,1,0:T(8,128)(2,1)}), bf16[16,256,256]{2,1,0:T(8,128)(2,1)S(1)}, u32[]{:S(2)}, u32[]{:S(2)}) async-start(bf16[16,256,256]{2,1,0:T(8,128)(2,1)} %broadcast_in_dim.8), calls=%async_computation | async-start | bytes 4194304 | tf_op jit(solution)/shard_map/all_to_all | solution.py:283
  15.8 21.7 %all-to-all-done.x_ref = bf16[16,256,256]{2,1,0:T(8,128)(2,1)S(1)} async-done(((bf16[16,256,256]{2,1,0:T(8,128)(2,1)}), bf16[16,256,256]{2,1,0:T(8,128)(2,1)S(1)}, u32[]{:S(2)}, u32[]{:S(2)}) %all-to-all-start) | async-done | bytes 2097184 | tf_op jit(solution)/shard_map/all_to_all | solution.py:283
  37.8 1.9 %copy-done = bf16[4096,3,128]{2,0,1:T(8,128)(2,1)S(1)} copy-done((bf16[4096,3,128]{2,0,1:T(8,128)(2,1)S(1)}, bf16[4096,3,128]{2,0,1:T(8,128)(2,1)}, u32[]{:S(2)}) %copy-start) | copy-done | bytes 3145752
  39.7 2.5 %project.1 = (bf16[256,128]{1,0:T(8,128)(2,1)S(1)}, bf16[4,256,256]{2,1,0:T(8,128)(2,1)S(1)}) custom-call(bf16[16,256,256]{2,1,0:T(8,128)(2,1)S(1)} %all-to-all-done.x_ref, f32[1,4096]{1,0:T(1,128)S(1)} %bitcast.18, bf16[3,4096,128]{2,1,0:T(8,128)(2,1)S(1)} %bitcast.16), custom_call_target="tpu_custom_call" | custom-call | tf_op jit(solution)/shard_map/project/pallas_call | solution.py:64
  42.2 15.6 %all-gather = bf16[1024,128]{1,0:T(8,128)(2,1)S(1)} all-gather(bf16[256,128]{1,0:T(8,128)(2,1)S(1)} %get-tuple-element.33), channel_id=2, replica_groups={{0,32,64,96},{16,48,80,112},{128,160,192,224},{144,176,208,240},{256,28..., dimensions={0}, use_global_device_ids=true | all-gather | bytes 327680 | tf_op jit(solution)/shard_map/all_gather | solution.py:290
  57.8 39.0 %all_to_all.20.own_ref = bf16[4,256,256]{2,1,0:T(8,128)(2,1)S(1)} all-to-all(bf16[4,256,256]{2,1,0:T(8,128)(2,1)S(1)} %get-tuple-element.41), channel_id=1, replica_groups={{0,128,256,384},{16,144,272,400},{32,160,288,416},{48,176,304,432},{64,..., dimensions={0} | all-to-all | bytes 1048576 | tf_op jit(solution)/shard_map/all_to_all | solution.py:292
  96.8 1.9 %collective-permute-start = (bf16[4,256,256]{2,1,0:T(8,128)(2,1)S(1)}, bf16[4,256,256]{2,1,0:T(8,128)(2,1)S(1)}, u32[]{:S(2)}, u32[]{:S(2)}) collective-permute-start(bf16[4,256,256]{2,1,0:T(8,128)(2,1)S(1)} %all_to_all.20.own_ref), channel_id=1, source_target_pairs={{0,16},{16,0},{32,48},{48,32},{64,80},{80,64},{96,112},{112,96},{1... | collective-permute-start | bytes 1572872 | tf_op jit(solution)/shard_map/ppermute | solution.py:298
  98.7 1.9 %collective-permute-done.other_ref = bf16[4,256,256]{2,1,0:T(8,128)(2,1)S(1)} collective-permute-done((bf16[4,256,256]{2,1,0:T(8,128)(2,1)S(1)}, bf16[4,256,256]{2,1,0:T(8,128)(2,1)S(1)}, u32[]{:S(2)}, u32[]{:S(2)}) %collective-permute-start) | collective-permute-done | bytes 524320 | tf_op jit(solution)/shard_map/ppermute | solution.py:298
  100.6 5.0 %attend.1 = bf16[4,144,256]{2,1,0:T(8,128)(2,1)S(1)} custom-call(bf16[4,256,128]{2,1,0:T(8,128)(2,1)S(1)} %bitcast.17, s32[4,1,256]{2,1,0:T(1,128)S(1)} %dynamic-slice_bitcast_fusion.qcode_ref, bf16[4,256,256]{2,1,0:T(8,128)(2,1)S(1)} %all_to_all.20.own_ref, bf16[4,256,256]{2,1,0:T(8,128)(2,1)S(1)} %collective-permute-done.other_ref, ...), custom_call_target="tpu_custom_call" | custom-call | tf_op jit(solution)/shard_map/attend/pallas_call | solution.py:135
  105.6 13.0 %all_to_all.21.part_ref = bf16[4,144,256]{2,1,0:T(8,128)(2,1)S(1)} all-to-all(bf16[4,144,256]{2,1,0:T(8,128)(2,1)S(1)} %attend.1), channel_id=1, replica_groups={{0,32,64,96},{16,48,80,112},{128,160,192,224},{144,176,208,240},{256,28..., dimensions={0} | all-to-all | bytes 589824 | tf_op jit(solution)/shard_map/all_to_all | solution.py:300
  119.8 7.0 %all-to-all-start.3 = ((bf16[16,256,128]{2,1,0:T(8,128)(2,1)}), bf16[16,256,128]{2,1,0:T(8,128)(2,1)S(1)}, u32[]{:S(2)}, u32[]{:S(2)}) async-start(bf16[16,256,128]{2,1,0:T(8,128)(2,1)} %combine.1), calls=%async_computation.3 | async-start | bytes 2097152 | tf_op jit(solution)/shard_map/all_to_all | solution.py:302
  126.8 3.4 %collective-permute-start.1 = (bf16[4,128,256]{2,1,0:T(8,128)(2,1)S(1)}, bf16[4,128,256]{2,1,0:T(8,128)(2,1)S(1)}, u32[]{:S(2)}, u32[]{:S(2)}) collective-permute-start(bf16[4,128,256]{2,1,0:T(8,128)(2,1)S(1)} %copy-done.8), channel_id=1, source_target_pairs={{0,1},{1,2},{2,3},{3,0},{4,5},{5,6},{6,7},{7,4},{8,9},{9,10},{10,1... | collective-permute-start | bytes 786440 | tf_op jit(solution)/shard_map/ppermute | solution.py:293
  130.2 4.6 %collective-permute-start.2 = (bf16[4,128,256]{2,1,0:T(8,128)(2,1)S(1)}, bf16[4,128,256]{2,1,0:T(8,128)(2,1)S(1)}, u32[]{:S(2)}, u32[]{:S(2)}) collective-permute-start(bf16[4,128,256]{2,1,0:T(8,128)(2,1)S(1)} %copy-done.6), channel_id=1, source_target_pairs={{0,2},{1,3},{2,0},{3,1},{4,6},{5,7},{6,4},{7,5},{8,10},{9,11},{10,... | collective-permute-start | bytes 786440 | tf_op jit(solution)/shard_map/ppermute | solution.py:293
  134.8 3.4 %collective-permute-start.3 = (bf16[4,128,256]{2,1,0:T(8,128)(2,1)S(1)}, bf16[4,128,256]{2,1,0:T(8,128)(2,1)S(1)}, u32[]{:S(2)}, u32[]{:S(2)}) collective-permute-start(bf16[4,128,256]{2,1,0:T(8,128)(2,1)S(1)} %copy-done.4), channel_id=1, source_target_pairs={{0,3},{1,0},{2,1},{3,2},{4,7},{5,4},{6,5},{7,6},{8,11},{9,8},{10,9... | collective-permute-start | bytes 786440 | tf_op jit(solution)/shard_map/ppermute | solution.py:293
  138.2 8.1 %collective-permute-done.1.refs_1_ = bf16[4,128,256]{2,1,0:T(8,128)(2,1)S(1)} collective-permute-done((bf16[4,128,256]{2,1,0:T(8,128)(2,1)S(1)}, bf16[4,128,256]{2,1,0:T(8,128)(2,1)S(1)}, u32[]{:S(2)}, u32[]{:S(2)}) %collective-permute-start.1) | collective-permute-done | bytes 262176 | tf_op jit(solution)/shard_map/ppermute | solution.py:293
  146.3 5.1 %collective-permute-done.2.refs_2_ = bf16[4,128,256]{2,1,0:T(8,128)(2,1)S(1)} collective-permute-done((bf16[4,128,256]{2,1,0:T(8,128)(2,1)S(1)}, bf16[4,128,256]{2,1,0:T(8,128)(2,1)S(1)}, u32[]{:S(2)}, u32[]{:S(2)}) %collective-permute-start.2) | collective-permute-done | bytes 262176 | tf_op jit(solution)/shard_map/ppermute | solution.py:293
  152.0 3.7 %collective-permute-start.4 = (bf16[4,128,256]{2,1,0:T(8,128)(2,1)S(1)}, bf16[4,128,256]{2,1,0:T(8,128)(2,1)S(1)}, u32[]{:S(2)}, u32[]{:S(2)}) collective-permute-start(bf16[4,128,256]{2,1,0:T(8,128)(2,1)S(1)} %get-tuple-element.48), channel_id=1, source_target_pairs={{0,4},{1,5},{2,6},{3,7},{4,8},{5,9},{6,10},{7,11},{8,12},{9,13},{1... | collective-permute-start | bytes 786440 | tf_op jit(solution)/shard_map/ppermute | solution.py:296
  155.7 3.0 %collective-permute-start.5 = (bf16[4,128,256]{2,1,0:T(8,128)(2,1)S(1)}, bf16[4,128,256]{2,1,0:T(8,128)(2,1)S(1)}, u32[]{:S(2)}, u32[]{:S(2)}) collective-permute-start(bf16[4,128,256]{2,1,0:T(8,128)(2,1)S(1)} %get-tuple-element.49), channel_id=1, source_target_pairs={{0,8},{1,9},{2,10},{3,11},{4,12},{5,13},{6,14},{7,15},{8,0},{9,1},... | collective-permute-start | bytes 786440 | tf_op jit(solution)/shard_map/ppermute | solution.py:296
  158.7 1.9 %collective-permute-start.6 = (bf16[4,128,256]{2,1,0:T(8,128)(2,1)S(1)}, bf16[4,128,256]{2,1,0:T(8,128)(2,1)S(1)}, u32[]{:S(2)}, u32[]{:S(2)}) collective-permute-start(bf16[4,128,256]{2,1,0:T(8,128)(2,1)S(1)} %get-tuple-element.50), channel_id=1, source_target_pairs={{0,12},{1,13},{2,14},{3,15},{4,0},{5,1},{6,2},{7,3},{8,4},{9,5},{1... | collective-permute-start | bytes 786440 | tf_op jit(solution)/shard_map/ppermute | solution.py:296
  160.6 2.4 %collective-permute-done.4.refs_1_ = bf16[4,128,256]{2,1,0:T(8,128)(2,1)S(1)} collective-permute-done((bf16[4,128,256]{2,1,0:T(8,128)(2,1)S(1)}, bf16[4,128,256]{2,1,0:T(8,128)(2,1)S(1)}, u32[]{:S(2)}, u32[]{:S(2)}) %collective-permute-start.4) | collective-permute-done | bytes 262176 | tf_op jit(solution)/shard_map/ppermute | solution.py:296
  163.0 5.2 %collective-permute-done.5.refs_2_ = bf16[4,128,256]{2,1,0:T(8,128)(2,1)S(1)} collective-permute-done((bf16[4,128,256]{2,1,0:T(8,128)(2,1)S(1)}, bf16[4,128,256]{2,1,0:T(8,128)(2,1)S(1)}, u32[]{:S(2)}, u32[]{:S(2)}) %collective-permute-start.5) | collective-permute-done | bytes 262176 | tf_op jit(solution)/shard_map/ppermute | solution.py:296
  168.3 3.1 %collective-permute-done.6.refs_3_ = bf16[4,128,256]{2,1,0:T(8,128)(2,1)S(1)} collective-permute-done((bf16[4,128,256]{2,1,0:T(8,128)(2,1)S(1)}, bf16[4,128,256]{2,1,0:T(8,128)(2,1)S(1)}, u32[]{:S(2)}, u32[]{:S(2)}) %collective-permute-start.6) | collective-permute-done | bytes 262176 | tf_op jit(solution)/shard_map/ppermute | solution.py:296
  171.3 1.9 %output.1 = bf16[256,256]{1,0:T(8,128)(2,1)} custom-call(s32[2]{0:T(128)S(1)} %pad_add_fusion.place_ref, bf16[16,256,128]{2,1,0:T(8,128)(2,1)S(1)} %all-to-all-done.3.attended_ref, bf16[4,128,256]{2,1,0:T(8,128)(2,1)S(1)} %get-tuple-element.47.refs_0_, bf16[4,128,256]{2,1,0:T(8,128)(2,1)S(1)} %collective-permute-done.4.refs_1_, ...), custom_call_target="tpu_custom_call" | custom-call | tf_op jit(solution)/shard_map/output/pallas_call | solution.py:240
  (40 shorter events, 5.8 us)
Async XLA Ops:
  2.4 9.6 %copy-start.11 = (s32[64]{0:T(128)S(1)}, s32[64]{0:T(128)}, u32[]{:S(2)}) copy-start(s32[64]{0:T(128)} %param.11) | copy-start | bytes 772
  2.4 9.7 %copy-start.9 = (s32[8192]{0:T(1024)S(1)}, s32[8192]{0:T(1024)}, u32[]{:S(2)}) copy-start(s32[8192]{0:T(1024)} %param.13) | copy-start | bytes 98308
  2.4 9.7 %copy-start.10 = (s32[8192]{0:T(1024)S(1)}, s32[8192]{0:T(1024)}, u32[]{:S(2)}) copy-start(s32[8192]{0:T(1024)} %param.12) | copy-start | bytes 98308
  2.4 10.5 %copy-start.1 = (bf16[128,4096]{1,0:T(8,128)(2,1)S(1)}, bf16[128,4096]{1,0:T(8,128)(2,1)}, u32[]{:S(2)}) copy-start(bf16[128,4096]{1,0:T(8,128)(2,1)} %w_ref.1) | copy-start | bytes 3145732
  2.4 35.0 %all-to-all-start = ((bf16[16,256,256]{2,1,0:T(8,128)(2,1)}), bf16[16,256,256]{2,1,0:T(8,128)(2,1)S(1)}, u32[]{:S(2)}, u32[]{:S(2)}) async-start(bf16[16,256,256]{2,1,0:T(8,128)(2,1)} %broadcast_in_dim.8), calls=%async_computation | async-start | bytes 4194304 | tf_op jit(solution)/shard_map/all_to_all | solution.py:283
  12.0 25.8 %copy-start.2 = (f32[4096]{0:T(1024)S(1)}, f32[4096]{0:T(1024)}, u32[]{:S(2)}) copy-start(f32[4096]{0:T(1024)} %param.8) | copy-start | bytes 49156
  13.6 0.7 copy-start.3
  14.3 0.7 copy-start.5
  15.0 0.7 copy-start.7
  37.8 1.9 %copy-start = (bf16[4096,3,128]{2,0,1:T(8,128)(2,1)S(1)}, bf16[4096,3,128]{2,0,1:T(8,128)(2,1)}, u32[]{:S(2)}) copy-start(bf16[4096,3,128]{2,0,1:T(8,128)(2,1)} %param.9) | copy-start | bytes 9437188
  96.8 3.8 %collective-permute-start = (bf16[4,256,256]{2,1,0:T(8,128)(2,1)S(1)}, bf16[4,256,256]{2,1,0:T(8,128)(2,1)S(1)}, u32[]{:S(2)}, u32[]{:S(2)}) collective-permute-start(bf16[4,256,256]{2,1,0:T(8,128)(2,1)S(1)} %all_to_all.20.own_ref), channel_id=1, source_target_pairs={{0,16},{16,0},{32,48},{48,32},{64,80},{80,64},{96,112},{112,96},{1... | collective-permute-start | bytes 1572872 | tf_op jit(solution)/shard_map/ppermute | solution.py:298
  105.6 21.2 %copy-start.8 = (bf16[4,128,256]{2,1,0:T(8,128)(2,1)S(1)}, bf16[4,128,256]{2,1,0:T(8,128)(2,1)}, u32[]{:S(2)}) copy-start(bf16[4,128,256]{2,1,0:T(8,128)(2,1)} %copy-done.7) | copy-start | bytes 786436
  105.6 24.6 %copy-start.6 = (bf16[4,128,256]{2,1,0:T(8,128)(2,1)S(1)}, bf16[4,128,256]{2,1,0:T(8,128)(2,1)}, u32[]{:S(2)}) copy-start(bf16[4,128,256]{2,1,0:T(8,128)(2,1)} %copy-done.5) | copy-start | bytes 786436
  105.6 29.2 %copy-start.4 = (bf16[4,128,256]{2,1,0:T(8,128)(2,1)S(1)}, bf16[4,128,256]{2,1,0:T(8,128)(2,1)}, u32[]{:S(2)}) copy-start(bf16[4,128,256]{2,1,0:T(8,128)(2,1)} %copy-done.3) | copy-start | bytes 786436
  119.8 51.5 %all-to-all-start.3 = ((bf16[16,256,128]{2,1,0:T(8,128)(2,1)}), bf16[16,256,128]{2,1,0:T(8,128)(2,1)S(1)}, u32[]{:S(2)}, u32[]{:S(2)}) async-start(bf16[16,256,128]{2,1,0:T(8,128)(2,1)} %combine.1), calls=%async_computation.3 | async-start | bytes 2097152 | tf_op jit(solution)/shard_map/all_to_all | solution.py:302
  126.8 19.5 %collective-permute-start.1 = (bf16[4,128,256]{2,1,0:T(8,128)(2,1)S(1)}, bf16[4,128,256]{2,1,0:T(8,128)(2,1)S(1)}, u32[]{:S(2)}, u32[]{:S(2)}) collective-permute-start(bf16[4,128,256]{2,1,0:T(8,128)(2,1)S(1)} %copy-done.8), channel_id=1, source_target_pairs={{0,1},{1,2},{2,3},{3,0},{4,5},{5,6},{6,7},{7,4},{8,9},{9,10},{10,1... | collective-permute-start | bytes 786440 | tf_op jit(solution)/shard_map/ppermute | solution.py:293
  130.2 21.2 %collective-permute-start.2 = (bf16[4,128,256]{2,1,0:T(8,128)(2,1)S(1)}, bf16[4,128,256]{2,1,0:T(8,128)(2,1)S(1)}, u32[]{:S(2)}, u32[]{:S(2)}) collective-permute-start(bf16[4,128,256]{2,1,0:T(8,128)(2,1)S(1)} %copy-done.6), channel_id=1, source_target_pairs={{0,2},{1,3},{2,0},{3,1},{4,6},{5,7},{6,4},{7,5},{8,10},{9,11},{10,... | collective-permute-start | bytes 786440 | tf_op jit(solution)/shard_map/ppermute | solution.py:293
  134.8 16.6 %collective-permute-start.3 = (bf16[4,128,256]{2,1,0:T(8,128)(2,1)S(1)}, bf16[4,128,256]{2,1,0:T(8,128)(2,1)S(1)}, u32[]{:S(2)}, u32[]{:S(2)}) collective-permute-start(bf16[4,128,256]{2,1,0:T(8,128)(2,1)S(1)} %copy-done.4), channel_id=1, source_target_pairs={{0,3},{1,0},{2,1},{3,2},{4,7},{5,4},{6,5},{7,6},{8,11},{9,8},{10,9... | collective-permute-start | bytes 786440 | tf_op jit(solution)/shard_map/ppermute | solution.py:293
  152.0 11.1 %collective-permute-start.4 = (bf16[4,128,256]{2,1,0:T(8,128)(2,1)S(1)}, bf16[4,128,256]{2,1,0:T(8,128)(2,1)S(1)}, u32[]{:S(2)}, u32[]{:S(2)}) collective-permute-start(bf16[4,128,256]{2,1,0:T(8,128)(2,1)S(1)} %get-tuple-element.48), channel_id=1, source_target_pairs={{0,4},{1,5},{2,6},{3,7},{4,8},{5,9},{6,10},{7,11},{8,12},{9,13},{1... | collective-permute-start | bytes 786440 | tf_op jit(solution)/shard_map/ppermute | solution.py:296
  155.7 12.6 %collective-permute-start.5 = (bf16[4,128,256]{2,1,0:T(8,128)(2,1)S(1)}, bf16[4,128,256]{2,1,0:T(8,128)(2,1)S(1)}, u32[]{:S(2)}, u32[]{:S(2)}) collective-permute-start(bf16[4,128,256]{2,1,0:T(8,128)(2,1)S(1)} %get-tuple-element.49), channel_id=1, source_target_pairs={{0,8},{1,9},{2,10},{3,11},{4,12},{5,13},{6,14},{7,15},{8,0},{9,1},... | collective-permute-start | bytes 786440 | tf_op jit(solution)/shard_map/ppermute | solution.py:296
  158.7 12.6 %collective-permute-start.6 = (bf16[4,128,256]{2,1,0:T(8,128)(2,1)S(1)}, bf16[4,128,256]{2,1,0:T(8,128)(2,1)S(1)}, u32[]{:S(2)}, u32[]{:S(2)}) collective-permute-start(bf16[4,128,256]{2,1,0:T(8,128)(2,1)S(1)} %get-tuple-element.50), channel_id=1, source_target_pairs={{0,12},{1,13},{2,14},{3,15},{4,0},{5,1},{6,2},{7,3},{8,4},{9,5},{1... | collective-permute-start | bytes 786440 | tf_op jit(solution)/shard_map/ppermute | solution.py:296
where the time goes:
time: 174 us; the launch traced here: 173 us
  blocking collectives  67.6 us (39%)
  waiting for transfers between devices  47.5 us (27%)
  starting transfers between devices  38.4 us (22%)
  Pallas kernels  11.9 us (7%)
  local copies, waits for them, and re-layouts  7.44 us (4%)
    all_to_all x1, blocking collectives, on_device(): own_kv = lax.all_to_all(kv, 'seq', 0, 0, axis_index_groups=far)  39 us
    all_to_all x1, waiting for transfers between devices, on_device(): gathered = lax.all_to_all(copies, 'head', 0, 0)  21.7 us
    all_gather x1, blocking collectives, on_device(): all_queries = lax.all_gather(queries, 'seq', axis_index_groups=near)  15.6 us
    ppermute x3, waiting for transfers between devices, on_device(): lax.ppermute(taken[k], 'head', along_y[k])  13.2 us
    all_to_all x1, blocking collectives, on_device(): parts = lax.all_to_all(parts, 'seq', 0, 0, axis_index_groups=near)  13 us
    ppermute x3, starting transfers between devices, on_device(): lax.ppermute(taken[k], 'head', along_y[k])  11.3 us
    ppermute x3, waiting for transfers between devices, on_device(): lax.ppermute(turned[k], 'head', along_x[k])  10.7 us
    all_to_all x1, starting transfers between devices, on_device(): gathered = lax.all_to_all(copies, 'head', 0, 0)  9.55 us
  transfers between devices with their start and end apart: 9, of which 7 were waited for; matrix products, arithmetic and copies ran while one was open for 0% of the time, Pallas kernels for 1%

commit v1 on v0

--- a/solution.py
+++ b/solution.py
@@ -22,64 +22,65 @@
 PART_ROWS = HD + 16
 
 
-def project_kernel(x_ref, gain_ref, w_ref, q_ref, kv_ref, inv_ref, acc_ref):
-    step = pl.program_id(0)
-    blocks = x_ref.shape[0]
-    per_step = blocks // pl.num_programs(0)
-
-    @pl.when(step == 0)
-    def _():
-        total = jnp.zeros((ROWS, x_ref.shape[2]), jnp.float32)
-        for j in range(blocks):
-            piece = x_ref[j].astype(jnp.float32)
-            total = total + piece * piece
-        mean = jnp.sum(total, axis=1, keepdims=True) * (1.0 / D)
-        inv_ref[...] = jnp.broadcast_to(lax.rsqrt(mean + EPSILON), inv_ref.shape)
-        acc_ref[...] = jnp.zeros_like(acc_ref)
-
-    width = x_ref.shape[2]
-    inverse = jnp.concatenate([inv_ref[...]] * (width // 128), axis=1)
-    sums = acc_ref[...]
-    for i in range(per_step):
-        piece = x_ref[step * per_step + i].astype(jnp.float32)
-        gain = gain_ref[:, i * width : (i + 1) * width]
-        normed = (piece * inverse * gain).astype(jnp.bfloat16)
-        rows = slice(i * width, (i + 1) * width)
-        weights = jnp.concatenate([w_ref[0, rows], w_ref[1, rows], w_ref[2, rows]], axis=1)
+def stage_kernel(w_ref, out_ref):
+    out_ref[...] = w_ref[...]
+
+
+def stage(w):
+    rows = 1024
+    spec = pl.BlockSpec((1, rows, HD), lambda i, j: (i, j, 0))
+    return pl.pallas_call(
+        stage_kernel,
+        grid=(w.shape[0], w.shape[1] // rows),
+        in_specs=[spec],
+        out_specs=spec,
+        out_shape=jax.ShapeDtypeStruct(w.shape, w.dtype),
+        compiler_params=pltpu.CompilerParams(vmem_limit_bytes=4 << 20),
+        name="stage",
+    )(w)
+
+
+def project_kernel(x_ref, gain_ref, w_ref, q_out, kv_out, q_ref, kv_ref, sems):
+    blocks, _, width = x_ref.shape
+    total = jnp.zeros((ROWS, width), jnp.float32)
+    for j in range(blocks):
+        piece = x_ref[j].astype(jnp.float32)
+        total = total + piece * piece
+    mean = jnp.sum(total, axis=1, keepdims=True) * (1.0 / D)
+    inverse = jnp.broadcast_to(lax.rsqrt(mean + EPSILON), (ROWS, width))
+    sums = jnp.zeros((ROWS, 3 * HD), jnp.float32)
+    for j in range(blocks):
+        cols = slice(j * width, (j + 1) * width)
+        normed = (x_ref[j].astype(jnp.float32) * inverse * gain_ref[:, cols]).astype(jnp.bfloat16)
+        weights = jnp.concatenate([w_ref[0, cols], w_ref[1, cols], w_ref[2, cols]], axis=1)
         sums = sums + jnp.dot(normed, weights, preferred_element_type=jnp.float32)
-    acc_ref[...] = sums
-
-    @pl.when(step == pl.num_programs(0) - 1)
-    def _():
-        done = sums.astype(jnp.bfloat16)
-        q_ref[...] = done[:, :HD]
-        for j in range(kv_ref.shape[0]):
-            kv_ref[j] = done[:, HD:]
-
-
-def project(x, gain, w, copies):
-    blocks, _, width = x.shape
-    steps = 4
-    depth = D // steps
+    done = sums.astype(jnp.bfloat16)
+    q_ref[...] = done[:, :HD]
+    kv_ref[...] = done[:, HD:]
+    sends = [
+        pltpu.make_async_copy(q_ref, q_out.at[j], sems.at[0, j]) for j in range(q_out.shape[0])
+    ] + [
+        pltpu.make_async_copy(kv_ref, kv_out.at[j], sems.at[1, j]) for j in range(kv_out.shape[0])
+    ]
+    for send in sends:
+        send.start()
+    for send in sends:
+        send.wait()
+
+
+def project(x, gain, w, q_copies, kv_copies):
     return pl.pallas_call(
         project_kernel,
-        grid=(steps,),
-        in_specs=[
-            pl.BlockSpec((blocks, ROWS, width), lambda s: (0, 0, 0)),
-            pl.BlockSpec((1, depth), lambda s: (0, s)),
-            pl.BlockSpec((3, depth, HD), lambda s: (0, s, 0)),
-        ],
-        out_specs=[
-            pl.BlockSpec((ROWS, HD), lambda s: (0, 0)),
-            pl.BlockSpec((copies, ROWS, 2 * HD), lambda s: (0, 0, 0)),
-        ],
+        in_specs=[pl.BlockSpec(memory_space=pltpu.VMEM)] * 3,
+        out_specs=[pl.BlockSpec(memory_space=pltpu.HBM)] * 2,
         out_shape=[
-            jax.ShapeDtypeStruct((ROWS, HD), jnp.bfloat16),
-            jax.ShapeDtypeStruct((copies, ROWS, 2 * HD), jnp.bfloat16),
+            jax.ShapeDtypeStruct((q_copies, ROWS, HD), jnp.bfloat16),
+            jax.ShapeDtypeStruct((kv_copies, ROWS, 2 * HD), jnp.bfloat16),
         ],
         scratch_shapes=[
-            pltpu.VMEM((ROWS, 128), jnp.float32),
-            pltpu.VMEM((ROWS, 3 * HD), jnp.float32),
+            pltpu.VMEM((ROWS, HD), jnp.bfloat16),
+            pltpu.VMEM((ROWS, 2 * HD), jnp.bfloat16),
+            pltpu.SemaphoreType.DMA((2, max(q_copies, kv_copies))),
         ],
         compiler_params=pltpu.CompilerParams(vmem_limit_bytes=GRANT),
         name="project",
@@ -204,8 +205,8 @@
 
 
 def turn_kernel(place_ref, *refs):
-    side = len(refs) // 2
-    for shift, out_ref in enumerate(refs[side:]):
+    side = (len(refs) + 1) // 2
+    for shift, out_ref in enumerate(refs[side:], 1):
         x = lax.rem(place_ref[0] + shift, side)
         for j in range(side):
             out_ref[j] = refs[j][x]
@@ -216,7 +217,7 @@
         turn_kernel,
         in_specs=[pl.BlockSpec(memory_space=pltpu.SMEM)]
         + [pl.BlockSpec(memory_space=pltpu.VMEM)] * len(pieces),
-        out_shape=[jax.ShapeDtypeStruct(p.shape, p.dtype) for p in pieces],
+        out_shape=[jax.ShapeDtypeStruct(p.shape, p.dtype) for p in pieces[1:]],
         compiler_params=pltpu.CompilerParams(vmem_limit_bytes=GRANT),
         name="turn",
     )(place, *pieces)
@@ -224,27 +225,29 @@
 
 def output_kernel(place_ref, attended_ref, *refs):
     out_ref = refs[-1]
-    side = len(refs) - 1
+    side = len(refs) // 2
+    taken, moved = refs[:side], refs[side:-1]
     total = jnp.zeros(out_ref.shape, jnp.float32)
     for k in range(side):
         for j in range(side):
             x = lax.rem(place_ref[0] + (side - k), side)
             y = lax.rem(place_ref[1] + (side - j), side)
             rows = attended_ref[x * side + y]
-            head_out = jnp.dot(rows, refs[k][j], preferred_element_type=jnp.float32)
+            w = taken[j][x] if k == 0 else moved[k - 1][j]
+            head_out = jnp.dot(rows, w, preferred_element_type=jnp.float32)
             total = total + head_out.astype(jnp.bfloat16).astype(jnp.float32)
     out_ref[...] = total.astype(jnp.bfloat16)
 
 
-def output(place, attended, pieces):
+def output(place, attended, taken, moved):
     return pl.pallas_call(
         output_kernel,
         in_specs=[pl.BlockSpec(memory_space=pltpu.SMEM)]
-        + [pl.BlockSpec(memory_space=pltpu.VMEM)] * (1 + len(pieces)),
-        out_shape=jax.ShapeDtypeStruct((ROWS, pieces[0].shape[2]), jnp.bfloat16),
+        + [pl.BlockSpec(memory_space=pltpu.VMEM)] * (1 + len(taken) + len(moved)),
+        out_shape=jax.ShapeDtypeStruct((ROWS, taken[0].shape[2]), jnp.bfloat16),
         compiler_params=pltpu.CompilerParams(vmem_limit_bytes=GRANT),
         name="output",
-    )(place, attended, *pieces)
+    )(place, attended, *taken, *moved)
 
 
 def make_on_device(n_seq, n_head):
@@ -283,24 +286,25 @@
         gathered = lax.all_to_all(copies, "head", 0, 0)
         query_code, key_code = codes(span_order, frame_id, camera_id)
         taken = take(place, w_out, side)
-        gathered, taken, query_code, key_code = lax.optimization_barrier(
-            (gathered, taken, query_code, key_code)
+        w_heads = stage(w_qkv.transpose(1, 0, 2))
+        gathered, taken, w_heads, query_code, key_code = lax.optimization_barrier(
+            (gathered, taken, w_heads, query_code, key_code)
         )
-        queries, kv = project(gathered, norm_gain.reshape(1, D), w_qkv.transpose(1, 0, 2), blocks)
-        all_queries = lax.all_gather(queries, "seq", axis_index_groups=near)
+        queries, kv = project(gathered, norm_gain.reshape(1, D), w_heads, BLOCK_Z, blocks)
+        all_queries = lax.all_to_all(queries, "seq", 0, 0, axis_index_groups=near)
         all_queries, kv, taken = lax.optimization_barrier((all_queries, kv, taken))
         own_kv = lax.all_to_all(kv, "seq", 0, 0, axis_index_groups=far)
         taken = [taken[0]] + [lax.ppermute(taken[k], "head", along_y[k]) for k in range(1, side)]
         turned = turn(place, taken)
-        w_columns = [turned[0]] + [
-            lax.ppermute(turned[k], "head", along_x[k]) for k in range(1, side)
+        moved = [
+            lax.ppermute(piece, "head", along_x[k]) for k, piece in enumerate(turned, 1)
         ]
         other_kv = lax.ppermute(own_kv, "seq", swap)
         parts = attend(all_queries, query_code, own_kv, other_kv, key_code)
         parts = lax.all_to_all(parts, "seq", 0, 0, axis_index_groups=near)
         attended = combine(parts, n_head)
         all_attended = lax.all_to_all(attended, "head", 0, 0)
-        return output(place, all_attended, w_columns)
+        return output(place, all_attended, taken, moved)
 
     return on_device
 

time: 174 us -> 173 us (level)
  waiting for transfers between devices: 47.5 us -> 43.5 us
  Pallas kernels: 11.9 us -> 14.2 us
    all_gather x1 -> x0, blocking collectives: 15.6 us -> none  [on_device(): all_queries = lax.all_gather(queries, 'seq', axis_index_groups=near)]
    all_to_all x0 -> x1, blocking collectives: none -> 13.2 us  [on_device(): all_queries = lax.all_to_all(queries, 'seq', 0, 0, axis_index_groups=near)]
    all_to_all x1, blocking collectives: 13 us -> 17.1 us  [on_device(): parts = lax.all_to_all(parts, 'seq', 0, 0, axis_index_groups=near)]
    all_to_all x1, waiting for transfers between devices: 21.7 us -> 17.7 us  [on_device(): gathered = lax.all_to_all(copies, 'head', 0, 0)]
    all_to_all x1, blocking collectives: 39 us -> 36 us  [on_device(): own_kv = lax.all_to_all(kv, 'seq', 0, 0, axis_index_groups=far)]
    pallas_call x1 -> x2, Pallas kernels: 2.49 us -> 4.74 us  [the longest x1 4.37 us: project(): pl.pallas_call(project_kernel, in_specs=[pl.BlockSpec(memory_space=pltpu....]
where the time goes in v1:
time: 173 us; the launch traced here: 172 us
  blocking collectives  66.2 us (38%)
  waiting for transfers between devices  43.5 us (25%)
  starting transfers between devices  39.1 us (23%)
  Pallas kernels  14.2 us (8%)
  local copies, waits for them, and re-layouts  8.64 us (5%)
    all_to_all x1, blocking collectives, on_device(): own_kv = lax.all_to_all(kv, 'seq', 0, 0, axis_index_groups=far)  36 us
    all_to_all x1, waiting for transfers between devices, on_device(): gathered = lax.all_to_all(copies, 'head', 0, 0)  17.7 us
    all_to_all x1, blocking collectives, on_device(): parts = lax.all_to_all(parts, 'seq', 0, 0, axis_index_groups=near)  17.1 us
    ppermute x3, waiting for transfers between devices, on_device(): lax.ppermute(taken[k], 'head', along_y[k])  13.2 us
    all_to_all x1, blocking collectives, on_device(): all_queries = lax.all_to_all(queries, 'seq', 0, 0, axis_index_groups=near)  13.2 us
    ppermute x3, starting transfers between devices, on_device(): lax.ppermute(taken[k], 'head', along_y[k])  11.3 us
    ppermute x3, waiting for transfers between devices, on_device(): lax.ppermute(piece, 'head', along_x[k])  10.7 us
    all_to_all x1, starting transfers between devices, on_device(): gathered = lax.all_to_all(copies, 'head', 0, 0)  10.1 us
  transfers between devices with their start and end apart: 9, of which 7 were waited for; matrix products, arithmetic and copies ran while one was open for 0% of the time, Pallas kernels for 1%

profile of v1, /device:TPU:6, one launch (start us, length us, event | category | flops | bytes accessed | tf_op | source)
XLA Modules:
  0.0 172.0 jit_solution(1879985916444250988)
XLA Ops:
  0.0 2.4 %broadcast_in_dim.8 = bf16[16,256,256]{2,1,0:T(8,128)(2,1)} broadcast(bf16[256,256]{1,0:T(8,128)(2,1)} %param.7), dimensions={1,2} | broadcast | bytes 2228224 | tf_op jit(solution)/shard_map/broadcast_in_dim | solution.py:285
  2.4 10.1 %all-to-all-start = ((bf16[16,256,256]{2,1,0:T(8,128)(2,1)}), bf16[16,256,256]{2,1,0:T(8,128)(2,1)}, u32[]{:S(2)}, u32[]{:S(2)}) async-start(bf16[16,256,256]{2,1,0:T(8,128)(2,1)} %broadcast_in_dim.8), calls=%async_computation | async-start | bytes 4194304 | tf_op jit(solution)/shard_map/all_to_all | solution.py:286
  13.3 1.9 %copy-done = bf16[4096,3,128]{2,0,1:T(8,128)(2,1)S(1)} copy-done((bf16[4096,3,128]{2,0,1:T(8,128)(2,1)S(1)}, bf16[4096,3,128]{2,0,1:T(8,128)(2,1)}, u32[]{:S(2)}) %copy-start) | copy-done | bytes 3145752
  19.6 17.7 %all-to-all-done.x_ref = bf16[16,256,256]{2,1,0:T(8,128)(2,1)} async-done(((bf16[16,256,256]{2,1,0:T(8,128)(2,1)}), bf16[16,256,256]{2,1,0:T(8,128)(2,1)}, u32[]{:S(2)}, u32[]{:S(2)}) %all-to-all-start) | async-done | bytes 2097184 | tf_op jit(solution)/shard_map/all_to_all | solution.py:286
  37.7 4.4 %project.1 = (bf16[4,256,128]{2,1,0:T(8,128)(2,1)S(1)}, bf16[4,256,256]{2,1,0:T(8,128)(2,1)S(1)}) custom-call(bf16[16,256,256]{2,1,0:T(8,128)(2,1)} %all-to-all-done.x_ref, f32[1,4096]{1,0:T(1,128)S(1)} %bitcast.16, bf16[3,4096,128]{2,1,0:T(8,128)(2,1)S(1)} %stage.1.w_ref), custom_call_target="tpu_custom_call" | custom-call | tf_op jit(solution)/shard_map/project/pallas_call | solution.py:72
  42.1 13.2 %all_to_all.25.q_ref = bf16[4,256,128]{2,1,0:T(8,128)(2,1)S(1)} all-to-all(bf16[4,256,128]{2,1,0:T(8,128)(2,1)S(1)} %get-tuple-element.34), channel_id=1, replica_groups={{0,32,64,96},{16,48,80,112},{128,160,192,224},{144,176,208,240},{256,28..., dimensions={0} | all-to-all | bytes 524288 | tf_op jit(solution)/shard_map/all_to_all | solution.py:294
  55.2 36.0 %all_to_all.26.own_ref = bf16[4,256,256]{2,1,0:T(8,128)(2,1)S(1)} all-to-all(bf16[4,256,256]{2,1,0:T(8,128)(2,1)S(1)} %get-tuple-element.42), channel_id=1, replica_groups={{0,128,256,384},{16,144,272,400},{32,160,288,416},{48,176,304,432},{64,..., dimensions={0} | all-to-all | bytes 1048576 | tf_op jit(solution)/shard_map/all_to_all | solution.py:296
  91.2 2.0 %collective-permute-start = (bf16[4,256,256]{2,1,0:T(8,128)(2,1)S(1)}, bf16[4,256,256]{2,1,0:T(8,128)(2,1)S(1)}, u32[]{:S(2)}, u32[]{:S(2)}) collective-permute-start(bf16[4,256,256]{2,1,0:T(8,128)(2,1)S(1)} %all_to_all.26.own_ref), channel_id=1, source_target_pairs={{0,16},{16,0},{32,48},{48,32},{64,80},{80,64},{96,112},{112,96},{1... | collective-permute-start | bytes 1572872 | tf_op jit(solution)/shard_map/ppermute | solution.py:302
  93.3 1.9 %collective-permute-done.other_ref = bf16[4,256,256]{2,1,0:T(8,128)(2,1)S(1)} collective-permute-done((bf16[4,256,256]{2,1,0:T(8,128)(2,1)S(1)}, bf16[4,256,256]{2,1,0:T(8,128)(2,1)S(1)}, u32[]{:S(2)}, u32[]{:S(2)}) %collective-permute-start) | collective-permute-done | bytes 524320 | tf_op jit(solution)/shard_map/ppermute | solution.py:302
  95.1 5.0 %attend.1 = bf16[4,144,256]{2,1,0:T(8,128)(2,1)S(1)} custom-call(bf16[4,256,128]{2,1,0:T(8,128)(2,1)S(1)} %all_to_all.25.q_ref, s32[4,1,256]{2,1,0:T(1,128)S(1)} %dynamic-slice_bitcast_fusion.qcode_ref, bf16[4,256,256]{2,1,0:T(8,128)(2,1)S(1)} %all_to_all.26.own_ref, bf16[4,256,256]{2,1,0:T(8,128)(2,1)S(1)} %collective-permute-done.other_ref, ...), custom_call_target="tpu_custom_call" | custom-call | tf_op jit(solution)/shard_map/attend/pallas_call | solution.py:136
  100.2 17.1 %all_to_all.27.part_ref = bf16[4,144,256]{2,1,0:T(8,128)(2,1)S(1)} all-to-all(bf16[4,144,256]{2,1,0:T(8,128)(2,1)S(1)} %attend.1), channel_id=1, replica_groups={{0,32,64,96},{16,48,80,112},{128,160,192,224},{144,176,208,240},{256,28..., dimensions={0} | all-to-all | bytes 589824 | tf_op jit(solution)/shard_map/all_to_all | solution.py:304
  118.5 7.1 %all-to-all-start.4 = ((bf16[16,256,128]{2,1,0:T(8,128)(2,1)}), bf16[16,256,128]{2,1,0:T(8,128)(2,1)S(1)}, u32[]{:S(2)}, u32[]{:S(2)}) async-start(bf16[16,256,128]{2,1,0:T(8,128)(2,1)} %combine.1), calls=%async_computation.4 | async-start | bytes 2097152 | tf_op jit(solution)/shard_map/all_to_all | solution.py:306
  125.6 3.4 %collective-permute-start.1 = (bf16[4,128,256]{2,1,0:T(8,128)(2,1)S(1)}, bf16[4,128,256]{2,1,0:T(8,128)(2,1)S(1)}, u32[]{:S(2)}, u32[]{:S(2)}) collective-permute-start(bf16[4,128,256]{2,1,0:T(8,128)(2,1)S(1)} %copy-done.8), channel_id=1, source_target_pairs={{0,1},{1,2},{2,3},{3,0},{4,5},{5,6},{6,7},{7,4},{8,9},{9,10},{10,1... | collective-permute-start | bytes 786440 | tf_op jit(solution)/shard_map/ppermute | solution.py:297
  129.0 4.6 %collective-permute-start.2 = (bf16[4,128,256]{2,1,0:T(8,128)(2,1)S(1)}, bf16[4,128,256]{2,1,0:T(8,128)(2,1)S(1)}, u32[]{:S(2)}, u32[]{:S(2)}) collective-permute-start(bf16[4,128,256]{2,1,0:T(8,128)(2,1)S(1)} %copy-done.6), channel_id=1, source_target_pairs={{0,2},{1,3},{2,0},{3,1},{4,6},{5,7},{6,4},{7,5},{8,10},{9,11},{10,... | collective-permute-start | bytes 786440 | tf_op jit(solution)/shard_map/ppermute | solution.py:297
  133.6 3.4 %collective-permute-start.3 = (bf16[4,128,256]{2,1,0:T(8,128)(2,1)S(1)}, bf16[4,128,256]{2,1,0:T(8,128)(2,1)S(1)}, u32[]{:S(2)}, u32[]{:S(2)}) collective-permute-start(bf16[4,128,256]{2,1,0:T(8,128)(2,1)S(1)} %copy-done.4), channel_id=1, source_target_pairs={{0,3},{1,0},{2,1},{3,2},{4,7},{5,4},{6,5},{7,6},{8,11},{9,8},{10,9... | collective-permute-start | bytes 786440 | tf_op jit(solution)/shard_map/ppermute | solution.py:297
  136.9 8.1 %collective-permute-done.1.refs_1_ = bf16[4,128,256]{2,1,0:T(8,128)(2,1)S(1)} collective-permute-done((bf16[4,128,256]{2,1,0:T(8,128)(2,1)S(1)}, bf16[4,128,256]{2,1,0:T(8,128)(2,1)S(1)}, u32[]{:S(2)}, u32[]{:S(2)}) %collective-permute-start.1) | collective-permute-done | bytes 262176 | tf_op jit(solution)/shard_map/ppermute | solution.py:297
  145.1 5.1 %collective-permute-done.2.refs_2_ = bf16[4,128,256]{2,1,0:T(8,128)(2,1)S(1)} collective-permute-done((bf16[4,128,256]{2,1,0:T(8,128)(2,1)S(1)}, bf16[4,128,256]{2,1,0:T(8,128)(2,1)S(1)}, u32[]{:S(2)}, u32[]{:S(2)}) %collective-permute-start.2) | collective-permute-done | bytes 262176 | tf_op jit(solution)/shard_map/ppermute | solution.py:297
  150.7 3.7 %collective-permute-start.4 = (bf16[4,128,256]{2,1,0:T(8,128)(2,1)S(1)}, bf16[4,128,256]{2,1,0:T(8,128)(2,1)S(1)}, u32[]{:S(2)}, u32[]{:S(2)}) collective-permute-start(bf16[4,128,256]{2,1,0:T(8,128)(2,1)S(1)} %get-tuple-element.48), channel_id=1, source_target_pairs={{0,4},{1,5},{2,6},{3,7},{4,8},{5,9},{6,10},{7,11},{8,12},{9,13},{1... | collective-permute-start | bytes 786440 | tf_op jit(solution)/shard_map/ppermute | solution.py:300
  154.5 3.0 %collective-permute-start.5 = (bf16[4,128,256]{2,1,0:T(8,128)(2,1)S(1)}, bf16[4,128,256]{2,1,0:T(8,128)(2,1)S(1)}, u32[]{:S(2)}, u32[]{:S(2)}) collective-permute-start(bf16[4,128,256]{2,1,0:T(8,128)(2,1)S(1)} %get-tuple-element.49), channel_id=1, source_target_pairs={{0,8},{1,9},{2,10},{3,11},{4,12},{5,13},{6,14},{7,15},{8,0},{9,1},... | collective-permute-start | bytes 786440 | tf_op jit(solution)/shard_map/ppermute | solution.py:300
  157.5 1.9 %collective-permute-start.6 = (bf16[4,128,256]{2,1,0:T(8,128)(2,1)S(1)}, bf16[4,128,256]{2,1,0:T(8,128)(2,1)S(1)}, u32[]{:S(2)}, u32[]{:S(2)}) collective-permute-start(bf16[4,128,256]{2,1,0:T(8,128)(2,1)S(1)} %get-tuple-element.50), channel_id=1, source_target_pairs={{0,12},{1,13},{2,14},{3,15},{4,0},{5,1},{6,2},{7,3},{8,4},{9,5},{1... | collective-permute-start | bytes 786440 | tf_op jit(solution)/shard_map/ppermute | solution.py:300
  159.4 2.4 %collective-permute-done.4.refs_4_ = bf16[4,128,256]{2,1,0:T(8,128)(2,1)S(1)} collective-permute-done((bf16[4,128,256]{2,1,0:T(8,128)(2,1)S(1)}, bf16[4,128,256]{2,1,0:T(8,128)(2,1)S(1)}, u32[]{:S(2)}, u32[]{:S(2)}) %collective-permute-start.4) | collective-permute-done | bytes 262176 | tf_op jit(solution)/shard_map/ppermute | solution.py:300
  161.8 5.2 %collective-permute-done.5.refs_5_ = bf16[4,128,256]{2,1,0:T(8,128)(2,1)S(1)} collective-permute-done((bf16[4,128,256]{2,1,0:T(8,128)(2,1)S(1)}, bf16[4,128,256]{2,1,0:T(8,128)(2,1)S(1)}, u32[]{:S(2)}, u32[]{:S(2)}) %collective-permute-start.5) | collective-permute-done | bytes 262176 | tf_op jit(solution)/shard_map/ppermute | solution.py:300
  167.0 3.1 %collective-permute-done.6.refs_6_ = bf16[4,128,256]{2,1,0:T(8,128)(2,1)S(1)} collective-permute-done((bf16[4,128,256]{2,1,0:T(8,128)(2,1)S(1)}, bf16[4,128,256]{2,1,0:T(8,128)(2,1)S(1)}, u32[]{:S(2)}, u32[]{:S(2)}) %collective-permute-start.6) | collective-permute-done | bytes 262176 | tf_op jit(solution)/shard_map/ppermute | solution.py:300
  170.1 1.9 %output.1 = bf16[256,256]{1,0:T(8,128)(2,1)} custom-call(s32[2]{0:T(128)S(1)} %pad_add_fusion.place_ref, bf16[16,256,128]{2,1,0:T(8,128)(2,1)S(1)} %all-to-all-done.4.attended_ref, bf16[4,128,256]{2,1,0:T(8,128)(2,1)S(1)} %get-tuple-element.44.refs_0_, bf16[4,128,256]{2,1,0:T(8,128)(2,1)S(1)} %collective-permute-done.1.refs_1_, ...), custom_call_target="tpu_custom_call" | custom-call | tf_op jit(solution)/shard_map/output/pallas_call | solution.py:243
  (41 shorter events, 7.3 us)
Async XLA Ops:
  0.0 12.5 %copy-start.11 = (s32[64]{0:T(128)S(1)}, s32[64]{0:T(128)}, u32[]{:S(2)}) copy-start(s32[64]{0:T(128)} %param.11) | copy-start | bytes 772
  0.0 12.5 %copy-start.9 = (s32[8192]{0:T(1024)S(1)}, s32[8192]{0:T(1024)}, u32[]{:S(2)}) copy-start(s32[8192]{0:T(1024)} %param.13) | copy-start | bytes 98308
  0.0 12.5 %copy-start.10 = (s32[8192]{0:T(1024)S(1)}, s32[8192]{0:T(1024)}, u32[]{:S(2)}) copy-start(s32[8192]{0:T(1024)} %param.12) | copy-start | bytes 98308
  2.4 34.9 %all-to-all-start = ((bf16[16,256,256]{2,1,0:T(8,128)(2,1)}), bf16[16,256,256]{2,1,0:T(8,128)(2,1)}, u32[]{:S(2)}, u32[]{:S(2)}) async-start(bf16[16,256,256]{2,1,0:T(8,128)(2,1)} %broadcast_in_dim.8), calls=%async_computation | async-start | bytes 4194304 | tf_op jit(solution)/shard_map/all_to_all | solution.py:286
  13.2 1.9 %copy-start = (bf16[4096,3,128]{2,0,1:T(8,128)(2,1)S(1)}, bf16[4096,3,128]{2,0,1:T(8,128)(2,1)}, u32[]{:S(2)}) copy-start(bf16[4096,3,128]{2,0,1:T(8,128)(2,1)} %param.9) | copy-start | bytes 9437188
  15.1 22.5 %copy-start.2 = (f32[4096]{0:T(1024)S(1)}, f32[4096]{0:T(1024)}, u32[]{:S(2)}) copy-start(f32[4096]{0:T(1024)} %param.8) | copy-start | bytes 49156
  15.6 1.2 copy-start.1
  17.5 0.7 copy-start.3
  18.2 0.7 copy-start.5
  18.9 0.7 copy-start.7
  91.2 34.4 %copy-start.8 = (bf16[4,128,256]{2,1,0:T(8,128)(2,1)S(1)}, bf16[4,128,256]{2,1,0:T(8,128)(2,1)}, u32[]{:S(2)}) copy-start(bf16[4,128,256]{2,1,0:T(8,128)(2,1)} %copy-done.7) | copy-start | bytes 786436
  91.2 37.8 %copy-start.6 = (bf16[4,128,256]{2,1,0:T(8,128)(2,1)S(1)}, bf16[4,128,256]{2,1,0:T(8,128)(2,1)}, u32[]{:S(2)}) copy-start(bf16[4,128,256]{2,1,0:T(8,128)(2,1)} %copy-done.5) | copy-start | bytes 786436
  91.2 42.4 %copy-start.4 = (bf16[4,128,256]{2,1,0:T(8,128)(2,1)S(1)}, bf16[4,128,256]{2,1,0:T(8,128)(2,1)}, u32[]{:S(2)}) copy-start(bf16[4,128,256]{2,1,0:T(8,128)(2,1)} %copy-done.3) | copy-start | bytes 786436
  91.2 3.9 %collective-permute-start = (bf16[4,256,256]{2,1,0:T(8,128)(2,1)S(1)}, bf16[4,256,256]{2,1,0:T(8,128)(2,1)S(1)}, u32[]{:S(2)}, u32[]{:S(2)}) collective-permute-start(bf16[4,256,256]{2,1,0:T(8,128)(2,1)S(1)} %all_to_all.26.own_ref), channel_id=1, source_target_pairs={{0,16},{16,0},{32,48},{48,32},{64,80},{80,64},{96,112},{112,96},{1... | collective-permute-start | bytes 1572872 | tf_op jit(solution)/shard_map/ppermute | solution.py:302
  118.5 51.6 %all-to-all-start.4 = ((bf16[16,256,128]{2,1,0:T(8,128)(2,1)}), bf16[16,256,128]{2,1,0:T(8,128)(2,1)S(1)}, u32[]{:S(2)}, u32[]{:S(2)}) async-start(bf16[16,256,128]{2,1,0:T(8,128)(2,1)} %combine.1), calls=%async_computation.4 | async-start | bytes 2097152 | tf_op jit(solution)/shard_map/all_to_all | solution.py:306
  125.6 19.5 %collective-permute-start.1 = (bf16[4,128,256]{2,1,0:T(8,128)(2,1)S(1)}, bf16[4,128,256]{2,1,0:T(8,128)(2,1)S(1)}, u32[]{:S(2)}, u32[]{:S(2)}) collective-permute-start(bf16[4,128,256]{2,1,0:T(8,128)(2,1)S(1)} %copy-done.8), channel_id=1, source_target_pairs={{0,1},{1,2},{2,3},{3,0},{4,5},{5,6},{6,7},{7,4},{8,9},{9,10},{10,1... | collective-permute-start | bytes 786440 | tf_op jit(solution)/shard_map/ppermute | solution.py:297
  129.0 21.2 %collective-permute-start.2 = (bf16[4,128,256]{2,1,0:T(8,128)(2,1)S(1)}, bf16[4,128,256]{2,1,0:T(8,128)(2,1)S(1)}, u32[]{:S(2)}, u32[]{:S(2)}) collective-permute-start(bf16[4,128,256]{2,1,0:T(8,128)(2,1)S(1)} %copy-done.6), channel_id=1, source_target_pairs={{0,2},{1,3},{2,0},{3,1},{4,6},{5,7},{6,4},{7,5},{8,10},{9,11},{10,... | collective-permute-start | bytes 786440 | tf_op jit(solution)/shard_map/ppermute | solution.py:297
  133.6 16.6 %collective-permute-start.3 = (bf16[4,128,256]{2,1,0:T(8,128)(2,1)S(1)}, bf16[4,128,256]{2,1,0:T(8,128)(2,1)S(1)}, u32[]{:S(2)}, u32[]{:S(2)}) collective-permute-start(bf16[4,128,256]{2,1,0:T(8,128)(2,1)S(1)} %copy-done.4), channel_id=1, source_target_pairs={{0,3},{1,0},{2,1},{3,2},{4,7},{5,4},{6,5},{7,6},{8,11},{9,8},{10,9... | collective-permute-start | bytes 786440 | tf_op jit(solution)/shard_map/ppermute | solution.py:297
  150.7 11.1 %collective-permute-start.4 = (bf16[4,128,256]{2,1,0:T(8,128)(2,1)S(1)}, bf16[4,128,256]{2,1,0:T(8,128)(2,1)S(1)}, u32[]{:S(2)}, u32[]{:S(2)}) collective-permute-start(bf16[4,128,256]{2,1,0:T(8,128)(2,1)S(1)} %get-tuple-element.48), channel_id=1, source_target_pairs={{0,4},{1,5},{2,6},{3,7},{4,8},{5,9},{6,10},{7,11},{8,12},{9,13},{1... | collective-permute-start | bytes 786440 | tf_op jit(solution)/shard_map/ppermute | solution.py:300
  154.5 12.6 %collective-permute-start.5 = (bf16[4,128,256]{2,1,0:T(8,128)(2,1)S(1)}, bf16[4,128,256]{2,1,0:T(8,128)(2,1)S(1)}, u32[]{:S(2)}, u32[]{:S(2)}) collective-permute-start(bf16[4,128,256]{2,1,0:T(8,128)(2,1)S(1)} %get-tuple-element.49), channel_id=1, source_target_pairs={{0,8},{1,9},{2,10},{3,11},{4,12},{5,13},{6,14},{7,15},{8,0},{9,1},... | collective-permute-start | bytes 786440 | tf_op jit(solution)/shard_map/ppermute | solution.py:300
  157.5 12.6 %collective-permute-start.6 = (bf16[4,128,256]{2,1,0:T(8,128)(2,1)S(1)}, bf16[4,128,256]{2,1,0:T(8,128)(2,1)S(1)}, u32[]{:S(2)}, u32[]{:S(2)}) collective-permute-start(bf16[4,128,256]{2,1,0:T(8,128)(2,1)S(1)} %get-tuple-element.50), channel_id=1, source_target_pairs={{0,12},{1,13},{2,14},{3,15},{4,0},{5,1},{6,2},{7,3},{8,4},{9,5},{1... | collective-permute-start | bytes 786440 | tf_op jit(solution)/shard_map/ppermute | solution.py:300

commit v2 on v1

v2 whole, which is shorter than its diff:
```python
import math

import jax
import jax.numpy as jnp
from jax import lax
from jax.experimental import pallas as pl
from jax.experimental.pallas import tpu as pltpu
from jax.sharding import PartitionSpec as P


D = 4096
HD = 128
ROWS = 256
SPAN = 128
CORES = 2
BLOCK_Z = 4
GRANT = 16 << 20
MASKED = -1e30
EPSILON = 1e-06
LOG2_E = 1.4426950408889634
SCALE = HD**-0.5 * LOG2_E
PART_ROWS = HD + 16


def stage_kernel(w_ref, out_ref):
    out_ref[...] = w_ref[...]


def stage(w):
    rows = 1024
    spec = pl.BlockSpec((1, rows, HD), lambda i, j: (i, j, 0))
    return pl.pallas_call(
        stage_kernel,
        grid=(w.shape[0], w.shape[1] // rows),
        in_specs=[spec],
        out_specs=spec,
        out_shape=jax.ShapeDtypeStruct(w.shape, w.dtype),
        compiler_params=pltpu.CompilerParams(vmem_limit_bytes=4 << 20),
        name="stage",
    )(w)


def project_kernel(x_ref, gain_ref, w_ref, q_ref, kv_ref):
    blocks, _, width = x_ref.shape
    total = jnp.zeros((ROWS, width), jnp.float32)
    for j in range(blocks):
        piece = x_ref[j].astype(jnp.float32)
        total = total + piece * piece
    mean = jnp.sum(total, axis=1, keepdims=True) * (1.0 / D)
    inverse = jnp.broadcast_to(lax.rsqrt(mean + EPSILON), (ROWS, width))
    sums = jnp.zeros((ROWS, 3 * HD), jnp.float32)
    for j in range(blocks):
        cols = slice(j * width, (j + 1) * width)
        normed = (x_ref[j].astype(jnp.float32) * inverse * gain_ref[:, cols]).astype(jnp.bfloat16)
        weights = jnp.concatenate([w_ref[0, cols], w_ref[1, cols], w_ref[2, cols]], axis=1)
        sums = sums + jnp.dot(normed, weights, preferred_element_type=jnp.float32)
    done = sums.astype(jnp.bfloat16)
    q_ref[...] = done[:, :HD]
    for j in range(kv_ref.shape[0]):
        kv_ref[j] = done[:, HD:]


def project(x, gain, w, copies):
    return pl.pallas_call(
        project_kernel,
        in_specs=[pl.BlockSpec(memory_space=pltpu.VMEM)] * 3,
        out_specs=[pl.BlockSpec(memory_space=pltpu.VMEM)] * 2,
        out_shape=[
            jax.ShapeDtypeStruct((ROWS, HD), jnp.bfloat16),
            jax.ShapeDtypeStruct((copies, ROWS, 2 * HD), jnp.bfloat16),
        ],
        compiler_params=pltpu.CompilerParams(vmem_limit_bytes=GRANT),
        name="project",
    )(x, gain, w)


def attend_kernel(qcode_ref, kcode_ref, own_ref, other_ref, *refs):
    q_refs, out_ref, vt_ref, column_ref = refs[:-3], refs[-3], refs[-2], refs[-1]
    groups = len(q_refs)
    block = lax.rem(lax.div(lax.axis_index("seq"), CORES), groups)
    count = own_ref.shape[0]
    unit = jnp.where(lax.broadcasted_iota(jnp.int32, (16, 128), 0) == 0, 8.0, 1.0)
    column_ref[...] = lax.dot_general(
        kcode_ref[...],
        unit.astype(jnp.bfloat16),
        (((0,), (0,)), ((), ())),
        preferred_element_type=jnp.float32,
    )
    for part, ref in enumerate((own_ref, other_ref)):
        for j in range(count):
            at = (part * count + j) * ROWS
            vt_ref[:, at : at + ROWS] = jnp.transpose(ref[j][:, HD:])

    for shift, q_ref in enumerate(q_refs):
        member = lax.rem(block + (groups - shift), groups)
        qcode = qcode_ref[member]
        qbase = (qcode & -8).astype(jnp.float32)
        qcode = qcode.astype(jnp.float32)
        queries = q_ref[...]
        scores = []
        for part, ref in enumerate((own_ref, other_ref)):
            for j in range(count):
                at = (part * count + j) * ROWS
                raw = lax.dot_general(
                    ref[j][:, :HD],
                    queries,
                    (((1,), (1,)), ((), ())),
                    preferred_element_type=jnp.float32,
                )
                code = column_ref[at : at + ROWS, :]
                kcode = jnp.concatenate([code] * (ROWS // 128), axis=1)
                seen = (kcode < qbase) | (kcode == qcode)
                scores.append(jnp.where(seen, raw * SCALE, MASKED))
        scores = jnp.concatenate(scores, axis=0)
        best = jnp.max(scores, axis=0, keepdims=True)
        weights = jnp.exp2(scores - best)
        total = jnp.sum(weights, axis=0, keepdims=True)
        mixed = jnp.dot(
            vt_ref[...], weights.astype(jnp.bfloat16), preferred_element_type=jnp.float32
        )
        out_ref[member, :HD] = (mixed / total).astype(jnp.bfloat16)
        level = best + jnp.log2(total)
        high = level.astype(jnp.bfloat16).astype(jnp.float32)
        rest = level - high
        middle = rest.astype(jnp.bfloat16).astype(jnp.float32)
        low = rest - middle
        row = lax.broadcasted_iota(jnp.int32, (16, ROWS), 0)
        stats = jnp.where(
            row == 0, high, jnp.where(row == 1, middle, jnp.where(row == 2, low, 0.0))
        )
        out_ref[member, HD:] = stats.astype(jnp.bfloat16)


def attend(queries, qcode, own_kv, other_kv, kcode):
    groups = len(queries)
    keys = kcode.shape[1]
    return pl.pallas_call(
        attend_kernel,
        in_specs=[pl.BlockSpec(memory_space=pltpu.VMEM)] * (4 + groups),
        out_shape=jax.ShapeDtypeStruct((groups, PART_ROWS, ROWS), jnp.bfloat16),
        scratch_shapes=[
            pltpu.VMEM((HD, keys), jnp.bfloat16),
            pltpu.VMEM((keys, 128), jnp.float32),
        ],
        compiler_params=pltpu.CompilerParams(vmem_limit_bytes=GRANT),
        name="attend",
    )(qcode, kcode, own_kv, other_kv, *queries)


def combine_kernel(part_ref, out_ref):
    groups = part_ref.shape[0]
    levels = []
    for j in range(groups):
        stats = part_ref[j, HD:].astype(jnp.float32)
        levels.append(stats[0:1] + stats[1:2] + stats[2:3])
    best = levels[0]
    for level in levels[1:]:
        best = jnp.maximum(best, level)
    total = jnp.zeros_like(best)
    mixed = jnp.zeros((HD, ROWS), jnp.float32)
    for j in range(groups):
        share = jnp.exp2(levels[j] - best)
        total = total + share
        mixed = mixed + share * part_ref[j, :HD].astype(jnp.float32)
    attended = jnp.transpose(mixed / total).astype(jnp.bfloat16)
    for j in range(out_ref.shape[0]):
        out_ref[j] = attended


def combine(parts, copies):
    return pl.pallas_call(
        combine_kernel,
        out_shape=jax.ShapeDtypeStruct((copies, ROWS, HD), jnp.bfloat16),
        compiler_params=pltpu.CompilerParams(vmem_limit_bytes=GRANT),
        name="combine",
    )(parts)


def head_place(side):
    head = lax.axis_index("head")
    return lax.div(head, side), lax.rem(head, side)


def take_kernel(w_ref, *out_refs):
    side = len(out_refs)
    _, own_y = head_place(side)
    width = out_refs[0].shape[2]
    for shift, out_ref in enumerate(out_refs):
        y = lax.rem(own_y + shift, side)
        for x in range(side):
            at = pl.multiple_of((x * side + y) * width, width)
            out_ref[x] = w_ref[:, pl.ds(at, width)]


def take(w, side):
    piece = jax.ShapeDtypeStruct((side, HD, w.shape[1] // side**2), w.dtype)
    return pl.pallas_call(
        take_kernel,
        in_specs=[pl.BlockSpec(memory_space=pltpu.VMEM)],
        out_shape=[piece] * side,
        compiler_params=pltpu.CompilerParams(vmem_limit_bytes=GRANT),
        name="take",
    )(w)


def turn_kernel(*refs):
    side = (len(refs) + 1) // 2
    own_x, _ = head_place(side)
    for shift, out_ref in enumerate(refs[side:], 1):
        x = lax.rem(own_x + shift, side)
        for j in range(side):
            out_ref[j] = refs[j][x]


def turn(pieces):
    return pl.pallas_call(
        turn_kernel,
        in_specs=[pl.BlockSpec(memory_space=pltpu.VMEM)] * len(pieces),
        out_shape=[jax.ShapeDtypeStruct(p.shape, p.dtype) for p in pieces[1:]],
        compiler_params=pltpu.CompilerParams(vmem_limit_bytes=GRANT),
        name="turn",
    )(*pieces)


def output_kernel(attended_ref, *refs):
    out_ref = refs[-1]
    side = len(refs) // 2
    own_x, own_y = head_place(side)
    taken, moved = refs[:side], refs[side:-1]
    total = jnp.zeros(out_ref.shape, jnp.float32)
    for k in range(side):
        for j in range(side):
            x = lax.rem(own_x + (side - k), side)
            y = lax.rem(own_y + (side - j), side)
            rows = attended_ref[x * side + y]
            w = taken[j][x] if k == 0 else moved[k - 1][j]
            head_out = jnp.dot(rows, w, preferred_element_type=jnp.float32)
            total = total + head_out.astype(jnp.bfloat16).astype(jnp.float32)
    out_ref[...] = total.astype(jnp.bfloat16)


def output(attended, taken, moved):
    return pl.pallas_call(
        output_kernel,
        in_specs=[pl.BlockSpec(memory_space=pltpu.VMEM)] * (1 + len(taken) + len(moved)),
        out_shape=jax.ShapeDtypeStruct((ROWS, taken[0].shape[2]), jnp.bfloat16),
        compiler_params=pltpu.CompilerParams(vmem_limit_bytes=GRANT),
        name="output",
    )(attended, *taken, *moved)


def make_on_device(n_seq, n_head):
    group = CORES * BLOCK_Z
    blocks = n_seq // group
    near = [
        [g * group + b * CORES + c for b in range(BLOCK_Z)] for g in range(blocks) for c in range(CORES)
    ]
    far = [[g * group + i for g in range(blocks)] for i in range(group)]
    swap = [(i, i ^ 1) for i in range(n_seq)]
    keys = CORES * blocks * ROWS

    def codes(span_order, frame_id, camera_id):
        code = (frame_id * 8 + camera_id).reshape(-1, SPAN)[span_order]
        code = code.reshape(blocks, BLOCK_Z, CORES, ROWS)
        place = lax.axis_index("seq")
        core = place % CORES
        query_code = lax.dynamic_index_in_dim(code, place // group, 0, keepdims=False)
        query_code = lax.dynamic_index_in_dim(query_code, core, 1, keepdims=False)
        key_code = lax.dynamic_index_in_dim(code, place // CORES % BLOCK_Z, 1, keepdims=False)
        own = lax.dynamic_index_in_dim(key_code, core, 1, keepdims=False)
        other = lax.dynamic_index_in_dim(key_code, 1 - core, 1, keepdims=False)
        key_code = jnp.concatenate([own, other]).reshape(1, keys)
        row = lax.broadcasted_iota(jnp.int32, (16, keys), 0)
        pair = jnp.where(row == 0, key_code >> 3, jnp.where(row == 1, key_code & 7, 0))
        return query_code[:, None, :], pair.astype(jnp.bfloat16)

    side = math.isqrt(n_head)
    along_block = [
        [(i, i // group * group + (i + k * CORES) % group) for i in range(n_seq)]
        for k in range(BLOCK_Z)
    ]
    along_x = [[(i, (i + k * side) % n_head) for i in range(n_head)] for k in range(side)]
    along_y = [
        [(i, i // side * side + (i + k) % side) for i in range(n_head)] for k in range(side)
    ]

    def on_device(tokens, norm_gain, w_qkv, w_out, span_order, frame_id, camera_id):
        copies = jnp.broadcast_to(tokens[None], (n_head,) + tokens.shape)
        gathered = lax.all_to_all(copies, "head", 0, 0)
        query_code, key_code = codes(span_order, frame_id, camera_id)
        taken = take(w_out, side)
        w_heads = stage(w_qkv.transpose(1, 0, 2))
        gathered, taken, w_heads, query_code, key_code = lax.optimization_barrier(
            (gathered, taken, w_heads, query_code, key_code)
        )
        queries, kv = project(gathered, norm_gain.reshape(1, D), w_heads, blocks)
        own_kv = lax.all_to_all(kv, "seq", 0, 0, axis_index_groups=far)
        all_queries = [queries] + [
            lax.ppermute(queries, "seq", along_block[k]) for k in range(1, BLOCK_Z)
        ]
        taken = [taken[0]] + [lax.ppermute(taken[k], "head", along_y[k]) for k in range(1, side)]
        turned = turn(taken)
        moved = [
            lax.ppermute(piece, "head", along_x[k]) for k, piece in enumerate(turned, 1)
        ]
        other_kv = lax.ppermute(own_kv, "seq", swap)
        parts = attend(all_queries, query_code, own_kv, other_kv, key_code)
        parts = lax.all_to_all(parts, "seq", 0, 0, axis_index_groups=near)
        attended = combine(parts, n_head)
        all_attended = lax.all_to_all(attended, "head", 0, 0)
        return output(all_attended, taken, moved)

    return on_device


def solution(mesh):
    placed = (P("seq", "head"), P(), P(None, None, "head"), P("head", None), P(), P(), P())
    return jax.shard_map(
        make_on_device(mesh.shape["seq"], mesh.shape["head"]),
        mesh=mesh,
        in_specs=placed,
        out_specs=P("seq", "head"),
        check_vma=False,
    )
```

time: 173 us -> 170 us (0.983)
  blocking collectives: 66.2 us -> 51 us
  starting transfers between devices: 39.1 us -> 53.5 us
  waiting for transfers between devices: 43.5 us -> 47.9 us
  Pallas kernels: 14.2 us -> 10.6 us
  local copies, waits for them, and re-layouts: 8.64 us -> 6.01 us
    ppermute x0 -> x3, starting transfers between devices: none -> 14.8 us  [on_device(): lax.ppermute(queries, 'seq', along_block[k])]
    all_to_all x1 -> x0, blocking collectives: 13.2 us -> none  [on_device(): all_queries = lax.all_to_all(queries, 'seq', 0, 0, axis_index_groups=near)]
    all_to_all x1, blocking collectives: 17.1 us -> 11.2 us  [on_device(): parts = lax.all_to_all(parts, 'seq', 0, 0, axis_index_groups=near)]
    ppermute x0 -> x3, waiting for transfers between devices: none -> 5.01 us  [on_device(): lax.ppermute(queries, 'seq', along_block[k])]
    all_to_all x1, blocking collectives: 36 us -> 39.9 us  [on_device(): own_kv = lax.all_to_all(kv, 'seq', 0, 0, axis_index_groups=far)]
    all_to_all x1, waiting for transfers between devices: 17.7 us -> 20.6 us  [on_device(): gathered = lax.all_to_all(copies, 'head', 0, 0)]
    pallas_call x4, Pallas kernels: 8.23 us -> 5.72 us  [the longest x1 4.15 us: attend(): pl.pallas_call(attend_kernel, in_specs=[pl.BlockSpec(memory_space=pltpu.V...]
    unnamed x26 -> x27, local copies, waits for them, and re-layouts: 5.25 us -> 2.84 us
  transfers between devices with their start and end apart: 9 -> 12, of which waited for: 7 -> 8; matrix products, arithmetic and copies ran while one was open for 0% -> 0% of each run, Pallas kernels for 1% -> 0%
where the time goes in v2:
time: 170 us; the launch traced here: 169 us
  starting transfers between devices  53.5 us (31%)
  blocking collectives  51 us (30%)
  waiting for transfers between devices  47.9 us (28%)
  Pallas kernels  10.6 us (6%)
  local copies, waits for them, and re-layouts  6.01 us (4%)
    all_to_all x1, blocking collectives, on_device(): own_kv = lax.all_to_all(kv, 'seq', 0, 0, axis_index_groups=far)  39.9 us
    all_to_all x1, waiting for transfers between devices, on_device(): gathered = lax.all_to_all(copies, 'head', 0, 0)  20.6 us
    ppermute x3, starting transfers between devices, on_device(): lax.ppermute(queries, 'seq', along_block[k])  14.8 us
    ppermute x3, waiting for transfers between devices, on_device(): lax.ppermute(taken[k], 'head', along_y[k])  12 us
    ppermute x3, starting transfers between devices, on_device(): lax.ppermute(taken[k], 'head', along_y[k])  11.3 us
    all_to_all x1, blocking collectives, on_device(): parts = lax.all_to_all(parts, 'seq', 0, 0, axis_index_groups=near)  11.2 us
    ppermute x3, waiting for transfers between devices, on_device(): lax.ppermute(piece, 'head', along_x[k])  10.3 us
    all_to_all x1, starting transfers between devices, on_device(): gathered = lax.all_to_all(copies, 'head', 0, 0)  10.1 us
  transfers between devices with their start and end apart: 12, of which 8 were waited for; matrix products, arithmetic and copies ran while one was open for 0% of the time, Pallas kernels for 0%

profile of v2, /device:TPU:6, one launch (start us, length us, event | category | flops | bytes accessed | tf_op | source)
XLA Modules:
  0.0 169.4 jit_solution(9605063401080657913)
XLA Ops:
  0.0 2.5 %broadcast_in_dim.28 = bf16[16,256,256]{2,1,0:T(8,128)(2,1)} broadcast(bf16[256,256]{1,0:T(8,128)(2,1)} %param.7), dimensions={1,2} | broadcast | bytes 2228224 | tf_op jit(solution)/shard_map/broadcast_in_dim | solution.py:288
  2.5 10.1 %all-to-all-start = ((bf16[16,256,256]{2,1,0:T(8,128)(2,1)}), bf16[16,256,256]{2,1,0:T(8,128)(2,1)}, u32[]{:S(2)}, u32[]{:S(2)}) async-start(bf16[16,256,256]{2,1,0:T(8,128)(2,1)} %broadcast_in_dim.28), calls=%async_computation | async-start | bytes 4194304 | tf_op jit(solution)/shard_map/all_to_all | solution.py:289
  14.3 2.1 %copy-done = bf16[4096,3,128]{2,0,1:T(8,128)(2,1)S(1)} copy-done((bf16[4096,3,128]{2,0,1:T(8,128)(2,1)S(1)}, bf16[4096,3,128]{2,0,1:T(8,128)(2,1)}, u32[]{:S(2)}) %copy-start) | copy-done | bytes 3145752
  16.9 20.6 %all-to-all-done.x_ref = bf16[16,256,256]{2,1,0:T(8,128)(2,1)} async-done(((bf16[16,256,256]{2,1,0:T(8,128)(2,1)}), bf16[16,256,256]{2,1,0:T(8,128)(2,1)}, u32[]{:S(2)}, u32[]{:S(2)}) %all-to-all-start) | async-done | bytes 2097184 | tf_op jit(solution)/shard_map/all_to_all | solution.py:289
  37.4 3.3 %project.1 = (bf16[256,128]{1,0:T(8,128)(2,1)S(1)}, bf16[4,256,256]{2,1,0:T(8,128)(2,1)S(1)}) custom-call(bf16[16,256,256]{2,1,0:T(8,128)(2,1)} %all-to-all-done.x_ref, f32[1,4096]{1,0:T(1,128)S(1)} %bitcast.17, bf16[3,4096,128]{2,1,0:T(8,128)(2,1)S(1)} %stage.1.w_ref), custom_call_target="tpu_custom_call" | custom-call | tf_op jit(solution)/shard_map/project/pallas_call | solution.py:64
  40.7 39.9 %all_to_all.20.own_ref = bf16[4,256,256]{2,1,0:T(8,128)(2,1)S(1)} all-to-all(bf16[4,256,256]{2,1,0:T(8,128)(2,1)S(1)} %get-tuple-element.30), channel_id=1, replica_groups={{0,128,256,384},{16,144,272,400},{32,160,288,416},{48,176,304,432},{64,..., dimensions={0} | all-to-all | bytes 1048576 | tf_op jit(solution)/shard_map/all_to_all | solution.py:297
  82.5 3.8 %collective-permute-start.3 = (bf16[256,128]{1,0:T(8,128)(2,1)S(1)}, bf16[256,128]{1,0:T(8,128)(2,1)S(1)}, u32[]{:S(2)}, u32[]{:S(2)}) collective-permute-start(bf16[256,128]{1,0:T(8,128)(2,1)S(1)} %get-tuple-element.31.refs_0_), channel_id=1, source_target_pairs={{0,96},{16,112},{32,0},{48,16},{64,32},{80,48},{96,64},{112,80},{1... | collective-permute-start | bytes 196616 | tf_op jit(solution)/shard_map/ppermute | solution.py:299
  86.3 8.1 %collective-permute-start.2 = (bf16[256,128]{1,0:T(8,128)(2,1)S(1)}, bf16[256,128]{1,0:T(8,128)(2,1)S(1)}, u32[]{:S(2)}, u32[]{:S(2)}) collective-permute-start(bf16[256,128]{1,0:T(8,128)(2,1)S(1)} %get-tuple-element.31.refs_0_), channel_id=1, source_target_pairs={{0,64},{16,80},{32,96},{48,112},{64,0},{80,16},{96,32},{112,48},{1... | collective-permute-start | bytes 196616 | tf_op jit(solution)/shard_map/ppermute | solution.py:299
  94.4 2.9 %collective-permute-start.1 = (bf16[256,128]{1,0:T(8,128)(2,1)S(1)}, bf16[256,128]{1,0:T(8,128)(2,1)S(1)}, u32[]{:S(2)}, u32[]{:S(2)}) collective-permute-start(bf16[256,128]{1,0:T(8,128)(2,1)S(1)} %get-tuple-element.31.refs_0_), channel_id=1, source_target_pairs={{0,32},{16,48},{32,64},{48,80},{64,96},{80,112},{96,0},{112,16},{1... | collective-permute-start | bytes 196616 | tf_op jit(solution)/shard_map/ppermute | solution.py:299
  98.3 4.1 %collective-permute-done.1.refs_1_ = bf16[256,128]{1,0:T(8,128)(2,1)S(1)} collective-permute-done((bf16[256,128]{1,0:T(8,128)(2,1)S(1)}, bf16[256,128]{1,0:T(8,128)(2,1)S(1)}, u32[]{:S(2)}, u32[]{:S(2)}) %collective-permute-start.1) | collective-permute-done | bytes 65568 | tf_op jit(solution)/shard_map/ppermute | solution.py:299
  102.4 4.1 %attend.1 = bf16[4,144,256]{2,1,0:T(8,128)(2,1)S(1)} custom-call(s32[4,1,256]{2,1,0:T(1,128)S(1)} %dynamic-slice_bitcast_fusion.qcode_ref, bf16[16,2048]{1,0:T(8,128)(2,1)S(1)} %select_convert_fusion.kcode_ref, bf16[4,256,256]{2,1,0:T(8,128)(2,1)S(1)} %all_to_all.20.own_ref, bf16[4,256,256]{2,1,0:T(8,128)(2,1)S(1)} %collective-permute-done.other_ref, ...), custom_call_target="tpu_custom_call" | custom-call | tf_op jit(solution)/shard_map/attend/pallas_call | solution.py:137
  106.6 11.2 %all_to_all.21.part_ref = bf16[4,144,256]{2,1,0:T(8,128)(2,1)S(1)} all-to-all(bf16[4,144,256]{2,1,0:T(8,128)(2,1)S(1)} %attend.1), channel_id=1, replica_groups={{0,32,64,96},{16,48,80,112},{128,160,192,224},{144,176,208,240},{256,28..., dimensions={0} | all-to-all | bytes 589824 | tf_op jit(solution)/shard_map/all_to_all | solution.py:308
  118.9 6.7 %all-to-all-start.3 = ((bf16[16,256,128]{2,1,0:T(8,128)(2,1)}), bf16[16,256,128]{2,1,0:T(8,128)(2,1)S(1)}, u32[]{:S(2)}, u32[]{:S(2)}) async-start(bf16[16,256,128]{2,1,0:T(8,128)(2,1)} %combine.1), calls=%async_computation.3 | async-start | bytes 2097152 | tf_op jit(solution)/shard_map/all_to_all | solution.py:310
  125.7 3.4 %collective-permute-start.4 = (bf16[4,128,256]{2,1,0:T(8,128)(2,1)S(1)}, bf16[4,128,256]{2,1,0:T(8,128)(2,1)S(1)}, u32[]{:S(2)}, u32[]{:S(2)}) collective-permute-start(bf16[4,128,256]{2,1,0:T(8,128)(2,1)S(1)} %copy-done.8), channel_id=1, source_target_pairs={{0,1},{1,2},{2,3},{3,0},{4,5},{5,6},{6,7},{7,4},{8,9},{9,10},{10,1... | collective-permute-start | bytes 786440 | tf_op jit(solution)/shard_map/ppermute | solution.py:301
  129.0 4.6 %collective-permute-start.5 = (bf16[4,128,256]{2,1,0:T(8,128)(2,1)S(1)}, bf16[4,128,256]{2,1,0:T(8,128)(2,1)S(1)}, u32[]{:S(2)}, u32[]{:S(2)}) collective-permute-start(bf16[4,128,256]{2,1,0:T(8,128)(2,1)S(1)} %copy-done.6), channel_id=1, source_target_pairs={{0,2},{1,3},{2,0},{3,1},{4,6},{5,7},{6,4},{7,5},{8,10},{9,11},{10,... | collective-permute-start | bytes 786440 | tf_op jit(solution)/shard_map/ppermute | solution.py:301
  133.6 3.4 %collective-permute-start.6 = (bf16[4,128,256]{2,1,0:T(8,128)(2,1)S(1)}, bf16[4,128,256]{2,1,0:T(8,128)(2,1)S(1)}, u32[]{:S(2)}, u32[]{:S(2)}) collective-permute-start(bf16[4,128,256]{2,1,0:T(8,128)(2,1)S(1)} %copy-done.4), channel_id=1, source_target_pairs={{0,3},{1,0},{2,1},{3,2},{4,7},{5,4},{6,5},{7,6},{8,11},{9,8},{10,9... | collective-permute-start | bytes 786440 | tf_op jit(solution)/shard_map/ppermute | solution.py:301
  137.0 7.5 %collective-permute-done.4.refs_1_ = bf16[4,128,256]{2,1,0:T(8,128)(2,1)S(1)} collective-permute-done((bf16[4,128,256]{2,1,0:T(8,128)(2,1)S(1)}, bf16[4,128,256]{2,1,0:T(8,128)(2,1)S(1)}, u32[]{:S(2)}, u32[]{:S(2)}) %collective-permute-start.4) | collective-permute-done | bytes 262176 | tf_op jit(solution)/shard_map/ppermute | solution.py:301
  144.6 4.5 %collective-permute-done.5.refs_2_ = bf16[4,128,256]{2,1,0:T(8,128)(2,1)S(1)} collective-permute-done((bf16[4,128,256]{2,1,0:T(8,128)(2,1)S(1)}, bf16[4,128,256]{2,1,0:T(8,128)(2,1)S(1)}, u32[]{:S(2)}, u32[]{:S(2)}) %collective-permute-start.5) | collective-permute-done | bytes 262176 | tf_op jit(solution)/shard_map/ppermute | solution.py:301
  149.1 3.5 %collective-permute-start.7 = (bf16[4,128,256]{2,1,0:T(8,128)(2,1)S(1)}, bf16[4,128,256]{2,1,0:T(8,128)(2,1)S(1)}, u32[]{:S(2)}, u32[]{:S(2)}) collective-permute-start(bf16[4,128,256]{2,1,0:T(8,128)(2,1)S(1)} %get-tuple-element.36), channel_id=1, source_target_pairs={{0,4},{1,5},{2,6},{3,7},{4,8},{5,9},{6,10},{7,11},{8,12},{9,13},{1... | collective-permute-start | bytes 786440 | tf_op jit(solution)/shard_map/ppermute | solution.py:304
  152.6 3.2 %collective-permute-start.8 = (bf16[4,128,256]{2,1,0:T(8,128)(2,1)S(1)}, bf16[4,128,256]{2,1,0:T(8,128)(2,1)S(1)}, u32[]{:S(2)}, u32[]{:S(2)}) collective-permute-start(bf16[4,128,256]{2,1,0:T(8,128)(2,1)S(1)} %get-tuple-element.37), channel_id=1, source_target_pairs={{0,8},{1,9},{2,10},{3,11},{4,12},{5,13},{6,14},{7,15},{8,0},{9,1},... | collective-permute-start | bytes 786440 | tf_op jit(solution)/shard_map/ppermute | solution.py:304
  155.8 1.9 %collective-permute-start.9 = (bf16[4,128,256]{2,1,0:T(8,128)(2,1)S(1)}, bf16[4,128,256]{2,1,0:T(8,128)(2,1)S(1)}, u32[]{:S(2)}, u32[]{:S(2)}) collective-permute-start(bf16[4,128,256]{2,1,0:T(8,128)(2,1)S(1)} %get-tuple-element.38), channel_id=1, source_target_pairs={{0,12},{1,13},{2,14},{3,15},{4,0},{5,1},{6,2},{7,3},{8,4},{9,5},{1... | collective-permute-start | bytes 786440 | tf_op jit(solution)/shard_map/ppermute | solution.py:304
  157.7 4.7 %collective-permute-done.7.refs_4_ = bf16[4,128,256]{2,1,0:T(8,128)(2,1)S(1)} collective-permute-done((bf16[4,128,256]{2,1,0:T(8,128)(2,1)S(1)}, bf16[4,128,256]{2,1,0:T(8,128)(2,1)S(1)}, u32[]{:S(2)}, u32[]{:S(2)}) %collective-permute-start.7) | collective-permute-done | bytes 262176 | tf_op jit(solution)/shard_map/ppermute | solution.py:304
  162.5 2.7 %collective-permute-done.8.refs_5_ = bf16[4,128,256]{2,1,0:T(8,128)(2,1)S(1)} collective-permute-done((bf16[4,128,256]{2,1,0:T(8,128)(2,1)S(1)}, bf16[4,128,256]{2,1,0:T(8,128)(2,1)S(1)}, u32[]{:S(2)}, u32[]{:S(2)}) %collective-permute-start.8) | collective-permute-done | bytes 262176 | tf_op jit(solution)/shard_map/ppermute | solution.py:304
  165.2 2.9 %collective-permute-done.9.refs_6_ = bf16[4,128,256]{2,1,0:T(8,128)(2,1)S(1)} collective-permute-done((bf16[4,128,256]{2,1,0:T(8,128)(2,1)S(1)}, bf16[4,128,256]{2,1,0:T(8,128)(2,1)S(1)}, u32[]{:S(2)}, u32[]{:S(2)}) %collective-permute-start.9) | collective-permute-done | bytes 262176 | tf_op jit(solution)/shard_map/ppermute | solution.py:304
  (47 shorter events, 7.5 us)
Async XLA Ops:
  0.0 12.6 %copy-start.11 = (s32[64]{0:T(128)S(1)}, s32[64]{0:T(128)}, u32[]{:S(2)}) copy-start(s32[64]{0:T(128)} %param.11) | copy-start | bytes 772
  0.0 12.6 %copy-start.9 = (s32[8192]{0:T(1024)S(1)}, s32[8192]{0:T(1024)}, u32[]{:S(2)}) copy-start(s32[8192]{0:T(1024)} %param.13) | copy-start | bytes 98308
  0.0 12.6 %copy-start.10 = (s32[8192]{0:T(1024)S(1)}, s32[8192]{0:T(1024)}, u32[]{:S(2)}) copy-start(s32[8192]{0:T(1024)} %param.12) | copy-start | bytes 98308
  0.0 13.4 %copy-start.1 = (bf16[128,4096]{1,0:T(8,128)(2,1)S(1)}, bf16[128,4096]{1,0:T(8,128)(2,1)}, u32[]{:S(2)}) copy-start(bf16[128,4096]{1,0:T(8,128)(2,1)} %w_ref.1) | copy-start | bytes 3145732
  2.5 34.9 %all-to-all-start = ((bf16[16,256,256]{2,1,0:T(8,128)(2,1)}), bf16[16,256,256]{2,1,0:T(8,128)(2,1)}, u32[]{:S(2)}, u32[]{:S(2)}) async-start(bf16[16,256,256]{2,1,0:T(8,128)(2,1)} %broadcast_in_dim.28), calls=%async_computation | async-start | bytes 4194304 | tf_op jit(solution)/shard_map/all_to_all | solution.py:289
  13.5 0.7 copy-start.7
  14.2 2.5 %copy-start.3 = (bf16[4,128,256]{2,1,0:T(8,128)(2,1)}, bf16[4,128,256]{2,1,0:T(8,128)(2,1)S(1)}, u32[]{:S(2)}) copy-start(bf16[4,128,256]{2,1,0:T(8,128)(2,1)S(1)} %get-tuple-element.35) | copy-start | bytes 786436
  14.2 2.5 %copy-start.5 = (bf16[4,128,256]{2,1,0:T(8,128)(2,1)}, bf16[4,128,256]{2,1,0:T(8,128)(2,1)S(1)}, u32[]{:S(2)}) copy-start(bf16[4,128,256]{2,1,0:T(8,128)(2,1)S(1)} %get-tuple-element.34) | copy-start | bytes 786436
  14.3 2.1 %copy-start = (bf16[4096,3,128]{2,0,1:T(8,128)(2,1)S(1)}, bf16[4096,3,128]{2,0,1:T(8,128)(2,1)}, u32[]{:S(2)}) copy-start(bf16[4096,3,128]{2,0,1:T(8,128)(2,1)} %param.9) | copy-start | bytes 9437188
  16.3 21.1 %copy-start.2 = (f32[4096]{0:T(1024)S(1)}, f32[4096]{0:T(1024)}, u32[]{:S(2)}) copy-start(f32[4096]{0:T(1024)} %param.8) | copy-start | bytes 49156
  40.7 84.9 %copy-start.8 = (bf16[4,128,256]{2,1,0:T(8,128)(2,1)S(1)}, bf16[4,128,256]{2,1,0:T(8,128)(2,1)}, u32[]{:S(2)}) copy-start(bf16[4,128,256]{2,1,0:T(8,128)(2,1)} %copy-done.7) | copy-start | bytes 786436
  40.7 88.3 %copy-start.6 = (bf16[4,128,256]{2,1,0:T(8,128)(2,1)S(1)}, bf16[4,128,256]{2,1,0:T(8,128)(2,1)}, u32[]{:S(2)}) copy-start(bf16[4,128,256]{2,1,0:T(8,128)(2,1)} %copy-done.5) | copy-start | bytes 786436
  40.7 92.9 %copy-start.4 = (bf16[4,128,256]{2,1,0:T(8,128)(2,1)S(1)}, bf16[4,128,256]{2,1,0:T(8,128)(2,1)}, u32[]{:S(2)}) copy-start(bf16[4,128,256]{2,1,0:T(8,128)(2,1)} %copy-done.3) | copy-start | bytes 786436
  80.6 21.8 %collective-permute-start = (bf16[4,256,256]{2,1,0:T(8,128)(2,1)S(1)}, bf16[4,256,256]{2,1,0:T(8,128)(2,1)S(1)}, u32[]{:S(2)}, u32[]{:S(2)}) collective-permute-start(bf16[4,256,256]{2,1,0:T(8,128)(2,1)S(1)} %all_to_all.20.own_ref), channel_id=1, source_target_pairs={{0,16},{16,0},{32,48},{48,32},{64,80},{80,64},{96,112},{112,96},{1... | collective-permute-start | bytes 1572872 | tf_op jit(solution)/shard_map/ppermute | solution.py:306
  82.5 14.9 %collective-permute-start.3 = (bf16[256,128]{1,0:T(8,128)(2,1)S(1)}, bf16[256,128]{1,0:T(8,128)(2,1)S(1)}, u32[]{:S(2)}, u32[]{:S(2)}) collective-permute-start(bf16[256,128]{1,0:T(8,128)(2,1)S(1)} %get-tuple-element.31.refs_0_), channel_id=1, source_target_pairs={{0,96},{16,112},{32,0},{48,16},{64,32},{80,48},{96,64},{112,80},{1... | collective-permute-start | bytes 196616 | tf_op jit(solution)/shard_map/ppermute | solution.py:299
  86.3 12.0 %collective-permute-start.2 = (bf16[256,128]{1,0:T(8,128)(2,1)S(1)}, bf16[256,128]{1,0:T(8,128)(2,1)S(1)}, u32[]{:S(2)}, u32[]{:S(2)}) collective-permute-start(bf16[256,128]{1,0:T(8,128)(2,1)S(1)} %get-tuple-element.31.refs_0_), channel_id=1, source_target_pairs={{0,64},{16,80},{32,96},{48,112},{64,0},{80,16},{96,32},{112,48},{1... | collective-permute-start | bytes 196616 | tf_op jit(solution)/shard_map/ppermute | solution.py:299
  94.4 8.0 %collective-permute-start.1 = (bf16[256,128]{1,0:T(8,128)(2,1)S(1)}, bf16[256,128]{1,0:T(8,128)(2,1)S(1)}, u32[]{:S(2)}, u32[]{:S(2)}) collective-permute-start(bf16[256,128]{1,0:T(8,128)(2,1)S(1)} %get-tuple-element.31.refs_0_), channel_id=1, source_target_pairs={{0,32},{16,48},{32,64},{48,80},{64,96},{80,112},{96,0},{112,16},{1... | collective-permute-start | bytes 196616 | tf_op jit(solution)/shard_map/ppermute | solution.py:299
  118.9 49.1 %all-to-all-start.3 = ((bf16[16,256,128]{2,1,0:T(8,128)(2,1)}), bf16[16,256,128]{2,1,0:T(8,128)(2,1)S(1)}, u32[]{:S(2)}, u32[]{:S(2)}) async-start(bf16[16,256,128]{2,1,0:T(8,128)(2,1)} %combine.1), calls=%async_computation.3 | async-start | bytes 2097152 | tf_op jit(solution)/shard_map/all_to_all | solution.py:310
  125.7 18.9 %collective-permute-start.4 = (bf16[4,128,256]{2,1,0:T(8,128)(2,1)S(1)}, bf16[4,128,256]{2,1,0:T(8,128)(2,1)S(1)}, u32[]{:S(2)}, u32[]{:S(2)}) collective-permute-start(bf16[4,128,256]{2,1,0:T(8,128)(2,1)S(1)} %copy-done.8), channel_id=1, source_target_pairs={{0,1},{1,2},{2,3},{3,0},{4,5},{5,6},{6,7},{7,4},{8,9},{9,10},{10,1... | collective-permute-start | bytes 786440 | tf_op jit(solution)/shard_map/ppermute | solution.py:301
  129.0 20.0 %collective-permute-start.5 = (bf16[4,128,256]{2,1,0:T(8,128)(2,1)S(1)}, bf16[4,128,256]{2,1,0:T(8,128)(2,1)S(1)}, u32[]{:S(2)}, u32[]{:S(2)}) collective-permute-start(bf16[4,128,256]{2,1,0:T(8,128)(2,1)S(1)} %copy-done.6), channel_id=1, source_target_pairs={{0,2},{1,3},{2,0},{3,1},{4,6},{5,7},{6,4},{7,5},{8,10},{9,11},{10,... | collective-permute-start | bytes 786440 | tf_op jit(solution)/shard_map/ppermute | solution.py:301
  133.6 15.4 %collective-permute-start.6 = (bf16[4,128,256]{2,1,0:T(8,128)(2,1)S(1)}, bf16[4,128,256]{2,1,0:T(8,128)(2,1)S(1)}, u32[]{:S(2)}, u32[]{:S(2)}) collective-permute-start(bf16[4,128,256]{2,1,0:T(8,128)(2,1)S(1)} %copy-done.4), channel_id=1, source_target_pairs={{0,3},{1,0},{2,1},{3,2},{4,7},{5,4},{6,5},{7,6},{8,11},{9,8},{10,9... | collective-permute-start | bytes 786440 | tf_op jit(solution)/shard_map/ppermute | solution.py:301
  149.1 13.4 %collective-permute-start.7 = (bf16[4,128,256]{2,1,0:T(8,128)(2,1)S(1)}, bf16[4,128,256]{2,1,0:T(8,128)(2,1)S(1)}, u32[]{:S(2)}, u32[]{:S(2)}) collective-permute-start(bf16[4,128,256]{2,1,0:T(8,128)(2,1)S(1)} %get-tuple-element.36), channel_id=1, source_target_pairs={{0,4},{1,5},{2,6},{3,7},{4,8},{5,9},{6,10},{7,11},{8,12},{9,13},{1... | collective-permute-start | bytes 786440 | tf_op jit(solution)/shard_map/ppermute | solution.py:304
  152.6 12.6 %collective-permute-start.8 = (bf16[4,128,256]{2,1,0:T(8,128)(2,1)S(1)}, bf16[4,128,256]{2,1,0:T(8,128)(2,1)S(1)}, u32[]{:S(2)}, u32[]{:S(2)}) collective-permute-start(bf16[4,128,256]{2,1,0:T(8,128)(2,1)S(1)} %get-tuple-element.37), channel_id=1, source_target_pairs={{0,8},{1,9},{2,10},{3,11},{4,12},{5,13},{6,14},{7,15},{8,0},{9,1},... | collective-permute-start | bytes 786440 | tf_op jit(solution)/shard_map/ppermute | solution.py:304
  155.8 12.2 %collective-permute-start.9 = (bf16[4,128,256]{2,1,0:T(8,128)(2,1)S(1)}, bf16[4,128,256]{2,1,0:T(8,128)(2,1)S(1)}, u32[]{:S(2)}, u32[]{:S(2)}) collective-permute-start(bf16[4,128,256]{2,1,0:T(8,128)(2,1)S(1)} %get-tuple-element.38), channel_id=1, source_target_pairs={{0,12},{1,13},{2,14},{3,15},{4,0},{5,1},{6,2},{7,3},{8,4},{9,5},{1... | collective-permute-start | bytes 786440 | tf_op jit(solution)/shard_map/ppermute | solution.py:304

commit v3 on v2

v3 whole, which is shorter than its diff:
```python
import jax
import jax.numpy as jnp
from jax import lax
from jax.experimental import pallas as pl
from jax.experimental.pallas import tpu as pltpu
from jax.sharding import PartitionSpec as P


D = 4096
HD = 128
ROWS = 256
SPAN = 128
CORES = 2
BLOCK_Z = 4
GRANT = 16 << 20
MASKED = -1e30
EPSILON = 1e-06
LOG2_E = 1.4426950408889634
SCALE = HD**-0.5 * LOG2_E
PART_ROWS = HD + 16


def stage_kernel(w_ref, out_ref):
    out_ref[...] = w_ref[...]


def stage(w):
    rows = 1024
    spec = pl.BlockSpec((1, rows, HD), lambda i, j: (i, j, 0))
    return pl.pallas_call(
        stage_kernel,
        grid=(w.shape[0], w.shape[1] // rows),
        in_specs=[spec],
        out_specs=spec,
        out_shape=jax.ShapeDtypeStruct(w.shape, w.dtype),
        compiler_params=pltpu.CompilerParams(vmem_limit_bytes=4 << 20),
        name="stage",
    )(w)


def project_kernel(x_ref, gain_ref, w_ref, q_ref, kv_ref):
    blocks, _, width = x_ref.shape
    total = jnp.zeros((ROWS, width), jnp.float32)
    for j in range(blocks):
        piece = x_ref[j].astype(jnp.float32)
        total = total + piece * piece
    mean = jnp.sum(total, axis=1, keepdims=True) * (1.0 / D)
    inverse = jnp.broadcast_to(lax.rsqrt(mean + EPSILON), (ROWS, width))
    sums = jnp.zeros((ROWS, 3 * HD), jnp.float32)
    for j in range(blocks):
        cols = slice(j * width, (j + 1) * width)
        normed = (x_ref[j].astype(jnp.float32) * inverse * gain_ref[:, cols]).astype(jnp.bfloat16)
        weights = jnp.concatenate([w_ref[0, cols], w_ref[1, cols], w_ref[2, cols]], axis=1)
        sums = sums + jnp.dot(normed, weights, preferred_element_type=jnp.float32)
    done = sums.astype(jnp.bfloat16)
    q_ref[...] = done[:, :HD]
    kv_ref[...] = done[:, HD:]


def project(x, gain, w):
    return pl.pallas_call(
        project_kernel,
        in_specs=[pl.BlockSpec(memory_space=pltpu.VMEM)] * 3,
        out_specs=[pl.BlockSpec(memory_space=pltpu.VMEM)] * 2,
        out_shape=[
            jax.ShapeDtypeStruct((ROWS, HD), jnp.bfloat16),
            jax.ShapeDtypeStruct((ROWS, 2 * HD), jnp.bfloat16),
        ],
        compiler_params=pltpu.CompilerParams(vmem_limit_bytes=GRANT),
        name="project",
    )(x, gain, w)


def attend_kernel(qcode_ref, kcode_ref, other_ref, *refs):
    count = other_ref.shape[0]
    own_refs, q_refs = refs[:count], refs[count:-3]
    out_ref, vt_ref, column_ref = refs[-3:]
    groups = len(q_refs)
    far_block = lax.div(lax.axis_index("seq"), CORES * groups)
    block = lax.rem(lax.div(lax.axis_index("seq"), CORES), groups)
    pieces = list(own_refs) + [other_ref.at[j] for j in range(count)]
    unit = jnp.where(lax.broadcasted_iota(jnp.int32, (16, 128), 0) == 0, 8.0, 1.0)
    column_ref[...] = lax.dot_general(
        kcode_ref[...],
        unit.astype(jnp.bfloat16),
        (((0,), (0,)), ((), ())),
        preferred_element_type=jnp.float32,
    )
    for j, ref in enumerate(pieces):
        vt_ref[:, j * ROWS : (j + 1) * ROWS] = jnp.transpose(ref[:, HD:])

    for shift, q_ref in enumerate(q_refs):
        member = lax.rem(block + (groups - shift), groups)
        qcode = qcode_ref[member]
        qbase = (qcode & -8).astype(jnp.float32)
        qcode = qcode.astype(jnp.float32)
        queries = q_ref[...]
        scores = []
        for j, ref in enumerate(pieces):
            raw = lax.dot_general(
                ref[:, :HD],
                queries,
                (((1,), (1,)), ((), ())),
                preferred_element_type=jnp.float32,
            )
            source = lax.rem(far_block + (count - j % count), count)
            at = pl.multiple_of((j // count * count + source) * ROWS, ROWS)
            code = column_ref[pl.ds(at, ROWS), :]
            kcode = jnp.concatenate([code] * (ROWS // 128), axis=1)
            seen = (kcode < qbase) | (kcode == qcode)
            scores.append(jnp.where(seen, raw * SCALE, MASKED))
        scores = jnp.concatenate(scores, axis=0)
        best = jnp.max(scores, axis=0, keepdims=True)
        weights = jnp.exp2(scores - best)
        total = jnp.sum(weights, axis=0, keepdims=True)
        mixed = jnp.dot(
            vt_ref[...], weights.astype(jnp.bfloat16), preferred_element_type=jnp.float32
        )
        out_ref[member, :HD] = (mixed / total).astype(jnp.bfloat16)
        level = best + jnp.log2(total)
        high = level.astype(jnp.bfloat16).astype(jnp.float32)
        rest = level - high
        middle = rest.astype(jnp.bfloat16).astype(jnp.float32)
        low = rest - middle
        row = lax.broadcasted_iota(jnp.int32, (16, ROWS), 0)
        stats = jnp.where(
            row == 0, high, jnp.where(row == 1, middle, jnp.where(row == 2, low, 0.0))
        )
        out_ref[member, HD:] = stats.astype(jnp.bfloat16)


def attend(queries, qcode, own_kv, other_kv, kcode):
    groups = len(queries)
    keys = kcode.shape[1]
    return pl.pallas_call(
        attend_kernel,
        in_specs=[pl.BlockSpec(memory_space=pltpu.VMEM)] * (3 + len(own_kv) + groups),
        out_shape=jax.ShapeDtypeStruct((groups, PART_ROWS, ROWS), jnp.bfloat16),
        scratch_shapes=[
            pltpu.VMEM((HD, keys), jnp.bfloat16),
            pltpu.VMEM((keys, 128), jnp.float32),
        ],
        compiler_params=pltpu.CompilerParams(vmem_limit_bytes=GRANT),
        name="attend",
    )(qcode, kcode, other_kv, *own_kv, *queries)


def combine_kernel(part_ref, out_ref):
    groups = part_ref.shape[0]
    levels = []
    for j in range(groups):
        stats = part_ref[j, HD:].astype(jnp.float32)
        levels.append(stats[0:1] + stats[1:2] + stats[2:3])
    best = levels[0]
    for level in levels[1:]:
        best = jnp.maximum(best, level)
    total = jnp.zeros_like(best)
    mixed = jnp.zeros((HD, ROWS), jnp.float32)
    for j in range(groups):
        share = jnp.exp2(levels[j] - best)
        total = total + share
        mixed = mixed + share * part_ref[j, :HD].astype(jnp.float32)
    attended = jnp.transpose(mixed / total).astype(jnp.bfloat16)
    for j in range(out_ref.shape[0]):
        out_ref[j] = attended


def combine(parts, copies):
    return pl.pallas_call(
        combine_kernel,
        out_shape=jax.ShapeDtypeStruct((copies, ROWS, HD), jnp.bfloat16),
        compiler_params=pltpu.CompilerParams(vmem_limit_bytes=GRANT),
        name="combine",
    )(parts)


def split_kernel(w_ref, out_ref):
    parts, _, width = out_ref.shape
    for j in range(parts):
        out_ref[j] = w_ref[:, j * width : (j + 1) * width]


def split(w, parts):
    return pl.pallas_call(
        split_kernel,
        in_specs=[pl.BlockSpec(memory_space=pltpu.VMEM)],
        out_shape=jax.ShapeDtypeStruct((parts, HD, w.shape[1] // parts), w.dtype),
        compiler_params=pltpu.CompilerParams(vmem_limit_bytes=GRANT),
        name="split",
    )(w)


def output_kernel(attended_ref, w_ref, out_ref):
    total = jnp.zeros(out_ref.shape, jnp.float32)
    for h in range(attended_ref.shape[0]):
        head_out = jnp.dot(attended_ref[h], w_ref[h], preferred_element_type=jnp.float32)
        total = total + head_out.astype(jnp.bfloat16).astype(jnp.float32)
    out_ref[...] = total.astype(jnp.bfloat16)


def output(attended, w):
    return pl.pallas_call(
        output_kernel,
        in_specs=[pl.BlockSpec(memory_space=pltpu.VMEM)] * 2,
        out_shape=jax.ShapeDtypeStruct((ROWS, w.shape[2]), jnp.bfloat16),
        compiler_params=pltpu.CompilerParams(vmem_limit_bytes=GRANT),
        name="output",
    )(attended, w)


def make_on_device(n_seq, n_head):
    group = CORES * BLOCK_Z
    blocks = n_seq // group
    near = [
        [g * group + b * CORES + c for b in range(BLOCK_Z)] for g in range(blocks) for c in range(CORES)
    ]
    swap = [(i, i ^ 1) for i in range(n_seq)]
    keys = CORES * blocks * ROWS

    def codes(span_order, frame_id, camera_id):
        code = (frame_id * 8 + camera_id).reshape(-1, SPAN)[span_order]
        code = code.reshape(blocks, BLOCK_Z, CORES, ROWS)
        place = lax.axis_index("seq")
        core = place % CORES
        query_code = lax.dynamic_index_in_dim(code, place // group, 0, keepdims=False)
        query_code = lax.dynamic_index_in_dim(query_code, core, 1, keepdims=False)
        key_code = lax.dynamic_index_in_dim(code, place // CORES % BLOCK_Z, 1, keepdims=False)
        own = lax.dynamic_index_in_dim(key_code, core, 1, keepdims=False)
        other = lax.dynamic_index_in_dim(key_code, 1 - core, 1, keepdims=False)
        key_code = jnp.concatenate([own, other]).reshape(1, keys)
        row = lax.broadcasted_iota(jnp.int32, (16, keys), 0)
        pair = jnp.where(row == 0, key_code >> 3, jnp.where(row == 1, key_code & 7, 0))
        return query_code[:, None, :], pair.astype(jnp.bfloat16)

    along_block = [
        [(i, i // group * group + (i + k * CORES) % group) for i in range(n_seq)]
        for k in range(BLOCK_Z)
    ]
    across = [[(i, (i + k * group) % n_seq) for i in range(n_seq)] for k in range(blocks)]

    def on_device(tokens, norm_gain, w_qkv, w_out, span_order, frame_id, camera_id):
        copies = jnp.broadcast_to(tokens[None], (n_head,) + tokens.shape)
        gathered = lax.all_to_all(copies, "head", 0, 0)
        query_code, key_code = codes(span_order, frame_id, camera_id)
        w_split = split(w_out, n_head)
        w_heads = stage(w_qkv.transpose(1, 0, 2))
        gathered, w_split, w_heads, query_code, key_code = lax.optimization_barrier(
            (gathered, w_split, w_heads, query_code, key_code)
        )
        queries, kv = project(gathered, norm_gain.reshape(1, D), w_heads)
        own_kv = [kv] * blocks
        for k in (1, blocks - 1):
            own_kv[k] = lax.ppermute(kv, "seq", across[k])
        for k in range(2, blocks - 1):
            own_kv[k] = lax.ppermute(kv, "seq", across[k])
        all_queries = [queries] + [
            lax.ppermute(queries, "seq", along_block[k]) for k in range(1, BLOCK_Z)
        ]
        w_columns = lax.all_to_all(w_split, "head", 0, 0)
        other_kv = lax.ppermute(jnp.stack(own_kv), "seq", swap)
        parts = attend(all_queries, query_code, own_kv, other_kv, key_code)
        parts, w_columns = lax.optimization_barrier((parts, w_columns))
        parts = lax.all_to_all(parts, "seq", 0, 0, axis_index_groups=near)
        attended = combine(parts, n_head)
        all_attended = lax.all_to_all(attended, "head", 0, 0)
        return output(all_attended, w_columns)

    return on_device


def solution(mesh):
    placed = (P("seq", "head"), P(), P(None, None, "head"), P("head", None), P(), P(), P())
    return jax.shard_map(
        make_on_device(mesh.shape["seq"], mesh.shape["head"]),
        mesh=mesh,
        in_specs=placed,
        out_specs=P("seq", "head"),
        check_vma=False,
    )
```

time: 170 us -> 142 us (0.84)
  blocking collectives: 51 us -> 31.1 us
  waiting for transfers between devices: 47.9 us -> 32.8 us
  starting transfers between devices: 53.5 us -> 59.7 us
    all_to_all x1, blocking collectives: 39.9 us -> 19.4 us  [on_device(): all_attended = lax.all_to_all(attended, 'head', 0, 0)]
    ppermute x7 -> x4, waiting for transfers between devices: 22.3 us -> 8.07 us  [the longest x3 8.07 us: on_device(): own_kv[k] = lax.ppermute(kv, 'seq', across[k])]
    ppermute x7 -> x4, starting transfers between devices: 21.9 us -> 27.4 us  [the longest x3 25.5 us: on_device(): own_kv[k] = lax.ppermute(kv, 'seq', across[k])]
  transfers between devices with their start and end apart: 12 -> 9, of which waited for: 8 -> 5; matrix products, arithmetic and copies ran while one was open for 0% -> 1% of each run, Pallas kernels for 0% -> 6%
where the time goes in v3:
time: 142 us; the launch traced here: 140 us
  starting transfers between devices  59.7 us (42%)
  waiting for transfers between devices  32.8 us (23%)
  blocking collectives  31.1 us (22%)
  Pallas kernels  10.6 us (7%)
  local copies, waits for them, and re-layouts  5.79 us (4%)
    ppermute x3, starting transfers between devices, on_device(): own_kv[k] = lax.ppermute(kv, 'seq', across[k])  25.5 us
    all_to_all x1, waiting for transfers between devices, on_device(): gathered = lax.all_to_all(copies, 'head', 0, 0)  20.8 us
    all_to_all x1, blocking collectives, on_device(): all_attended = lax.all_to_all(attended, 'head', 0, 0)  19.4 us
    ppermute x3, starting transfers between devices, on_device(): lax.ppermute(queries, 'seq', along_block[k])  15 us
    all_to_all x1, blocking collectives, on_device(): parts = lax.all_to_all(parts, 'seq', 0, 0, axis_index_groups=near)  11.7 us
    all_to_all x1, starting transfers between devices, on_device(): gathered = lax.all_to_all(copies, 'head', 0, 0)  10.1 us
    ppermute x3, waiting for transfers between devices, on_device(): own_kv[k] = lax.ppermute(kv, 'seq', across[k])  8.07 us
    all_to_all x1, starting transfers between devices, on_device(): w_columns = lax.all_to_all(w_split, 'head', 0, 0)  7.24 us
  transfers between devices with their start and end apart: 9, of which 5 were waited for; matrix products, arithmetic and copies ran while one was open for 1% of the time, Pallas kernels for 6%

profile of v3, /device:TPU:6, one launch (start us, length us, event | category | flops | bytes accessed | tf_op | source)
XLA Modules:
  0.0 140.4 jit_solution(14133986583951696644)
XLA Ops:
  0.0 2.5 %broadcast_in_dim.28 = bf16[16,256,256]{2,1,0:T(8,128)(2,1)} broadcast(bf16[256,256]{1,0:T(8,128)(2,1)} %param.7), dimensions={1,2} | broadcast | bytes 2228224 | tf_op jit(solution)/shard_map/broadcast_in_dim | solution.py:242
  2.5 10.1 %all-to-all-start = ((bf16[16,256,256]{2,1,0:T(8,128)(2,1)}), bf16[16,256,256]{2,1,0:T(8,128)(2,1)}, u32[]{:S(2)}, u32[]{:S(2)}) async-start(bf16[16,256,256]{2,1,0:T(8,128)(2,1)} %broadcast_in_dim.28), calls=%async_computation | async-start | bytes 4194304 | tf_op jit(solution)/shard_map/all_to_all | solution.py:243
  12.7 2.3 %copy-done.1 = bf16[4096,3,128]{2,0,1:T(8,128)(2,1)S(1)} copy-done((bf16[4096,3,128]{2,0,1:T(8,128)(2,1)S(1)}, bf16[4096,3,128]{2,0,1:T(8,128)(2,1)}, u32[]{:S(2)}) %copy-start.1) | copy-done | bytes 3145752
  14.9 0.4 stage.1.w_ref
  15.3 0.2 copy-done.6
  15.7 0.6 gather_fusion
  16.6 20.8 %all-to-all-done.x_ref = bf16[16,256,256]{2,1,0:T(8,128)(2,1)} async-done(((bf16[16,256,256]{2,1,0:T(8,128)(2,1)}), bf16[16,256,256]{2,1,0:T(8,128)(2,1)}, u32[]{:S(2)}, u32[]{:S(2)}) %all-to-all-start) | async-done | bytes 2097184 | tf_op jit(solution)/shard_map/all_to_all | solution.py:243
  37.4 7.2 %all-to-all-start.1 = ((bf16[16,128,256]{2,1,0:T(8,128)(2,1)}), bf16[16,128,256]{2,1,0:T(8,128)(2,1)}, u32[]{:S(2)}, u32[]{:S(2)}) async-start(bf16[16,128,256]{2,1,0:T(8,128)(2,1)} %copy-done), calls=%async_computation.1 | async-start | bytes 2097152 | tf_op jit(solution)/shard_map/all_to_all | solution.py:259
  44.6 3.3 %project.1 = (bf16[256,128]{1,0:T(8,128)(2,1)S(1)}, bf16[256,256]{1,0:T(8,128)(2,1)S(1)}) custom-call(bf16[16,256,256]{2,1,0:T(8,128)(2,1)} %all-to-all-done.x_ref, f32[1,4096]{1,0:T(1,128)S(1)} %bitcast.25, bf16[3,4096,128]{2,1,0:T(8,128)(2,1)S(1)} %stage.1.w_ref), custom_call_target="tpu_custom_call" | custom-call | tf_op jit(solution)/shard_map/project/pallas_call | solution.py:61
  47.9 12.8 %collective-permute-start.2 = (bf16[256,256]{1,0:T(8,128)(2,1)S(1)}, bf16[256,256]{1,0:T(8,128)(2,1)S(1)}, u32[]{:S(2)}, u32[]{:S(2)}) collective-permute-start(bf16[256,256]{1,0:T(8,128)(2,1)S(1)} %get-tuple-element.18.refs_0_), channel_id=1, source_target_pairs={{0,384},{16,400},{32,416},{48,432},{64,448},{80,464},{96,480},{112... | collective-permute-start | bytes 393224 | tf_op jit(solution)/shard_map/ppermute | solution.py:253
  60.7 4.9 %collective-permute-start.1 = (bf16[256,256]{1,0:T(8,128)(2,1)S(1)}, bf16[256,256]{1,0:T(8,128)(2,1)S(1)}, u32[]{:S(2)}, u32[]{:S(2)}) collective-permute-start(bf16[256,256]{1,0:T(8,128)(2,1)S(1)} %get-tuple-element.18.refs_0_), channel_id=1, source_target_pairs={{0,256},{16,272},{32,288},{48,304},{64,320},{80,336},{96,352},{112... | collective-permute-start | bytes 393224 | tf_op jit(solution)/shard_map/ppermute | solution.py:255
  65.6 7.8 %collective-permute-start = (bf16[256,256]{1,0:T(8,128)(2,1)S(1)}, bf16[256,256]{1,0:T(8,128)(2,1)S(1)}, u32[]{:S(2)}, u32[]{:S(2)}) collective-permute-start(bf16[256,256]{1,0:T(8,128)(2,1)S(1)} %get-tuple-element.18.refs_0_), channel_id=1, source_target_pairs={{0,128},{16,144},{32,160},{48,176},{64,192},{80,208},{96,224},{112... | collective-permute-start | bytes 393224 | tf_op jit(solution)/shard_map/ppermute | solution.py:253
  73.5 5.2 %collective-permute-done.2.refs_3_ = bf16[256,256]{1,0:T(8,128)(2,1)S(1)} collective-permute-done((bf16[256,256]{1,0:T(8,128)(2,1)S(1)}, bf16[256,256]{1,0:T(8,128)(2,1)S(1)}, u32[]{:S(2)}, u32[]{:S(2)}) %collective-permute-start.2) | collective-permute-done | bytes 131104 | tf_op jit(solution)/shard_map/ppermute | solution.py:253
  78.7 2.8 %collective-permute-done.1.refs_2_ = bf16[256,256]{1,0:T(8,128)(2,1)S(1)} collective-permute-done((bf16[256,256]{1,0:T(8,128)(2,1)S(1)}, bf16[256,256]{1,0:T(8,128)(2,1)S(1)}, u32[]{:S(2)}, u32[]{:S(2)}) %collective-permute-start.1) | collective-permute-done | bytes 131104 | tf_op jit(solution)/shard_map/ppermute | solution.py:255
  81.6 1.9 %collective-permute-start.3 = (bf16[4,256,256]{2,1,0:T(8,128)(2,1)S(1)}, bf16[4,256,256]{2,1,0:T(8,128)(2,1)S(1)}, u32[]{:S(2)}, u32[]{:S(2)}) collective-permute-start(bf16[4,256,256]{2,1,0:T(8,128)(2,1)S(1)} %pad_maximum_fusion), channel_id=1, source_target_pairs={{0,16},{16,0},{32,48},{48,32},{64,80},{80,64},{96,112},{112,96},{1... | collective-permute-start | bytes 1572872 | tf_op jit(solution)/shard_map/ppermute | solution.py:260
  83.5 5.9 %collective-permute-start.4 = (bf16[256,128]{1,0:T(8,128)(2,1)S(1)}, bf16[256,128]{1,0:T(8,128)(2,1)S(1)}, u32[]{:S(2)}, u32[]{:S(2)}) collective-permute-start(bf16[256,128]{1,0:T(8,128)(2,1)S(1)} %get-tuple-element.19.refs_4_), channel_id=1, source_target_pairs={{0,32},{16,48},{32,64},{48,80},{64,96},{80,112},{96,0},{112,16},{1... | collective-permute-start | bytes 196616 | tf_op jit(solution)/shard_map/ppermute | solution.py:257
  89.4 6.9 %collective-permute-start.5 = (bf16[256,128]{1,0:T(8,128)(2,1)S(1)}, bf16[256,128]{1,0:T(8,128)(2,1)S(1)}, u32[]{:S(2)}, u32[]{:S(2)}) collective-permute-start(bf16[256,128]{1,0:T(8,128)(2,1)S(1)} %get-tuple-element.19.refs_4_), channel_id=1, source_target_pairs={{0,64},{16,80},{32,96},{48,112},{64,0},{80,16},{96,32},{112,48},{1... | collective-permute-start | bytes 196616 | tf_op jit(solution)/shard_map/ppermute | solution.py:257
  96.3 2.2 %collective-permute-start.6 = (bf16[256,128]{1,0:T(8,128)(2,1)S(1)}, bf16[256,128]{1,0:T(8,128)(2,1)S(1)}, u32[]{:S(2)}, u32[]{:S(2)}) collective-permute-start(bf16[256,128]{1,0:T(8,128)(2,1)S(1)} %get-tuple-element.19.refs_4_), channel_id=1, source_target_pairs={{0,96},{16,112},{32,0},{48,16},{64,32},{80,48},{96,64},{112,80},{1... | collective-permute-start | bytes 196616 | tf_op jit(solution)/shard_map/ppermute | solution.py:257
  98.5 1.6 %collective-permute-done.5.refs_6_ = bf16[256,128]{1,0:T(8,128)(2,1)S(1)} collective-permute-done((bf16[256,128]{1,0:T(8,128)(2,1)S(1)}, bf16[256,128]{1,0:T(8,128)(2,1)S(1)}, u32[]{:S(2)}, u32[]{:S(2)}) %collective-permute-start.5) | collective-permute-done | bytes 65568 | tf_op jit(solution)/shard_map/ppermute | solution.py:257
  100.1 2.3 %collective-permute-done.6.refs_7_ = bf16[256,128]{1,0:T(8,128)(2,1)S(1)} collective-permute-done((bf16[256,128]{1,0:T(8,128)(2,1)S(1)}, bf16[256,128]{1,0:T(8,128)(2,1)S(1)}, u32[]{:S(2)}, u32[]{:S(2)}) %collective-permute-start.6) | collective-permute-done | bytes 65568 | tf_op jit(solution)/shard_map/ppermute | solution.py:257
  102.4 4.1 %attend.1 = bf16[4,144,256]{2,1,0:T(8,128)(2,1)S(1)} custom-call(s32[4,1,256]{2,1,0:T(1,128)S(1)} %dynamic-slice_bitcast_fusion.qcode_ref, bf16[16,2048]{1,0:T(8,128)(2,1)S(1)} %select_convert_fusion.kcode_ref, bf16[4,256,256]{2,1,0:T(8,128)(2,1)S(1)} %collective-permute-done.3.other_ref, bf16[256,256]{1,0:T(8,128)(2,1)S(1)} %get-tuple-element.18.refs_0_, ...), custom_call_target="tpu_custom_call" | custom-call | tf_op jit(solution)/shard_map/attend/pallas_call | solution.py:135
  106.6 11.7 %all_to_all.20.part_ref = bf16[4,144,256]{2,1,0:T(8,128)(2,1)S(1)} all-to-all(bf16[4,144,256]{2,1,0:T(8,128)(2,1)S(1)} %attend.1), channel_id=1, replica_groups={{0,32,64,96},{16,48,80,112},{128,160,192,224},{144,176,208,240},{256,28..., dimensions={0} | all-to-all | bytes 589824 | tf_op jit(solution)/shard_map/all_to_all | solution.py:263
  118.5 19.4 %all_to_all.21.attended_ref = bf16[16,256,128]{2,1,0:T(8,128)(2,1)S(1)} all-to-all(bf16[16,256,128]{2,1,0:T(8,128)(2,1)S(1)} %combine.1), channel_id=1, replica_groups=mesh['seq'=32,'head'=16] {'head'}, dimensions={0} | all-to-all | bytes 2097152 | tf_op jit(solution)/shard_map/all_to_all | solution.py:265
  137.9 2.6 %output.1 = bf16[256,256]{1,0:T(8,128)(2,1)} custom-call(bf16[16,256,128]{2,1,0:T(8,128)(2,1)S(1)} %all_to_all.21.attended_ref, bf16[16,128,256]{2,1,0:T(8,128)(2,1)} %all-to-all-done.1.w_ref), custom_call_target="tpu_custom_call" | custom-call | tf_op jit(solution)/shard_map/output/pallas_call | solution.py:202
  (31 shorter events, 0.7 us)
Async XLA Ops:
  0.0 12.6 %copy-start.2 = (bf16[128,4096]{1,0:T(8,128)(2,1)S(1)}, bf16[128,4096]{1,0:T(8,128)(2,1)}, u32[]{:S(2)}) copy-start(bf16[128,4096]{1,0:T(8,128)(2,1)} %w_ref.1) | copy-start | bytes 3145732
  2.5 34.9 %all-to-all-start = ((bf16[16,256,256]{2,1,0:T(8,128)(2,1)}), bf16[16,256,256]{2,1,0:T(8,128)(2,1)}, u32[]{:S(2)}, u32[]{:S(2)}) async-start(bf16[16,256,256]{2,1,0:T(8,128)(2,1)} %broadcast_in_dim.28), calls=%async_computation | async-start | bytes 4194304 | tf_op jit(solution)/shard_map/all_to_all | solution.py:243
  12.6 2.7 %copy-start = (bf16[16,128,256]{2,1,0:T(8,128)(2,1)}, bf16[16,128,256]{2,1,0:T(8,128)(2,1)S(1)}, u32[]{:S(2)}) copy-start(bf16[16,128,256]{2,1,0:T(8,128)(2,1)S(1)} %split.1) | copy-start | bytes 3145732
  12.7 2.3 %copy-start.1 = (bf16[4096,3,128]{2,0,1:T(8,128)(2,1)S(1)}, bf16[4096,3,128]{2,0,1:T(8,128)(2,1)}, u32[]{:S(2)}) copy-start(bf16[4096,3,128]{2,0,1:T(8,128)(2,1)} %param.9) | copy-start | bytes 9437188
  14.9 0.7 copy-start.6
  14.9 0.8 copy-start.4
  14.9 0.8 copy-start.5
  14.9 29.7 %copy-start.3 = (f32[4096]{0:T(1024)S(1)}, f32[4096]{0:T(1024)}, u32[]{:S(2)}) copy-start(f32[4096]{0:T(1024)} %param.8) | copy-start | bytes 49156
  37.4 69.2 %all-to-all-start.1 = ((bf16[16,128,256]{2,1,0:T(8,128)(2,1)}), bf16[16,128,256]{2,1,0:T(8,128)(2,1)}, u32[]{:S(2)}, u32[]{:S(2)}) async-start(bf16[16,128,256]{2,1,0:T(8,128)(2,1)} %copy-done), calls=%async_computation.1 | async-start | bytes 2097152 | tf_op jit(solution)/shard_map/all_to_all | solution.py:259
  47.9 30.8 %collective-permute-start.2 = (bf16[256,256]{1,0:T(8,128)(2,1)S(1)}, bf16[256,256]{1,0:T(8,128)(2,1)S(1)}, u32[]{:S(2)}, u32[]{:S(2)}) collective-permute-start(bf16[256,256]{1,0:T(8,128)(2,1)S(1)} %get-tuple-element.18.refs_0_), channel_id=1, source_target_pairs={{0,384},{16,400},{32,416},{48,432},{64,448},{80,464},{96,480},{112... | collective-permute-start | bytes 393224 | tf_op jit(solution)/shard_map/ppermute | solution.py:253
  60.7 20.8 %collective-permute-start.1 = (bf16[256,256]{1,0:T(8,128)(2,1)S(1)}, bf16[256,256]{1,0:T(8,128)(2,1)S(1)}, u32[]{:S(2)}, u32[]{:S(2)}) collective-permute-start(bf16[256,256]{1,0:T(8,128)(2,1)S(1)} %get-tuple-element.18.refs_0_), channel_id=1, source_target_pairs={{0,256},{16,272},{32,288},{48,304},{64,320},{80,336},{96,352},{112... | collective-permute-start | bytes 393224 | tf_op jit(solution)/shard_map/ppermute | solution.py:255
  65.6 15.9 %collective-permute-start = (bf16[256,256]{1,0:T(8,128)(2,1)S(1)}, bf16[256,256]{1,0:T(8,128)(2,1)S(1)}, u32[]{:S(2)}, u32[]{:S(2)}) collective-permute-start(bf16[256,256]{1,0:T(8,128)(2,1)S(1)} %get-tuple-element.18.refs_0_), channel_id=1, source_target_pairs={{0,128},{16,144},{32,160},{48,176},{64,192},{80,208},{96,224},{112... | collective-permute-start | bytes 393224 | tf_op jit(solution)/shard_map/ppermute | solution.py:253
  81.6 20.8 %collective-permute-start.3 = (bf16[4,256,256]{2,1,0:T(8,128)(2,1)S(1)}, bf16[4,256,256]{2,1,0:T(8,128)(2,1)S(1)}, u32[]{:S(2)}, u32[]{:S(2)}) collective-permute-start(bf16[4,256,256]{2,1,0:T(8,128)(2,1)S(1)} %pad_maximum_fusion), channel_id=1, source_target_pairs={{0,16},{16,0},{32,48},{48,32},{64,80},{80,64},{96,112},{112,96},{1... | collective-permute-start | bytes 1572872 | tf_op jit(solution)/shard_map/ppermute | solution.py:260
  83.5 15.0 %collective-permute-start.4 = (bf16[256,128]{1,0:T(8,128)(2,1)S(1)}, bf16[256,128]{1,0:T(8,128)(2,1)S(1)}, u32[]{:S(2)}, u32[]{:S(2)}) collective-permute-start(bf16[256,128]{1,0:T(8,128)(2,1)S(1)} %get-tuple-element.19.refs_4_), channel_id=1, source_target_pairs={{0,32},{16,48},{32,64},{48,80},{64,96},{80,112},{96,0},{112,16},{1... | collective-permute-start | bytes 196616 | tf_op jit(solution)/shard_map/ppermute | solution.py:257
  89.4 10.7 %collective-permute-start.5 = (bf16[256,128]{1,0:T(8,128)(2,1)S(1)}, bf16[256,128]{1,0:T(8,128)(2,1)S(1)}, u32[]{:S(2)}, u32[]{:S(2)}) collective-permute-start(bf16[256,128]{1,0:T(8,128)(2,1)S(1)} %get-tuple-element.19.refs_4_), channel_id=1, source_target_pairs={{0,64},{16,80},{32,96},{48,112},{64,0},{80,16},{96,32},{112,48},{1... | collective-permute-start | bytes 196616 | tf_op jit(solution)/shard_map/ppermute | solution.py:257
  96.3 6.2 %collective-permute-start.6 = (bf16[256,128]{1,0:T(8,128)(2,1)S(1)}, bf16[256,128]{1,0:T(8,128)(2,1)S(1)}, u32[]{:S(2)}, u32[]{:S(2)}) collective-permute-start(bf16[256,128]{1,0:T(8,128)(2,1)S(1)} %get-tuple-element.19.refs_4_), channel_id=1, source_target_pairs={{0,96},{16,112},{32,0},{48,16},{64,32},{80,48},{96,64},{112,80},{1... | collective-permute-start | bytes 196616 | tf_op jit(solution)/shard_map/ppermute | solution.py:257

commit v4 on v3

--- a/solution.py
+++ b/solution.py
@@ -20,6 +20,27 @@
 PART_ROWS = HD + 16
 
 
+def spread_kernel(x_ref, out_ref, sems):
+    sends = [
+        pltpu.make_async_copy(x_ref, out_ref.at[j], sems.at[j]) for j in range(out_ref.shape[0])
+    ]
+    for send in sends:
+        send.start()
+    for send in sends:
+        send.wait()
+
+
+def spread(x, copies):
+    return pl.pallas_call(
+        spread_kernel,
+        in_specs=[pl.BlockSpec(memory_space=pltpu.VMEM)],
+        out_specs=pl.BlockSpec(memory_space=pltpu.HBM),
+        out_shape=jax.ShapeDtypeStruct((copies,) + x.shape, x.dtype),
+        scratch_shapes=[pltpu.SemaphoreType.DMA((copies,))],
+        name="spread",
+    )(x)
+
+
 def stage_kernel(w_ref, out_ref):
     out_ref[...] = w_ref[...]
 
@@ -38,34 +59,64 @@
     )(w)
 
 
-def project_kernel(x_ref, gain_ref, w_ref, q_ref, kv_ref):
-    blocks, _, width = x_ref.shape
-    total = jnp.zeros((ROWS, width), jnp.float32)
-    for j in range(blocks):
-        piece = x_ref[j].astype(jnp.float32)
-        total = total + piece * piece
-    mean = jnp.sum(total, axis=1, keepdims=True) * (1.0 / D)
-    inverse = jnp.broadcast_to(lax.rsqrt(mean + EPSILON), (ROWS, width))
-    sums = jnp.zeros((ROWS, 3 * HD), jnp.float32)
-    for j in range(blocks):
-        cols = slice(j * width, (j + 1) * width)
-        normed = (x_ref[j].astype(jnp.float32) * inverse * gain_ref[:, cols]).astype(jnp.bfloat16)
-        weights = jnp.concatenate([w_ref[0, cols], w_ref[1, cols], w_ref[2, cols]], axis=1)
+def project_kernel(x_ref, gain_ref, w_ref, q_ref, kv_ref, inv_ref, acc_ref):
+    step = pl.program_id(0)
+    blocks = x_ref.shape[0]
+    per_step = blocks // pl.num_programs(0)
+
+    @pl.when(step == 0)
+    def _():
+        total = jnp.zeros((ROWS, x_ref.shape[2]), jnp.float32)
+        for j in range(blocks):
+            piece = x_ref[j].astype(jnp.float32)
+            total = total + piece * piece
+        mean = jnp.sum(total, axis=1, keepdims=True) * (1.0 / D)
+        inv_ref[...] = jnp.broadcast_to(lax.rsqrt(mean + EPSILON), inv_ref.shape)
+        acc_ref[...] = jnp.zeros_like(acc_ref)
+
+    width = x_ref.shape[2]
+    inverse = jnp.concatenate([inv_ref[...]] * (width // 128), axis=1)
+    sums = acc_ref[...]
+    for i in range(per_step):
+        piece = x_ref[step * per_step + i].astype(jnp.float32)
+        gain = gain_ref[:, i * width : (i + 1) * width]
+        normed = (piece * inverse * gain).astype(jnp.bfloat16)
+        rows = slice(i * width, (i + 1) * width)
+        weights = jnp.concatenate([w_ref[0, rows], w_ref[1, rows], w_ref[2, rows]], axis=1)
         sums = sums + jnp.dot(normed, weights, preferred_element_type=jnp.float32)
-    done = sums.astype(jnp.bfloat16)
-    q_ref[...] = done[:, :HD]
-    kv_ref[...] = done[:, HD:]
+    acc_ref[...] = sums
+
+    @pl.when(step == pl.num_programs(0) - 1)
+    def _():
+        done = sums.astype(jnp.bfloat16)
+        q_ref[...] = done[:, :HD]
+        kv_ref[...] = done[:, HD:]
 
 
 def project(x, gain, w):
+    blocks, _, width = x.shape
+    steps = 4
+    depth = D // steps
     return pl.pallas_call(
         project_kernel,
-        in_specs=[pl.BlockSpec(memory_space=pltpu.VMEM)] * 3,
-        out_specs=[pl.BlockSpec(memory_space=pltpu.VMEM)] * 2,
+        grid=(steps,),
+        in_specs=[
+            pl.BlockSpec((blocks, ROWS, width), lambda s: (0, 0, 0)),
+            pl.BlockSpec((1, depth), lambda s: (0, s)),
+            pl.BlockSpec((3, depth, HD), lambda s: (0, s, 0)),
+        ],
+        out_specs=[
+            pl.BlockSpec((ROWS, HD), lambda s: (0, 0)),
+            pl.BlockSpec((ROWS, 2 * HD), lambda s: (0, 0)),
+        ],
         out_shape=[
             jax.ShapeDtypeStruct((ROWS, HD), jnp.bfloat16),
             jax.ShapeDtypeStruct((ROWS, 2 * HD), jnp.bfloat16),
         ],
+        scratch_shapes=[
+            pltpu.VMEM((ROWS, 128), jnp.float32),
+            pltpu.VMEM((ROWS, 3 * HD), jnp.float32),
+        ],
         compiler_params=pltpu.CompilerParams(vmem_limit_bytes=GRANT),
         name="project",
     )(x, gain, w)
@@ -73,7 +124,9 @@
 
 def attend_kernel(qcode_ref, kcode_ref, other_ref, *refs):
     count = other_ref.shape[0]
-    own_refs, q_refs = refs[:count], refs[count:-3]
+    own_refs = refs[:count]
+    queries_ref, neighbour_ref, pair_ref = refs[count:-3]
+    q_refs = [queries_ref, neighbour_ref, pair_ref.at[0], pair_ref.at[1]]
     out_ref, vt_ref, column_ref = refs[-3:]
     groups = len(q_refs)
     far_block = lax.div(lax.axis_index("seq"), CORES * groups)
@@ -90,7 +143,7 @@
         vt_ref[:, j * ROWS : (j + 1) * ROWS] = jnp.transpose(ref[:, HD:])
 
     for shift, q_ref in enumerate(q_refs):
-        member = lax.rem(block + (groups - shift), groups)
+        member = lax.bitwise_xor(block, shift)
         qcode = qcode_ref[member]
         qbase = (qcode & -8).astype(jnp.float32)
         qcode = qcode.astype(jnp.float32)
@@ -130,11 +183,11 @@
 
 
 def attend(queries, qcode, own_kv, other_kv, kcode):
-    groups = len(queries)
+    groups = qcode.shape[0]
     keys = kcode.shape[1]
     return pl.pallas_call(
         attend_kernel,
-        in_specs=[pl.BlockSpec(memory_space=pltpu.VMEM)] * (3 + len(own_kv) + groups),
+        in_specs=[pl.BlockSpec(memory_space=pltpu.VMEM)] * (3 + len(own_kv) + len(queries)),
         out_shape=jax.ShapeDtypeStruct((groups, PART_ROWS, ROWS), jnp.bfloat16),
         scratch_shapes=[
             pltpu.VMEM((HD, keys), jnp.bfloat16),
@@ -232,15 +285,12 @@
         pair = jnp.where(row == 0, key_code >> 3, jnp.where(row == 1, key_code & 7, 0))
         return query_code[:, None, :], pair.astype(jnp.bfloat16)
 
-    along_block = [
-        [(i, i // group * group + (i + k * CORES) % group) for i in range(n_seq)]
-        for k in range(BLOCK_Z)
-    ]
+    flip_one = [(i, i ^ CORES) for i in range(n_seq)]
+    flip_two = [(i, i ^ 2 * CORES) for i in range(n_seq)]
     across = [[(i, (i + k * group) % n_seq) for i in range(n_seq)] for k in range(blocks)]
 
     def on_device(tokens, norm_gain, w_qkv, w_out, span_order, frame_id, camera_id):
-        copies = jnp.broadcast_to(tokens[None], (n_head,) + tokens.shape)
-        gathered = lax.all_to_all(copies, "head", 0, 0)
+        gathered = lax.all_to_all(spread(tokens, n_head), "head", 0, 0)
         query_code, key_code = codes(span_order, frame_id, camera_id)
         w_split = split(w_out, n_head)
         w_heads = stage(w_qkv.transpose(1, 0, 2))
@@ -251,14 +301,13 @@
         own_kv = [kv] * blocks
         for k in (1, blocks - 1):
             own_kv[k] = lax.ppermute(kv, "seq", across[k])
+        neighbour = lax.ppermute(queries, "seq", flip_one)
         for k in range(2, blocks - 1):
             own_kv[k] = lax.ppermute(kv, "seq", across[k])
-        all_queries = [queries] + [
-            lax.ppermute(queries, "seq", along_block[k]) for k in range(1, BLOCK_Z)
-        ]
+        pair = lax.ppermute(jnp.stack([queries, neighbour]), "seq", flip_two)
         w_columns = lax.all_to_all(w_split, "head", 0, 0)
         other_kv = lax.ppermute(jnp.stack(own_kv), "seq", swap)
-        parts = attend(all_queries, query_code, own_kv, other_kv, key_code)
+        parts = attend((queries, neighbour, pair), query_code, own_kv, other_kv, key_code)
         parts, w_columns = lax.optimization_barrier((parts, w_columns))
         parts = lax.all_to_all(parts, "seq", 0, 0, axis_index_groups=near)
         attended = combine(parts, n_head)

time: 142 us -> 149 us (1.049)
  waiting for transfers between devices: 32.8 us -> 38 us
  blocking collectives: 31.1 us -> 35.2 us
  Pallas kernels: 10.6 us -> 13.8 us
  local copies, waits for them, and re-layouts: 5.79 us -> 3.29 us
  starting transfers between devices: 59.7 us -> 57.5 us
    ppermute x3 -> x2, waiting for transfers between devices: 3.93 us -> 9.11 us  [the longest x1 6.37 us: on_device(): pair = lax.ppermute(jnp.stack([queries, neighbour]), 'seq', flip_two)]
    pallas_call x1 -> x2, Pallas kernels: 3.28 us -> 6.46 us  [the longest x1 4.02 us: project(): pl.pallas_call(project_kernel, grid=(steps,), in_specs=[pl.BlockSpec((blo...]
    all_to_all x1, blocking collectives: 11.7 us -> 14.3 us  [on_device(): parts = lax.all_to_all(parts, 'seq', 0, 0, axis_index_groups=near)]
    broadcast_in_dim x1 -> x0, local copies, waits for them, and re-layouts: 2.49 us -> none  [on_device(): copies = jnp.broadcast_to(tokens[None], (n_head,) + tokens.shape)]
    ppermute x3 -> x2, starting transfers between devices: 15 us -> 12.7 us  [the longest x1 6.88 us: on_device(): pair = lax.ppermute(jnp.stack([queries, neighbour]), 'seq', flip_two)]
    all_to_all x1, blocking collectives: 19.4 us -> 20.9 us  [on_device(): all_attended = lax.all_to_all(attended, 'head', 0, 0)]
  transfers between devices with their start and end apart: 9 -> 8, of which waited for: 5 -> 5; matrix products, arithmetic and copies ran while one was open for 1% -> 1% of each run, Pallas kernels for 6% -> 6%
where the time goes in v4:
time: 149 us; the launch traced here: 148 us
  starting transfers between devices  57.5 us (39%)
  waiting for transfers between devices  38 us (26%)
  blocking collectives  35.2 us (24%)
  Pallas kernels  13.8 us (9%)
  local copies, waits for them, and re-layouts  3.29 us (2%)
    ppermute x3, starting transfers between devices, on_device(): own_kv[k] = lax.ppermute(kv, 'seq', across[k])  25.5 us
    all_to_all x1, blocking collectives, on_device(): all_attended = lax.all_to_all(attended, 'head', 0, 0)  20.9 us
    all_to_all x1, waiting for transfers between devices, on_device(): gathered = lax.all_to_all(spread(tokens, n_head), 'head', 0, 0)  20.8 us
    all_to_all x1, blocking collectives, on_device(): parts = lax.all_to_all(parts, 'seq', 0, 0, axis_index_groups=near)  14.3 us
    all_to_all x1, starting transfers between devices, on_device(): gathered = lax.all_to_all(spread(tokens, n_head), 'head', 0, 0)  10.1 us
    ppermute x3, waiting for transfers between devices, on_device(): own_kv[k] = lax.ppermute(kv, 'seq', across[k])  8.05 us
    all_to_all x1, starting transfers between devices, on_device(): w_columns = lax.all_to_all(w_split, 'head', 0, 0)  7.23 us
    ppermute x1, starting transfers between devices, on_device(): pair = lax.ppermute(jnp.stack([queries, neighbour]), 'seq', flip_two)  6.88 us
  transfers between devices with their start and end apart: 8, of which 5 were waited for; matrix products, arithmetic and copies ran while one was open for 1% of the time, Pallas kernels for 6%

profile of v4, /device:TPU:6, one launch (start us, length us, event | category | flops | bytes accessed | tf_op | source)
XLA Modules:
  0.0 148.2 jit_solution(16052550479270607102)
XLA Ops:
  0.0 2.4 %spread.1 = bf16[16,256,256]{2,1,0:T(8,128)(2,1)} custom-call(bf16[256,256]{1,0:T(8,128)(2,1)} %x_ref.1), custom_call_target="tpu_custom_call" | custom-call | tf_op jit(solution)/shard_map/spread/pallas_call | solution.py:34
  2.5 10.1 %all-to-all-start = ((bf16[16,256,256]{2,1,0:T(8,128)(2,1)}), bf16[16,256,256]{2,1,0:T(8,128)(2,1)}, u32[]{:S(2)}, u32[]{:S(2)}) async-start(bf16[16,256,256]{2,1,0:T(8,128)(2,1)} %spread.1), calls=%async_computation | async-start | bytes 4194304 | tf_op jit(solution)/shard_map/all_to_all | solution.py:293
  12.6 2.3 %copy-done.1 = bf16[4096,3,128]{2,0,1:T(8,128)(2,1)S(1)} copy-done((bf16[4096,3,128]{2,0,1:T(8,128)(2,1)S(1)}, bf16[4096,3,128]{2,0,1:T(8,128)(2,1)}, u32[]{:S(2)}) %copy-start.1) | copy-done | bytes 3145752
  14.9 0.4 stage.1.w_ref
  15.3 0.2 copy-done.6
  15.7 0.6 gather_fusion
  16.5 20.8 %all-to-all-done.x_ref = bf16[16,256,256]{2,1,0:T(8,128)(2,1)} async-done(((bf16[16,256,256]{2,1,0:T(8,128)(2,1)}), bf16[16,256,256]{2,1,0:T(8,128)(2,1)}, u32[]{:S(2)}, u32[]{:S(2)}) %all-to-all-start) | async-done | bytes 2097184 | tf_op jit(solution)/shard_map/all_to_all | solution.py:293
  37.4 7.2 %all-to-all-start.1 = ((bf16[16,128,256]{2,1,0:T(8,128)(2,1)}), bf16[16,128,256]{2,1,0:T(8,128)(2,1)}, u32[]{:S(2)}, u32[]{:S(2)}) async-start(bf16[16,128,256]{2,1,0:T(8,128)(2,1)} %copy-done), calls=%async_computation.1 | async-start | bytes 2097152 | tf_op jit(solution)/shard_map/all_to_all | solution.py:308
  44.6 4.0 %project.1 = (bf16[256,128]{1,0:T(8,128)(2,1)S(1)}, bf16[256,256]{1,0:T(8,128)(2,1)S(1)}) custom-call(bf16[16,256,256]{2,1,0:T(8,128)(2,1)} %all-to-all-done.x_ref, f32[1,4096]{1,0:T(1,128)S(1)} %bitcast.29, bf16[3,4096,128]{2,1,0:T(8,128)(2,1)S(1)} %stage.1.w_ref), custom_call_target="tpu_custom_call" | custom-call | tf_op jit(solution)/shard_map/project/pallas_call | solution.py:100
  48.6 12.8 %collective-permute-start.2 = (bf16[256,256]{1,0:T(8,128)(2,1)S(1)}, bf16[256,256]{1,0:T(8,128)(2,1)S(1)}, u32[]{:S(2)}, u32[]{:S(2)}) collective-permute-start(bf16[256,256]{1,0:T(8,128)(2,1)S(1)} %get-tuple-element.18.refs_0_), channel_id=1, source_target_pairs={{0,384},{16,400},{32,416},{48,432},{64,448},{80,464},{96,480},{112... | collective-permute-start | bytes 393224 | tf_op jit(solution)/shard_map/ppermute | solution.py:303
  61.4 4.9 %collective-permute-start.1 = (bf16[256,256]{1,0:T(8,128)(2,1)S(1)}, bf16[256,256]{1,0:T(8,128)(2,1)S(1)}, u32[]{:S(2)}, u32[]{:S(2)}) collective-permute-start(bf16[256,256]{1,0:T(8,128)(2,1)S(1)} %get-tuple-element.18.refs_0_), channel_id=1, source_target_pairs={{0,256},{16,272},{32,288},{48,304},{64,320},{80,336},{96,352},{112... | collective-permute-start | bytes 393224 | tf_op jit(solution)/shard_map/ppermute | solution.py:306
  66.3 7.8 %collective-permute-start = (bf16[256,256]{1,0:T(8,128)(2,1)S(1)}, bf16[256,256]{1,0:T(8,128)(2,1)S(1)}, u32[]{:S(2)}, u32[]{:S(2)}) collective-permute-start(bf16[256,256]{1,0:T(8,128)(2,1)S(1)} %get-tuple-element.18.refs_0_), channel_id=1, source_target_pairs={{0,128},{16,144},{32,160},{48,176},{64,192},{80,208},{96,224},{112... | collective-permute-start | bytes 393224 | tf_op jit(solution)/shard_map/ppermute | solution.py:303
  74.2 5.3 %collective-permute-done.2.refs_3_ = bf16[256,256]{1,0:T(8,128)(2,1)S(1)} collective-permute-done((bf16[256,256]{1,0:T(8,128)(2,1)S(1)}, bf16[256,256]{1,0:T(8,128)(2,1)S(1)}, u32[]{:S(2)}, u32[]{:S(2)}) %collective-permute-start.2) | collective-permute-done | bytes 131104 | tf_op jit(solution)/shard_map/ppermute | solution.py:303
  79.5 2.7 %collective-permute-done.1.refs_2_ = bf16[256,256]{1,0:T(8,128)(2,1)S(1)} collective-permute-done((bf16[256,256]{1,0:T(8,128)(2,1)S(1)}, bf16[256,256]{1,0:T(8,128)(2,1)S(1)}, u32[]{:S(2)}, u32[]{:S(2)}) %collective-permute-start.1) | collective-permute-done | bytes 131104 | tf_op jit(solution)/shard_map/ppermute | solution.py:306
  82.3 1.9 %collective-permute-start.3 = (bf16[4,256,256]{2,1,0:T(8,128)(2,1)S(1)}, bf16[4,256,256]{2,1,0:T(8,128)(2,1)S(1)}, u32[]{:S(2)}, u32[]{:S(2)}) collective-permute-start(bf16[4,256,256]{2,1,0:T(8,128)(2,1)S(1)} %pad_maximum_fusion), channel_id=1, source_target_pairs={{0,16},{16,0},{32,48},{48,32},{64,80},{80,64},{96,112},{112,96},{1... | collective-permute-start | bytes 1572872 | tf_op jit(solution)/shard_map/ppermute | solution.py:309
  84.2 5.9 %collective-permute-start.4 = (bf16[256,128]{1,0:T(8,128)(2,1)S(1)}, bf16[256,128]{1,0:T(8,128)(2,1)S(1)}, u32[]{:S(2)}, u32[]{:S(2)}) collective-permute-start(bf16[256,128]{1,0:T(8,128)(2,1)S(1)} %get-tuple-element.19.refs_4_), channel_id=1, source_target_pairs={{0,32},{16,48},{32,0},{48,16},{64,96},{80,112},{96,64},{112,80},{1... | collective-permute-start | bytes 196616 | tf_op jit(solution)/shard_map/ppermute | solution.py:304
  90.1 2.7 %collective-permute-done.4.refs_5_ = bf16[256,128]{1,0:T(8,128)(2,1)S(1)} collective-permute-done((bf16[256,128]{1,0:T(8,128)(2,1)S(1)}, bf16[256,128]{1,0:T(8,128)(2,1)S(1)}, u32[]{:S(2)}, u32[]{:S(2)}) %collective-permute-start.4) | collective-permute-done | bytes 65568 | tf_op jit(solution)/shard_map/ppermute | solution.py:304
  92.9 6.9 %collective-permute-start.5 = (bf16[2,256,128]{2,1,0:T(8,128)(2,1)S(1)}, bf16[2,256,128]{2,1,0:T(8,128)(2,1)S(1)}, u32[]{:S(2)}, u32[]{:S(2)}) collective-permute-start(bf16[2,256,128]{2,1,0:T(8,128)(2,1)S(1)} %pad_maximum_fusion.1), channel_id=1, source_target_pairs={{0,64},{16,80},{32,96},{48,112},{64,0},{80,16},{96,32},{112,48},{1... | collective-permute-start | bytes 393224 | tf_op jit(solution)/shard_map/ppermute | solution.py:307
  99.7 6.4 %collective-permute-done.5.refs_6_ = bf16[2,256,128]{2,1,0:T(8,128)(2,1)S(1)} collective-permute-done((bf16[2,256,128]{2,1,0:T(8,128)(2,1)S(1)}, bf16[2,256,128]{2,1,0:T(8,128)(2,1)S(1)}, u32[]{:S(2)}, u32[]{:S(2)}) %collective-permute-start.5) | collective-permute-done | bytes 131104 | tf_op jit(solution)/shard_map/ppermute | solution.py:307
  106.1 4.0 %attend.1 = bf16[4,144,256]{2,1,0:T(8,128)(2,1)S(1)} custom-call(s32[4,1,256]{2,1,0:T(1,128)S(1)} %dynamic-slice_bitcast_fusion.qcode_ref, bf16[16,2048]{1,0:T(8,128)(2,1)S(1)} %select_convert_fusion.kcode_ref, bf16[4,256,256]{2,1,0:T(8,128)(2,1)S(1)} %collective-permute-done.3.other_ref, bf16[256,256]{1,0:T(8,128)(2,1)S(1)} %get-tuple-element.18.refs_0_, ...), custom_call_target="tpu_custom_call" | custom-call | tf_op jit(solution)/shard_map/attend/pallas_call | solution.py:188
  110.2 14.3 %all_to_all.20.part_ref = bf16[4,144,256]{2,1,0:T(8,128)(2,1)S(1)} all-to-all(bf16[4,144,256]{2,1,0:T(8,128)(2,1)S(1)} %attend.1), channel_id=1, replica_groups={{0,32,64,96},{16,48,80,112},{128,160,192,224},{144,176,208,240},{256,28..., dimensions={0} | all-to-all | bytes 589824 | tf_op jit(solution)/shard_map/all_to_all | solution.py:312
  124.5 0.2 combine.1
  124.8 20.9 %all_to_all.21.attended_ref = bf16[16,256,128]{2,1,0:T(8,128)(2,1)S(1)} all-to-all(bf16[16,256,128]{2,1,0:T(8,128)(2,1)S(1)} %combine.1), channel_id=1, replica_groups=mesh['seq'=32,'head'=16] {'head'}, dimensions={0} | all-to-all | bytes 2097152 | tf_op jit(solution)/shard_map/all_to_all | solution.py:314
  145.6 2.6 %output.1 = bf16[256,256]{1,0:T(8,128)(2,1)} custom-call(bf16[16,256,128]{2,1,0:T(8,128)(2,1)S(1)} %all_to_all.21.attended_ref, bf16[16,128,256]{2,1,0:T(8,128)(2,1)} %all-to-all-done.1.w_ref), custom_call_target="tpu_custom_call" | custom-call | tf_op jit(solution)/shard_map/output/pallas_call | solution.py:255
  (30 shorter events, 0.5 us)
Async XLA Ops:
  0.0 12.5 %copy-start.2 = (bf16[128,4096]{1,0:T(8,128)(2,1)S(1)}, bf16[128,4096]{1,0:T(8,128)(2,1)}, u32[]{:S(2)}) copy-start(bf16[128,4096]{1,0:T(8,128)(2,1)} %w_ref.1) | copy-start | bytes 3145732
  2.5 34.9 %all-to-all-start = ((bf16[16,256,256]{2,1,0:T(8,128)(2,1)}), bf16[16,256,256]{2,1,0:T(8,128)(2,1)}, u32[]{:S(2)}, u32[]{:S(2)}) async-start(bf16[16,256,256]{2,1,0:T(8,128)(2,1)} %spread.1), calls=%async_computation | async-start | bytes 4194304 | tf_op jit(solution)/shard_map/all_to_all | solution.py:293
  12.6 2.7 %copy-start = (bf16[16,128,256]{2,1,0:T(8,128)(2,1)}, bf16[16,128,256]{2,1,0:T(8,128)(2,1)S(1)}, u32[]{:S(2)}) copy-start(bf16[16,128,256]{2,1,0:T(8,128)(2,1)S(1)} %split.1) | copy-start | bytes 3145732
  12.6 2.3 %copy-start.1 = (bf16[4096,3,128]{2,0,1:T(8,128)(2,1)S(1)}, bf16[4096,3,128]{2,0,1:T(8,128)(2,1)}, u32[]{:S(2)}) copy-start(bf16[4096,3,128]{2,0,1:T(8,128)(2,1)} %param.9) | copy-start | bytes 9437188
  14.9 0.7 copy-start.6
  14.9 0.8 copy-start.4
  14.9 0.8 copy-start.5
  14.9 29.7 %copy-start.3 = (f32[4096]{0:T(1024)S(1)}, f32[4096]{0:T(1024)}, u32[]{:S(2)}) copy-start(f32[4096]{0:T(1024)} %param.8) | copy-start | bytes 49156
  37.4 72.8 %all-to-all-start.1 = ((bf16[16,128,256]{2,1,0:T(8,128)(2,1)}), bf16[16,128,256]{2,1,0:T(8,128)(2,1)}, u32[]{:S(2)}, u32[]{:S(2)}) async-start(bf16[16,128,256]{2,1,0:T(8,128)(2,1)} %copy-done), calls=%async_computation.1 | async-start | bytes 2097152 | tf_op jit(solution)/shard_map/all_to_all | solution.py:308
  48.6 30.9 %collective-permute-start.2 = (bf16[256,256]{1,0:T(8,128)(2,1)S(1)}, bf16[256,256]{1,0:T(8,128)(2,1)S(1)}, u32[]{:S(2)}, u32[]{:S(2)}) collective-permute-start(bf16[256,256]{1,0:T(8,128)(2,1)S(1)} %get-tuple-element.18.refs_0_), channel_id=1, source_target_pairs={{0,384},{16,400},{32,416},{48,432},{64,448},{80,464},{96,480},{112... | collective-permute-start | bytes 393224 | tf_op jit(solution)/shard_map/ppermute | solution.py:303
  61.4 20.8 %collective-permute-start.1 = (bf16[256,256]{1,0:T(8,128)(2,1)S(1)}, bf16[256,256]{1,0:T(8,128)(2,1)S(1)}, u32[]{:S(2)}, u32[]{:S(2)}) collective-permute-start(bf16[256,256]{1,0:T(8,128)(2,1)S(1)} %get-tuple-element.18.refs_0_), channel_id=1, source_target_pairs={{0,256},{16,272},{32,288},{48,304},{64,320},{80,336},{96,352},{112... | collective-permute-start | bytes 393224 | tf_op jit(solution)/shard_map/ppermute | solution.py:306
  66.3 15.9 %collective-permute-start = (bf16[256,256]{1,0:T(8,128)(2,1)S(1)}, bf16[256,256]{1,0:T(8,128)(2,1)S(1)}, u32[]{:S(2)}, u32[]{:S(2)}) collective-permute-start(bf16[256,256]{1,0:T(8,128)(2,1)S(1)} %get-tuple-element.18.refs_0_), channel_id=1, source_target_pairs={{0,128},{16,144},{32,160},{48,176},{64,192},{80,208},{96,224},{112... | collective-permute-start | bytes 393224 | tf_op jit(solution)/shard_map/ppermute | solution.py:303
  82.3 23.8 %collective-permute-start.3 = (bf16[4,256,256]{2,1,0:T(8,128)(2,1)S(1)}, bf16[4,256,256]{2,1,0:T(8,128)(2,1)S(1)}, u32[]{:S(2)}, u32[]{:S(2)}) collective-permute-start(bf16[4,256,256]{2,1,0:T(8,128)(2,1)S(1)} %pad_maximum_fusion), channel_id=1, source_target_pairs={{0,16},{16,0},{32,48},{48,32},{64,80},{80,64},{96,112},{112,96},{1... | collective-permute-start | bytes 1572872 | tf_op jit(solution)/shard_map/ppermute | solution.py:309
  84.2 8.6 %collective-permute-start.4 = (bf16[256,128]{1,0:T(8,128)(2,1)S(1)}, bf16[256,128]{1,0:T(8,128)(2,1)S(1)}, u32[]{:S(2)}, u32[]{:S(2)}) collective-permute-start(bf16[256,128]{1,0:T(8,128)(2,1)S(1)} %get-tuple-element.19.refs_4_), channel_id=1, source_target_pairs={{0,32},{16,48},{32,0},{48,16},{64,96},{80,112},{96,64},{112,80},{1... | collective-permute-start | bytes 196616 | tf_op jit(solution)/shard_map/ppermute | solution.py:304
  92.9 13.3 %collective-permute-start.5 = (bf16[2,256,128]{2,1,0:T(8,128)(2,1)S(1)}, bf16[2,256,128]{2,1,0:T(8,128)(2,1)S(1)}, u32[]{:S(2)}, u32[]{:S(2)}) collective-permute-start(bf16[2,256,128]{2,1,0:T(8,128)(2,1)S(1)} %pad_maximum_fusion.1), channel_id=1, source_target_pairs={{0,64},{16,80},{32,96},{48,112},{64,0},{80,16},{96,32},{112,48},{1... | collective-permute-start | bytes 393224 | tf_op jit(solution)/shard_map/ppermute | solution.py:307

commit v5 on v3

--- a/solution.py
+++ b/solution.py
@@ -71,17 +71,13 @@
     )(x, gain, w)
 
 
-def attend_kernel(qcode_ref, kcode_ref, other_ref, *refs):
-    count = other_ref.shape[0]
-    own_refs, q_refs = refs[:count], refs[count:-3]
-    out_ref, vt_ref, column_ref = refs[-3:]
+def visit(pieces, first, places, qcodes_ref, kcode_ref, q_refs, column_ref, vt_ref):
+    unit = jnp.where(lax.broadcasted_iota(jnp.int32, (16, 128), 0) == 0, 8.0, 1.0)
+    count = len(pieces)
+    block, far_block = places
     groups = len(q_refs)
-    far_block = lax.div(lax.axis_index("seq"), CORES * groups)
-    block = lax.rem(lax.div(lax.axis_index("seq"), CORES), groups)
-    pieces = list(own_refs) + [other_ref.at[j] for j in range(count)]
-    unit = jnp.where(lax.broadcasted_iota(jnp.int32, (16, 128), 0) == 0, 8.0, 1.0)
     column_ref[...] = lax.dot_general(
-        kcode_ref[...],
+        kcode_ref[:, first : first + count * ROWS],
         unit.astype(jnp.bfloat16),
         (((0,), (0,)), ((), ())),
         preferred_element_type=jnp.float32,
@@ -91,7 +87,7 @@
 
     for shift, q_ref in enumerate(q_refs):
         member = lax.rem(block + (groups - shift), groups)
-        qcode = qcode_ref[member]
+        qcode = qcodes_ref[member]
         qbase = (qcode & -8).astype(jnp.float32)
         qcode = qcode.astype(jnp.float32)
         queries = q_ref[...]
@@ -103,19 +99,65 @@
                 (((1,), (1,)), ((), ())),
                 preferred_element_type=jnp.float32,
             )
-            source = lax.rem(far_block + (count - j % count), count)
-            at = pl.multiple_of((j // count * count + source) * ROWS, ROWS)
+            at = pl.multiple_of(lax.rem(far_block + (count - j), count) * ROWS, ROWS)
             code = column_ref[pl.ds(at, ROWS), :]
             kcode = jnp.concatenate([code] * (ROWS // 128), axis=1)
             seen = (kcode < qbase) | (kcode == qcode)
             scores.append(jnp.where(seen, raw * SCALE, MASKED))
         scores = jnp.concatenate(scores, axis=0)
         best = jnp.max(scores, axis=0, keepdims=True)
-        weights = jnp.exp2(scores - best)
-        total = jnp.sum(weights, axis=0, keepdims=True)
-        mixed = jnp.dot(
-            vt_ref[...], weights.astype(jnp.bfloat16), preferred_element_type=jnp.float32
-        )
+        yield shift, member, best, scores
+
+
+def weigh(scores, best, vt_ref):
+    weights = jnp.exp2(scores - best)
+    total = jnp.sum(weights, axis=0, keepdims=True)
+    mixed = jnp.dot(vt_ref[...], weights.astype(jnp.bfloat16), preferred_element_type=jnp.float32)
+    return total, mixed
+
+
+def places_of(groups):
+    place = lax.axis_index("seq")
+    return lax.rem(lax.div(place, CORES), groups), lax.div(place, CORES * groups)
+
+
+def attend_own_kernel(qcode_ref, kcode_ref, *refs):
+    groups = qcode_ref.shape[0]
+    own_refs, q_refs = refs[:-groups - 4], refs[-groups - 4 : -4]
+    mixed_ref, stat_ref, vt_ref, column_ref = refs[-4:]
+    steps = visit(
+        own_refs, 0, places_of(groups), qcode_ref, kcode_ref, q_refs, column_ref, vt_ref
+    )
+    for shift, _, best, scores in steps:
+        total, mixed = weigh(scores, best, vt_ref)
+        mixed_ref[shift] = mixed
+        stat_ref[shift, 0:1] = best
+        stat_ref[shift, 1:2] = total
+
+
+def attend_other_kernel(qcode_ref, kcode_ref, other_ref, own_mixed_ref, own_stat_ref, *refs):
+    groups = qcode_ref.shape[0]
+    q_refs = refs[:groups]
+    out_ref, vt_ref, column_ref = refs[groups:]
+    count = other_ref.shape[0]
+    pieces = [other_ref.at[j] for j in range(count)]
+    steps = visit(
+        pieces,
+        count * ROWS,
+        places_of(groups),
+        qcode_ref,
+        kcode_ref,
+        q_refs,
+        column_ref,
+        vt_ref,
+    )
+    for shift, member, best, scores in steps:
+        own_best = own_stat_ref[shift, 0:1]
+        best = jnp.maximum(best, own_best)
+        total, mixed = weigh(scores, best, vt_ref)
+        factor = jnp.exp2(own_best - best)
+        total = total + factor * own_stat_ref[shift, 1:2]
+        mixed = mixed + factor * own_mixed_ref[shift]
         out_ref[member, :HD] = (mixed / total).astype(jnp.bfloat16)
         level = best + jnp.log2(total)
         high = level.astype(jnp.bfloat16).astype(jnp.float32)
@@ -129,20 +171,39 @@
         out_ref[member, HD:] = stats.astype(jnp.bfloat16)
 
 
-def attend(queries, qcode, own_kv, other_kv, kcode):
+def attend_own(queries, qcode, own_kv, kcode):
     groups = len(queries)
-    keys = kcode.shape[1]
-    return pl.pallas_call(
-        attend_kernel,
-        in_specs=[pl.BlockSpec(memory_space=pltpu.VMEM)] * (3 + len(own_kv) + groups),
+    keys = len(own_kv) * ROWS
+    return pl.pallas_call(
+        attend_own_kernel,
+        in_specs=[pl.BlockSpec(memory_space=pltpu.VMEM)] * (2 + len(own_kv) + groups),
+        out_shape=[
+            jax.ShapeDtypeStruct((groups, HD, ROWS), jnp.float32),
+            jax.ShapeDtypeStruct((groups, 8, ROWS), jnp.float32),
+        ],
+        scratch_shapes=[
+            pltpu.VMEM((HD, keys), jnp.bfloat16),
+            pltpu.VMEM((keys, 128), jnp.float32),
+        ],
+        compiler_params=pltpu.CompilerParams(vmem_limit_bytes=GRANT),
+        name="attend_own",
+    )(qcode, kcode, *own_kv, *queries)
+
+
+def attend_other(queries, qcode, other_kv, kcode, own_mixed, own_stat):
+    groups = len(queries)
+    keys = other_kv.shape[0] * ROWS
+    return pl.pallas_call(
+        attend_other_kernel,
+        in_specs=[pl.BlockSpec(memory_space=pltpu.VMEM)] * (5 + groups),
         out_shape=jax.ShapeDtypeStruct((groups, PART_ROWS, ROWS), jnp.bfloat16),
         scratch_shapes=[
             pltpu.VMEM((HD, keys), jnp.bfloat16),
             pltpu.VMEM((keys, 128), jnp.float32),
         ],
         compiler_params=pltpu.CompilerParams(vmem_limit_bytes=GRANT),
-        name="attend",
-    )(qcode, kcode, other_kv, *own_kv, *queries)
+        name="attend_other",
+    )(qcode, kcode, other_kv, own_mixed, own_stat, *queries)
 
 
 def combine_kernel(part_ref, out_ref):
@@ -258,7 +319,10 @@
         ]
         w_columns = lax.all_to_all(w_split, "head", 0, 0)
         other_kv = lax.ppermute(jnp.stack(own_kv), "seq", swap)
-        parts = attend(all_queries, query_code, own_kv, other_kv, key_code)
+        own_mixed, own_stat = attend_own(all_queries, query_code, own_kv, key_code)
+        parts = attend_other(
+            all_queries, query_code, other_kv, key_code, own_mixed, own_stat
+        )
         parts, w_columns = lax.optimization_barrier((parts, w_columns))
         parts = lax.all_to_all(parts, "seq", 0, 0, axis_index_groups=near)
         attended = combine(parts, n_head)

time: 142 us -> 144 us (1.014)
  waiting for transfers between devices: 32.8 us -> 34.7 us
    ppermute x3, waiting for transfers between devices: 3.93 us -> 5.47 us  [on_device(): lax.ppermute(queries, 'seq', along_block[k])]
    pallas_call x1 -> x2, Pallas kernels: 4.09 us -> 4.86 us  [the longest x1 2.47 us: attend_other(): pl.pallas_call(attend_other_kernel, in_specs=[pl.BlockSpec(memory_space=p...]
where the time goes in v5:
time: 144 us; the launch traced here: 142 us
  starting transfers between devices  59.4 us (41%)
  waiting for transfers between devices  34.7 us (24%)
  blocking collectives  31 us (22%)
  Pallas kernels  11.4 us (8%)
  local copies, waits for them, and re-layouts  5.44 us (4%)
    ppermute x3, starting transfers between devices, on_device(): own_kv[k] = lax.ppermute(kv, 'seq', across[k])  25.5 us
    all_to_all x1, waiting for transfers between devices, on_device(): gathered = lax.all_to_all(copies, 'head', 0, 0)  21.2 us
    all_to_all x1, blocking collectives, on_device(): all_attended = lax.all_to_all(attended, 'head', 0, 0)  19.6 us
    ppermute x3, starting transfers between devices, on_device(): lax.ppermute(queries, 'seq', along_block[k])  14.6 us
    all_to_all x1, blocking collectives, on_device(): parts = lax.all_to_all(parts, 'seq', 0, 0, axis_index_groups=near)  11.4 us
    all_to_all x1, starting transfers between devices, on_device(): gathered = lax.all_to_all(copies, 'head', 0, 0)  10.1 us
    ppermute x3, waiting for transfers between devices, on_device(): own_kv[k] = lax.ppermute(kv, 'seq', across[k])  8.07 us
    all_to_all x1, starting transfers between devices, on_device(): w_columns = lax.all_to_all(w_split, 'head', 0, 0)  7.23 us
  transfers between devices with their start and end apart: 9, of which 5 were waited for; matrix products, arithmetic and copies ran while one was open for 1% of the time, Pallas kernels for 6%

profile of v5, /device:TPU:6, one launch (start us, length us, event | category | flops | bytes accessed | tf_op | source)
XLA Modules:
  0.0 142.4 jit_solution(2053946373685372932)
XLA Ops:
  0.0 2.5 %broadcast_in_dim.28 = bf16[16,256,256]{2,1,0:T(8,128)(2,1)} broadcast(bf16[256,256]{1,0:T(8,128)(2,1)} %param.7), dimensions={1,2} | broadcast | bytes 2228224 | tf_op jit(solution)/shard_map/broadcast_in_dim | solution.py:303
  2.5 10.1 %all-to-all-start = ((bf16[16,256,256]{2,1,0:T(8,128)(2,1)}), bf16[16,256,256]{2,1,0:T(8,128)(2,1)}, u32[]{:S(2)}, u32[]{:S(2)}) async-start(bf16[16,256,256]{2,1,0:T(8,128)(2,1)} %broadcast_in_dim.28), calls=%async_computation | async-start | bytes 4194304 | tf_op jit(solution)/shard_map/all_to_all | solution.py:304
  12.6 0.6 gather_fusion
  13.4 2.3 %copy-done.1 = bf16[4096,3,128]{2,0,1:T(8,128)(2,1)S(1)} copy-done((bf16[4096,3,128]{2,0,1:T(8,128)(2,1)S(1)}, bf16[4096,3,128]{2,0,1:T(8,128)(2,1)}, u32[]{:S(2)}) %copy-start.1) | copy-done | bytes 3145752
  15.7 0.4 stage.1.w_ref
  16.2 21.2 %all-to-all-done.x_ref = bf16[16,256,256]{2,1,0:T(8,128)(2,1)} async-done(((bf16[16,256,256]{2,1,0:T(8,128)(2,1)}), bf16[16,256,256]{2,1,0:T(8,128)(2,1)}, u32[]{:S(2)}, u32[]{:S(2)}) %all-to-all-start) | async-done | bytes 2097184 | tf_op jit(solution)/shard_map/all_to_all | solution.py:304
  37.4 7.2 %all-to-all-start.1 = ((bf16[16,128,256]{2,1,0:T(8,128)(2,1)}), bf16[16,128,256]{2,1,0:T(8,128)(2,1)}, u32[]{:S(2)}, u32[]{:S(2)}) async-start(bf16[16,128,256]{2,1,0:T(8,128)(2,1)} %copy-done), calls=%async_computation.1 | async-start | bytes 2097152 | tf_op jit(solution)/shard_map/all_to_all | solution.py:320
  44.6 3.3 %project.1 = (bf16[256,128]{1,0:T(8,128)(2,1)S(1)}, bf16[256,256]{1,0:T(8,128)(2,1)S(1)}) custom-call(bf16[16,256,256]{2,1,0:T(8,128)(2,1)} %all-to-all-done.x_ref, f32[1,4096]{1,0:T(1,128)S(1)} %bitcast.25, bf16[3,4096,128]{2,1,0:T(8,128)(2,1)S(1)} %stage.1.w_ref), custom_call_target="tpu_custom_call" | custom-call | tf_op jit(solution)/shard_map/project/pallas_call | solution.py:61
  47.9 12.8 %collective-permute-start.2 = (bf16[256,256]{1,0:T(8,128)(2,1)S(1)}, bf16[256,256]{1,0:T(8,128)(2,1)S(1)}, u32[]{:S(2)}, u32[]{:S(2)}) collective-permute-start(bf16[256,256]{1,0:T(8,128)(2,1)S(1)} %get-tuple-element.20.refs_0_), channel_id=1, source_target_pairs={{0,384},{16,400},{32,416},{48,432},{64,448},{80,464},{96,480},{112... | collective-permute-start | bytes 393224 | tf_op jit(solution)/shard_map/ppermute | solution.py:314
  60.7 4.9 %collective-permute-start.1 = (bf16[256,256]{1,0:T(8,128)(2,1)S(1)}, bf16[256,256]{1,0:T(8,128)(2,1)S(1)}, u32[]{:S(2)}, u32[]{:S(2)}) collective-permute-start(bf16[256,256]{1,0:T(8,128)(2,1)S(1)} %get-tuple-element.20.refs_0_), channel_id=1, source_target_pairs={{0,256},{16,272},{32,288},{48,304},{64,320},{80,336},{96,352},{112... | collective-permute-start | bytes 393224 | tf_op jit(solution)/shard_map/ppermute | solution.py:316
  65.6 7.8 %collective-permute-start = (bf16[256,256]{1,0:T(8,128)(2,1)S(1)}, bf16[256,256]{1,0:T(8,128)(2,1)S(1)}, u32[]{:S(2)}, u32[]{:S(2)}) collective-permute-start(bf16[256,256]{1,0:T(8,128)(2,1)S(1)} %get-tuple-element.20.refs_0_), channel_id=1, source_target_pairs={{0,128},{16,144},{32,160},{48,176},{64,192},{80,208},{96,224},{112... | collective-permute-start | bytes 393224 | tf_op jit(solution)/shard_map/ppermute | solution.py:314
  73.5 5.3 %collective-permute-done.2.refs_3_ = bf16[256,256]{1,0:T(8,128)(2,1)S(1)} collective-permute-done((bf16[256,256]{1,0:T(8,128)(2,1)S(1)}, bf16[256,256]{1,0:T(8,128)(2,1)S(1)}, u32[]{:S(2)}, u32[]{:S(2)}) %collective-permute-start.2) | collective-permute-done | bytes 131104 | tf_op jit(solution)/shard_map/ppermute | solution.py:314
  78.8 2.8 %collective-permute-done.1.refs_2_ = bf16[256,256]{1,0:T(8,128)(2,1)S(1)} collective-permute-done((bf16[256,256]{1,0:T(8,128)(2,1)S(1)}, bf16[256,256]{1,0:T(8,128)(2,1)S(1)}, u32[]{:S(2)}, u32[]{:S(2)}) %collective-permute-start.1) | collective-permute-done | bytes 131104 | tf_op jit(solution)/shard_map/ppermute | solution.py:316
  81.6 1.9 %collective-permute-start.3 = (bf16[4,256,256]{2,1,0:T(8,128)(2,1)S(1)}, bf16[4,256,256]{2,1,0:T(8,128)(2,1)S(1)}, u32[]{:S(2)}, u32[]{:S(2)}) collective-permute-start(bf16[4,256,256]{2,1,0:T(8,128)(2,1)S(1)} %pad_maximum_fusion), channel_id=1, source_target_pairs={{0,16},{16,0},{32,48},{48,32},{64,80},{80,64},{96,112},{112,96},{1... | collective-permute-start | bytes 1572872 | tf_op jit(solution)/shard_map/ppermute | solution.py:321
  83.6 10.3 %collective-permute-start.6 = (bf16[256,128]{1,0:T(8,128)(2,1)S(1)}, bf16[256,128]{1,0:T(8,128)(2,1)S(1)}, u32[]{:S(2)}, u32[]{:S(2)}) collective-permute-start(bf16[256,128]{1,0:T(8,128)(2,1)S(1)} %get-tuple-element.21.refs_4_.refs_0_), channel_id=1, source_target_pairs={{0,96},{16,112},{32,0},{48,16},{64,32},{80,48},{96,64},{112,80},{1... | collective-permute-start | bytes 196616 | tf_op jit(solution)/shard_map/ppermute | solution.py:318
  93.8 1.9 %collective-permute-start.5 = (bf16[256,128]{1,0:T(8,128)(2,1)S(1)}, bf16[256,128]{1,0:T(8,128)(2,1)S(1)}, u32[]{:S(2)}, u32[]{:S(2)}) collective-permute-start(bf16[256,128]{1,0:T(8,128)(2,1)S(1)} %get-tuple-element.21.refs_4_.refs_0_), channel_id=1, source_target_pairs={{0,64},{16,80},{32,96},{48,112},{64,0},{80,16},{96,32},{112,48},{1... | collective-permute-start | bytes 196616 | tf_op jit(solution)/shard_map/ppermute | solution.py:318
  95.7 2.5 %collective-permute-start.4 = (bf16[256,128]{1,0:T(8,128)(2,1)S(1)}, bf16[256,128]{1,0:T(8,128)(2,1)S(1)}, u32[]{:S(2)}, u32[]{:S(2)}) collective-permute-start(bf16[256,128]{1,0:T(8,128)(2,1)S(1)} %get-tuple-element.21.refs_4_.refs_0_), channel_id=1, source_target_pairs={{0,32},{16,48},{32,64},{48,80},{64,96},{80,112},{96,0},{112,16},{1... | collective-permute-start | bytes 196616 | tf_op jit(solution)/shard_map/ppermute | solution.py:318
  98.2 2.6 %collective-permute-done.5.refs_6_.refs_2_ = bf16[256,128]{1,0:T(8,128)(2,1)S(1)} collective-permute-done((bf16[256,128]{1,0:T(8,128)(2,1)S(1)}, bf16[256,128]{1,0:T(8,128)(2,1)S(1)}, u32[]{:S(2)}, u32[]{:S(2)}) %collective-permute-start.5) | collective-permute-done | bytes 65568 | tf_op jit(solution)/shard_map/ppermute | solution.py:318
  100.9 2.8 %collective-permute-done.4.refs_5_.refs_1_ = bf16[256,128]{1,0:T(8,128)(2,1)S(1)} collective-permute-done((bf16[256,128]{1,0:T(8,128)(2,1)S(1)}, bf16[256,128]{1,0:T(8,128)(2,1)S(1)}, u32[]{:S(2)}, u32[]{:S(2)}) %collective-permute-start.4) | collective-permute-done | bytes 65568 | tf_op jit(solution)/shard_map/ppermute | solution.py:318
  103.7 2.4 %attend_own.1 = (f32[4,128,256]{2,1,0:T(8,128)S(1)}, f32[4,8,256]{2,1,0:T(8,128)S(1)}) custom-call(s32[4,1,256]{2,1,0:T(1,128)S(1)} %dynamic-slice_bitcast_fusion.qcode_ref, bf16[16,2048]{1,0:T(8,128)(2,1)S(1)} %select_convert_fusion.kcode_ref, bf16[256,256]{1,0:T(8,128)(2,1)S(1)} %get-tuple-element.20.refs_0_, ...), custom_call_target="tpu_custom_call" | custom-call | tf_op jit(solution)/shard_map/attend_own/pallas_call | solution.py:177
  106.1 2.5 %attend_other.1 = bf16[4,144,256]{2,1,0:T(8,128)(2,1)S(1)} custom-call(s32[4,1,256]{2,1,0:T(1,128)S(1)} %dynamic-slice_bitcast_fusion.qcode_ref, bf16[16,2048]{1,0:T(8,128)(2,1)S(1)} %select_convert_fusion.kcode_ref, bf16[4,256,256]{2,1,0:T(8,128)(2,1)S(1)} %collective-permute-done.3.other_ref, f32[4,128,256]{2,1,0:T(8,128)S(1)} %get-tuple-element.22.own_mixed_ref, ...), custom_call_target="tpu_custom_call" | custom-call | tf_op jit(solution)/shard_map/attend_other/pallas_call | solution.py:196
  108.6 11.4 %all_to_all.20.part_ref = bf16[4,144,256]{2,1,0:T(8,128)(2,1)S(1)} all-to-all(bf16[4,144,256]{2,1,0:T(8,128)(2,1)S(1)} %attend_other.1), channel_id=1, replica_groups={{0,32,64,96},{16,48,80,112},{128,160,192,224},{144,176,208,240},{256,28..., dimensions={0} | all-to-all | bytes 589824 | tf_op jit(solution)/shard_map/all_to_all | solution.py:327
  120.3 19.6 %all_to_all.21.attended_ref = bf16[16,256,128]{2,1,0:T(8,128)(2,1)S(1)} all-to-all(bf16[16,256,128]{2,1,0:T(8,128)(2,1)S(1)} %combine.1), channel_id=1, replica_groups=mesh['seq'=32,'head'=16] {'head'}, dimensions={0} | all-to-all | bytes 2097152 | tf_op jit(solution)/shard_map/all_to_all | solution.py:329
  139.8 2.6 %output.1 = bf16[256,256]{1,0:T(8,128)(2,1)} custom-call(bf16[16,256,128]{2,1,0:T(8,128)(2,1)S(1)} %all_to_all.21.attended_ref, bf16[16,128,256]{2,1,0:T(8,128)(2,1)} %all-to-all-done.1.w_ref), custom_call_target="tpu_custom_call" | custom-call | tf_op jit(solution)/shard_map/output/pallas_call | solution.py:263
  (32 shorter events, 0.6 us)
Async XLA Ops:
  0.0 12.6 %copy-start.6 = (s32[64]{0:T(128)S(1)}, s32[64]{0:T(128)}, u32[]{:S(2)}) copy-start(s32[64]{0:T(128)} %param.11) | copy-start | bytes 772
  0.0 12.6 %copy-start.4 = (s32[8192]{0:T(1024)S(1)}, s32[8192]{0:T(1024)}, u32[]{:S(2)}) copy-start(s32[8192]{0:T(1024)} %param.13) | copy-start | bytes 98308
  0.0 12.6 %copy-start.5 = (s32[8192]{0:T(1024)S(1)}, s32[8192]{0:T(1024)}, u32[]{:S(2)}) copy-start(s32[8192]{0:T(1024)} %param.12) | copy-start | bytes 98308
  0.0 13.3 %copy-start.2 = (bf16[128,4096]{1,0:T(8,128)(2,1)S(1)}, bf16[128,4096]{1,0:T(8,128)(2,1)}, u32[]{:S(2)}) copy-start(bf16[128,4096]{1,0:T(8,128)(2,1)} %w_ref.1) | copy-start | bytes 3145732
  2.5 34.9 %all-to-all-start = ((bf16[16,256,256]{2,1,0:T(8,128)(2,1)}), bf16[16,256,256]{2,1,0:T(8,128)(2,1)}, u32[]{:S(2)}, u32[]{:S(2)}) async-start(bf16[16,256,256]{2,1,0:T(8,128)(2,1)} %broadcast_in_dim.28), calls=%async_computation | async-start | bytes 4194304 | tf_op jit(solution)/shard_map/all_to_all | solution.py:304
  13.4 2.7 %copy-start = (bf16[16,128,256]{2,1,0:T(8,128)(2,1)}, bf16[16,128,256]{2,1,0:T(8,128)(2,1)S(1)}, u32[]{:S(2)}) copy-start(bf16[16,128,256]{2,1,0:T(8,128)(2,1)S(1)} %split.1) | copy-start | bytes 3145732
  13.4 2.3 %copy-start.1 = (bf16[4096,3,128]{2,0,1:T(8,128)(2,1)S(1)}, bf16[4096,3,128]{2,0,1:T(8,128)(2,1)}, u32[]{:S(2)}) copy-start(bf16[4096,3,128]{2,0,1:T(8,128)(2,1)} %param.9) | copy-start | bytes 9437188
  15.7 28.9 %copy-start.3 = (f32[4096]{0:T(1024)S(1)}, f32[4096]{0:T(1024)}, u32[]{:S(2)}) copy-start(f32[4096]{0:T(1024)} %param.8) | copy-start | bytes 49156
  37.4 71.2 %all-to-all-start.1 = ((bf16[16,128,256]{2,1,0:T(8,128)(2,1)}), bf16[16,128,256]{2,1,0:T(8,128)(2,1)}, u32[]{:S(2)}, u32[]{:S(2)}) async-start(bf16[16,128,256]{2,1,0:T(8,128)(2,1)} %copy-done), calls=%async_computation.1 | async-start | bytes 2097152 | tf_op jit(solution)/shard_map/all_to_all | solution.py:320
  47.9 30.8 %collective-permute-start.2 = (bf16[256,256]{1,0:T(8,128)(2,1)S(1)}, bf16[256,256]{1,0:T(8,128)(2,1)S(1)}, u32[]{:S(2)}, u32[]{:S(2)}) collective-permute-start(bf16[256,256]{1,0:T(8,128)(2,1)S(1)} %get-tuple-element.20.refs_0_), channel_id=1, source_target_pairs={{0,384},{16,400},{32,416},{48,432},{64,448},{80,464},{96,480},{112... | collective-permute-start | bytes 393224 | tf_op jit(solution)/shard_map/ppermute | solution.py:314
  60.7 20.8 %collective-permute-start.1 = (bf16[256,256]{1,0:T(8,128)(2,1)S(1)}, bf16[256,256]{1,0:T(8,128)(2,1)S(1)}, u32[]{:S(2)}, u32[]{:S(2)}) collective-permute-start(bf16[256,256]{1,0:T(8,128)(2,1)S(1)} %get-tuple-element.20.refs_0_), channel_id=1, source_target_pairs={{0,256},{16,272},{32,288},{48,304},{64,320},{80,336},{96,352},{112... | collective-permute-start | bytes 393224 | tf_op jit(solution)/shard_map/ppermute | solution.py:316
  65.6 15.9 %collective-permute-start = (bf16[256,256]{1,0:T(8,128)(2,1)S(1)}, bf16[256,256]{1,0:T(8,128)(2,1)S(1)}, u32[]{:S(2)}, u32[]{:S(2)}) collective-permute-start(bf16[256,256]{1,0:T(8,128)(2,1)S(1)} %get-tuple-element.20.refs_0_), channel_id=1, source_target_pairs={{0,128},{16,144},{32,160},{48,176},{64,192},{80,208},{96,224},{112... | collective-permute-start | bytes 393224 | tf_op jit(solution)/shard_map/ppermute | solution.py:314
  81.6 24.5 %collective-permute-start.3 = (bf16[4,256,256]{2,1,0:T(8,128)(2,1)S(1)}, bf16[4,256,256]{2,1,0:T(8,128)(2,1)S(1)}, u32[]{:S(2)}, u32[]{:S(2)}) collective-permute-start(bf16[4,256,256]{2,1,0:T(8,128)(2,1)S(1)} %pad_maximum_fusion), channel_id=1, source_target_pairs={{0,16},{16,0},{32,48},{48,32},{64,80},{80,64},{96,112},{112,96},{1... | collective-permute-start | bytes 1572872 | tf_op jit(solution)/shard_map/ppermute | solution.py:321
  83.6 14.7 %collective-permute-start.6 = (bf16[256,128]{1,0:T(8,128)(2,1)S(1)}, bf16[256,128]{1,0:T(8,128)(2,1)S(1)}, u32[]{:S(2)}, u32[]{:S(2)}) collective-permute-start(bf16[256,128]{1,0:T(8,128)(2,1)S(1)} %get-tuple-element.21.refs_4_.refs_0_), channel_id=1, source_target_pairs={{0,96},{16,112},{32,0},{48,16},{64,32},{80,48},{96,64},{112,80},{1... | collective-permute-start | bytes 196616 | tf_op jit(solution)/shard_map/ppermute | solution.py:318
  93.8 7.1 %collective-permute-start.5 = (bf16[256,128]{1,0:T(8,128)(2,1)S(1)}, bf16[256,128]{1,0:T(8,128)(2,1)S(1)}, u32[]{:S(2)}, u32[]{:S(2)}) collective-permute-start(bf16[256,128]{1,0:T(8,128)(2,1)S(1)} %get-tuple-element.21.refs_4_.refs_0_), channel_id=1, source_target_pairs={{0,64},{16,80},{32,96},{48,112},{64,0},{80,16},{96,32},{112,48},{1... | collective-permute-start | bytes 196616 | tf_op jit(solution)/shard_map/ppermute | solution.py:318
  95.7 8.0 %collective-permute-start.4 = (bf16[256,128]{1,0:T(8,128)(2,1)S(1)}, bf16[256,128]{1,0:T(8,128)(2,1)S(1)}, u32[]{:S(2)}, u32[]{:S(2)}) collective-permute-start(bf16[256,128]{1,0:T(8,128)(2,1)S(1)} %get-tuple-element.21.refs_4_.refs_0_), channel_id=1, source_target_pairs={{0,32},{16,48},{32,64},{48,80},{64,96},{80,112},{96,0},{112,16},{1... | collective-permute-start | bytes 196616 | tf_op jit(solution)/shard_map/ppermute | solution.py:318

commit v6 on v5

--- a/solution.py
+++ b/solution.py
@@ -314,9 +314,9 @@
             own_kv[k] = lax.ppermute(kv, "seq", across[k])
         for k in range(2, blocks - 1):
             own_kv[k] = lax.ppermute(kv, "seq", across[k])
-        all_queries = [queries] + [
-            lax.ppermute(queries, "seq", along_block[k]) for k in range(1, BLOCK_Z)
-        ]
+        all_queries = [queries]
+        for k in range(1, BLOCK_Z):
+            all_queries.append(lax.ppermute(queries, "seq", along_block[k]))
         w_columns = lax.all_to_all(w_split, "head", 0, 0)
         other_kv = lax.ppermute(jnp.stack(own_kv), "seq", swap)
         own_mixed, own_stat = attend_own(all_queries, query_code, own_kv, key_code)

time: 144 us -> 144 us (level)
  no operation moved by 1% of the time
where the time goes in v6:
time: 144 us; the launch traced here: 142 us
  starting transfers between devices  59.4 us (41%)
  waiting for transfers between devices  34.7 us (24%)
  blocking collectives  31 us (22%)
  Pallas kernels  11.4 us (8%)
  local copies, waits for them, and re-layouts  5.44 us (4%)
    ppermute x3, starting transfers between devices, on_device(): own_kv[k] = lax.ppermute(kv, 'seq', across[k])  25.5 us
    all_to_all x1, waiting for transfers between devices, on_device(): gathered = lax.all_to_all(copies, 'head', 0, 0)  21.2 us
    all_to_all x1, blocking collectives, on_device(): all_attended = lax.all_to_all(attended, 'head', 0, 0)  19.6 us
    ppermute x3, starting transfers between devices, on_device(): all_queries.append(lax.ppermute(queries, 'seq', along_block[k]))  14.6 us
    all_to_all x1, blocking collectives, on_device(): parts = lax.all_to_all(parts, 'seq', 0, 0, axis_index_groups=near)  11.4 us
    all_to_all x1, starting transfers between devices, on_device(): gathered = lax.all_to_all(copies, 'head', 0, 0)  10.1 us
    ppermute x3, waiting for transfers between devices, on_device(): own_kv[k] = lax.ppermute(kv, 'seq', across[k])  8.07 us
    all_to_all x1, starting transfers between devices, on_device(): w_columns = lax.all_to_all(w_split, 'head', 0, 0)  7.23 us
  transfers between devices with their start and end apart: 9, of which 5 were waited for; matrix products, arithmetic and copies ran while one was open for 1% of the time, Pallas kernels for 6%

profile of v6, /device:TPU:6, one launch (start us, length us, event | category | flops | bytes accessed | tf_op | source)
XLA Modules:
  0.0 142.4 jit_solution(2053946373685372932)
XLA Ops:
  0.0 2.5 %broadcast_in_dim.28 = bf16[16,256,256]{2,1,0:T(8,128)(2,1)} broadcast(bf16[256,256]{1,0:T(8,128)(2,1)} %param.7), dimensions={1,2} | broadcast | bytes 2228224 | tf_op jit(solution)/shard_map/broadcast_in_dim | solution.py:303
  2.5 10.1 %all-to-all-start = ((bf16[16,256,256]{2,1,0:T(8,128)(2,1)}), bf16[16,256,256]{2,1,0:T(8,128)(2,1)}, u32[]{:S(2)}, u32[]{:S(2)}) async-start(bf16[16,256,256]{2,1,0:T(8,128)(2,1)} %broadcast_in_dim.28), calls=%async_computation | async-start | bytes 4194304 | tf_op jit(solution)/shard_map/all_to_all | solution.py:304
  12.6 0.6 gather_fusion
  13.4 2.3 %copy-done.1 = bf16[4096,3,128]{2,0,1:T(8,128)(2,1)S(1)} copy-done((bf16[4096,3,128]{2,0,1:T(8,128)(2,1)S(1)}, bf16[4096,3,128]{2,0,1:T(8,128)(2,1)}, u32[]{:S(2)}) %copy-start.1) | copy-done | bytes 3145752
  15.7 0.4 stage.1.w_ref
  16.2 21.2 %all-to-all-done.x_ref = bf16[16,256,256]{2,1,0:T(8,128)(2,1)} async-done(((bf16[16,256,256]{2,1,0:T(8,128)(2,1)}), bf16[16,256,256]{2,1,0:T(8,128)(2,1)}, u32[]{:S(2)}, u32[]{:S(2)}) %all-to-all-start) | async-done | bytes 2097184 | tf_op jit(solution)/shard_map/all_to_all | solution.py:304
  37.4 7.2 %all-to-all-start.1 = ((bf16[16,128,256]{2,1,0:T(8,128)(2,1)}), bf16[16,128,256]{2,1,0:T(8,128)(2,1)}, u32[]{:S(2)}, u32[]{:S(2)}) async-start(bf16[16,128,256]{2,1,0:T(8,128)(2,1)} %copy-done), calls=%async_computation.1 | async-start | bytes 2097152 | tf_op jit(solution)/shard_map/all_to_all | solution.py:320
  44.6 3.3 %project.1 = (bf16[256,128]{1,0:T(8,128)(2,1)S(1)}, bf16[256,256]{1,0:T(8,128)(2,1)S(1)}) custom-call(bf16[16,256,256]{2,1,0:T(8,128)(2,1)} %all-to-all-done.x_ref, f32[1,4096]{1,0:T(1,128)S(1)} %bitcast.25, bf16[3,4096,128]{2,1,0:T(8,128)(2,1)S(1)} %stage.1.w_ref), custom_call_target="tpu_custom_call" | custom-call | tf_op jit(solution)/shard_map/project/pallas_call | solution.py:61
  47.9 12.8 %collective-permute-start.2 = (bf16[256,256]{1,0:T(8,128)(2,1)S(1)}, bf16[256,256]{1,0:T(8,128)(2,1)S(1)}, u32[]{:S(2)}, u32[]{:S(2)}) collective-permute-start(bf16[256,256]{1,0:T(8,128)(2,1)S(1)} %get-tuple-element.20.refs_0_), channel_id=1, source_target_pairs={{0,384},{16,400},{32,416},{48,432},{64,448},{80,464},{96,480},{112... | collective-permute-start | bytes 393224 | tf_op jit(solution)/shard_map/ppermute | solution.py:314
  60.7 4.9 %collective-permute-start.1 = (bf16[256,256]{1,0:T(8,128)(2,1)S(1)}, bf16[256,256]{1,0:T(8,128)(2,1)S(1)}, u32[]{:S(2)}, u32[]{:S(2)}) collective-permute-start(bf16[256,256]{1,0:T(8,128)(2,1)S(1)} %get-tuple-element.20.refs_0_), channel_id=1, source_target_pairs={{0,256},{16,272},{32,288},{48,304},{64,320},{80,336},{96,352},{112... | collective-permute-start | bytes 393224 | tf_op jit(solution)/shard_map/ppermute | solution.py:316
  65.6 7.8 %collective-permute-start = (bf16[256,256]{1,0:T(8,128)(2,1)S(1)}, bf16[256,256]{1,0:T(8,128)(2,1)S(1)}, u32[]{:S(2)}, u32[]{:S(2)}) collective-permute-start(bf16[256,256]{1,0:T(8,128)(2,1)S(1)} %get-tuple-element.20.refs_0_), channel_id=1, source_target_pairs={{0,128},{16,144},{32,160},{48,176},{64,192},{80,208},{96,224},{112... | collective-permute-start | bytes 393224 | tf_op jit(solution)/shard_map/ppermute | solution.py:314
  73.5 5.3 %collective-permute-done.2.refs_3_ = bf16[256,256]{1,0:T(8,128)(2,1)S(1)} collective-permute-done((bf16[256,256]{1,0:T(8,128)(2,1)S(1)}, bf16[256,256]{1,0:T(8,128)(2,1)S(1)}, u32[]{:S(2)}, u32[]{:S(2)}) %collective-permute-start.2) | collective-permute-done | bytes 131104 | tf_op jit(solution)/shard_map/ppermute | solution.py:314
  78.8 2.8 %collective-permute-done.1.refs_2_ = bf16[256,256]{1,0:T(8,128)(2,1)S(1)} collective-permute-done((bf16[256,256]{1,0:T(8,128)(2,1)S(1)}, bf16[256,256]{1,0:T(8,128)(2,1)S(1)}, u32[]{:S(2)}, u32[]{:S(2)}) %collective-permute-start.1) | collective-permute-done | bytes 131104 | tf_op jit(solution)/shard_map/ppermute | solution.py:316
  81.6 1.9 %collective-permute-start.3 = (bf16[4,256,256]{2,1,0:T(8,128)(2,1)S(1)}, bf16[4,256,256]{2,1,0:T(8,128)(2,1)S(1)}, u32[]{:S(2)}, u32[]{:S(2)}) collective-permute-start(bf16[4,256,256]{2,1,0:T(8,128)(2,1)S(1)} %pad_maximum_fusion), channel_id=1, source_target_pairs={{0,16},{16,0},{32,48},{48,32},{64,80},{80,64},{96,112},{112,96},{1... | collective-permute-start | bytes 1572872 | tf_op jit(solution)/shard_map/ppermute | solution.py:321
  83.6 10.3 %collective-permute-start.6 = (bf16[256,128]{1,0:T(8,128)(2,1)S(1)}, bf16[256,128]{1,0:T(8,128)(2,1)S(1)}, u32[]{:S(2)}, u32[]{:S(2)}) collective-permute-start(bf16[256,128]{1,0:T(8,128)(2,1)S(1)} %get-tuple-element.21.refs_4_.refs_0_), channel_id=1, source_target_pairs={{0,96},{16,112},{32,0},{48,16},{64,32},{80,48},{96,64},{112,80},{1... | collective-permute-start | bytes 196616 | tf_op jit(solution)/shard_map/ppermute | solution.py:319
  93.8 1.9 %collective-permute-start.5 = (bf16[256,128]{1,0:T(8,128)(2,1)S(1)}, bf16[256,128]{1,0:T(8,128)(2,1)S(1)}, u32[]{:S(2)}, u32[]{:S(2)}) collective-permute-start(bf16[256,128]{1,0:T(8,128)(2,1)S(1)} %get-tuple-element.21.refs_4_.refs_0_), channel_id=1, source_target_pairs={{0,64},{16,80},{32,96},{48,112},{64,0},{80,16},{96,32},{112,48},{1... | collective-permute-start | bytes 196616 | tf_op jit(solution)/shard_map/ppermute | solution.py:319
  95.7 2.5 %collective-permute-start.4 = (bf16[256,128]{1,0:T(8,128)(2,1)S(1)}, bf16[256,128]{1,0:T(8,128)(2,1)S(1)}, u32[]{:S(2)}, u32[]{:S(2)}) collective-permute-start(bf16[256,128]{1,0:T(8,128)(2,1)S(1)} %get-tuple-element.21.refs_4_.refs_0_), channel_id=1, source_target_pairs={{0,32},{16,48},{32,64},{48,80},{64,96},{80,112},{96,0},{112,16},{1... | collective-permute-start | bytes 196616 | tf_op jit(solution)/shard_map/ppermute | solution.py:319
  98.2 2.6 %collective-permute-done.5.refs_6_.refs_2_ = bf16[256,128]{1,0:T(8,128)(2,1)S(1)} collective-permute-done((bf16[256,128]{1,0:T(8,128)(2,1)S(1)}, bf16[256,128]{1,0:T(8,128)(2,1)S(1)}, u32[]{:S(2)}, u32[]{:S(2)}) %collective-permute-start.5) | collective-permute-done | bytes 65568 | tf_op jit(solution)/shard_map/ppermute | solution.py:319
  100.9 2.8 %collective-permute-done.4.refs_5_.refs_1_ = bf16[256,128]{1,0:T(8,128)(2,1)S(1)} collective-permute-done((bf16[256,128]{1,0:T(8,128)(2,1)S(1)}, bf16[256,128]{1,0:T(8,128)(2,1)S(1)}, u32[]{:S(2)}, u32[]{:S(2)}) %collective-permute-start.4) | collective-permute-done | bytes 65568 | tf_op jit(solution)/shard_map/ppermute | solution.py:319
  103.7 2.4 %attend_own.1 = (f32[4,128,256]{2,1,0:T(8,128)S(1)}, f32[4,8,256]{2,1,0:T(8,128)S(1)}) custom-call(s32[4,1,256]{2,1,0:T(1,128)S(1)} %dynamic-slice_bitcast_fusion.qcode_ref, bf16[16,2048]{1,0:T(8,128)(2,1)S(1)} %select_convert_fusion.kcode_ref, bf16[256,256]{1,0:T(8,128)(2,1)S(1)} %get-tuple-element.20.refs_0_, ...), custom_call_target="tpu_custom_call" | custom-call | tf_op jit(solution)/shard_map/attend_own/pallas_call | solution.py:177
  106.1 2.5 %attend_other.1 = bf16[4,144,256]{2,1,0:T(8,128)(2,1)S(1)} custom-call(s32[4,1,256]{2,1,0:T(1,128)S(1)} %dynamic-slice_bitcast_fusion.qcode_ref, bf16[16,2048]{1,0:T(8,128)(2,1)S(1)} %select_convert_fusion.kcode_ref, bf16[4,256,256]{2,1,0:T(8,128)(2,1)S(1)} %collective-permute-done.3.other_ref, f32[4,128,256]{2,1,0:T(8,128)S(1)} %get-tuple-element.22.own_mixed_ref, ...), custom_call_target="tpu_custom_call" | custom-call | tf_op jit(solution)/shard_map/attend_other/pallas_call | solution.py:196
  108.6 11.4 %all_to_all.20.part_ref = bf16[4,144,256]{2,1,0:T(8,128)(2,1)S(1)} all-to-all(bf16[4,144,256]{2,1,0:T(8,128)(2,1)S(1)} %attend_other.1), channel_id=1, replica_groups={{0,32,64,96},{16,48,80,112},{128,160,192,224},{144,176,208,240},{256,28..., dimensions={0} | all-to-all | bytes 589824 | tf_op jit(solution)/shard_map/all_to_all | solution.py:327
  120.3 19.6 %all_to_all.21.attended_ref = bf16[16,256,128]{2,1,0:T(8,128)(2,1)S(1)} all-to-all(bf16[16,256,128]{2,1,0:T(8,128)(2,1)S(1)} %combine.1), channel_id=1, replica_groups=mesh['seq'=32,'head'=16] {'head'}, dimensions={0} | all-to-all | bytes 2097152 | tf_op jit(solution)/shard_map/all_to_all | solution.py:329
  139.8 2.6 %output.1 = bf16[256,256]{1,0:T(8,128)(2,1)} custom-call(bf16[16,256,128]{2,1,0:T(8,128)(2,1)S(1)} %all_to_all.21.attended_ref, bf16[16,128,256]{2,1,0:T(8,128)(2,1)} %all-to-all-done.1.w_ref), custom_call_target="tpu_custom_call" | custom-call | tf_op jit(solution)/shard_map/output/pallas_call | solution.py:263
  (32 shorter events, 0.6 us)
Async XLA Ops:
  0.0 12.6 %copy-start.6 = (s32[64]{0:T(128)S(1)}, s32[64]{0:T(128)}, u32[]{:S(2)}) copy-start(s32[64]{0:T(128)} %param.11) | copy-start | bytes 772
  0.0 12.6 %copy-start.4 = (s32[8192]{0:T(1024)S(1)}, s32[8192]{0:T(1024)}, u32[]{:S(2)}) copy-start(s32[8192]{0:T(1024)} %param.13) | copy-start | bytes 98308
  0.0 12.6 %copy-start.5 = (s32[8192]{0:T(1024)S(1)}, s32[8192]{0:T(1024)}, u32[]{:S(2)}) copy-start(s32[8192]{0:T(1024)} %param.12) | copy-start | bytes 98308
  0.0 13.3 %copy-start.2 = (bf16[128,4096]{1,0:T(8,128)(2,1)S(1)}, bf16[128,4096]{1,0:T(8,128)(2,1)}, u32[]{:S(2)}) copy-start(bf16[128,4096]{1,0:T(8,128)(2,1)} %w_ref.1) | copy-start | bytes 3145732
  2.5 34.9 %all-to-all-start = ((bf16[16,256,256]{2,1,0:T(8,128)(2,1)}), bf16[16,256,256]{2,1,0:T(8,128)(2,1)}, u32[]{:S(2)}, u32[]{:S(2)}) async-start(bf16[16,256,256]{2,1,0:T(8,128)(2,1)} %broadcast_in_dim.28), calls=%async_computation | async-start | bytes 4194304 | tf_op jit(solution)/shard_map/all_to_all | solution.py:304
  13.4 2.7 %copy-start = (bf16[16,128,256]{2,1,0:T(8,128)(2,1)}, bf16[16,128,256]{2,1,0:T(8,128)(2,1)S(1)}, u32[]{:S(2)}) copy-start(bf16[16,128,256]{2,1,0:T(8,128)(2,1)S(1)} %split.1) | copy-start | bytes 3145732
  13.4 2.3 %copy-start.1 = (bf16[4096,3,128]{2,0,1:T(8,128)(2,1)S(1)}, bf16[4096,3,128]{2,0,1:T(8,128)(2,1)}, u32[]{:S(2)}) copy-start(bf16[4096,3,128]{2,0,1:T(8,128)(2,1)} %param.9) | copy-start | bytes 9437188
  15.7 28.9 %copy-start.3 = (f32[4096]{0:T(1024)S(1)}, f32[4096]{0:T(1024)}, u32[]{:S(2)}) copy-start(f32[4096]{0:T(1024)} %param.8) | copy-start | bytes 49156
  37.4 71.2 %all-to-all-start.1 = ((bf16[16,128,256]{2,1,0:T(8,128)(2,1)}), bf16[16,128,256]{2,1,0:T(8,128)(2,1)}, u32[]{:S(2)}, u32[]{:S(2)}) async-start(bf16[16,128,256]{2,1,0:T(8,128)(2,1)} %copy-done), calls=%async_computation.1 | async-start | bytes 2097152 | tf_op jit(solution)/shard_map/all_to_all | solution.py:320
  47.9 30.8 %collective-permute-start.2 = (bf16[256,256]{1,0:T(8,128)(2,1)S(1)}, bf16[256,256]{1,0:T(8,128)(2,1)S(1)}, u32[]{:S(2)}, u32[]{:S(2)}) collective-permute-start(bf16[256,256]{1,0:T(8,128)(2,1)S(1)} %get-tuple-element.20.refs_0_), channel_id=1, source_target_pairs={{0,384},{16,400},{32,416},{48,432},{64,448},{80,464},{96,480},{112... | collective-permute-start | bytes 393224 | tf_op jit(solution)/shard_map/ppermute | solution.py:314
  60.7 20.8 %collective-permute-start.1 = (bf16[256,256]{1,0:T(8,128)(2,1)S(1)}, bf16[256,256]{1,0:T(8,128)(2,1)S(1)}, u32[]{:S(2)}, u32[]{:S(2)}) collective-permute-start(bf16[256,256]{1,0:T(8,128)(2,1)S(1)} %get-tuple-element.20.refs_0_), channel_id=1, source_target_pairs={{0,256},{16,272},{32,288},{48,304},{64,320},{80,336},{96,352},{112... | collective-permute-start | bytes 393224 | tf_op jit(solution)/shard_map/ppermute | solution.py:316
  65.6 15.9 %collective-permute-start = (bf16[256,256]{1,0:T(8,128)(2,1)S(1)}, bf16[256,256]{1,0:T(8,128)(2,1)S(1)}, u32[]{:S(2)}, u32[]{:S(2)}) collective-permute-start(bf16[256,256]{1,0:T(8,128)(2,1)S(1)} %get-tuple-element.20.refs_0_), channel_id=1, source_target_pairs={{0,128},{16,144},{32,160},{48,176},{64,192},{80,208},{96,224},{112... | collective-permute-start | bytes 393224 | tf_op jit(solution)/shard_map/ppermute | solution.py:314
  81.6 24.5 %collective-permute-start.3 = (bf16[4,256,256]{2,1,0:T(8,128)(2,1)S(1)}, bf16[4,256,256]{2,1,0:T(8,128)(2,1)S(1)}, u32[]{:S(2)}, u32[]{:S(2)}) collective-permute-start(bf16[4,256,256]{2,1,0:T(8,128)(2,1)S(1)} %pad_maximum_fusion), channel_id=1, source_target_pairs={{0,16},{16,0},{32,48},{48,32},{64,80},{80,64},{96,112},{112,96},{1... | collective-permute-start | bytes 1572872 | tf_op jit(solution)/shard_map/ppermute | solution.py:321
  83.6 14.7 %collective-permute-start.6 = (bf16[256,128]{1,0:T(8,128)(2,1)S(1)}, bf16[256,128]{1,0:T(8,128)(2,1)S(1)}, u32[]{:S(2)}, u32[]{:S(2)}) collective-permute-start(bf16[256,128]{1,0:T(8,128)(2,1)S(1)} %get-tuple-element.21.refs_4_.refs_0_), channel_id=1, source_target_pairs={{0,96},{16,112},{32,0},{48,16},{64,32},{80,48},{96,64},{112,80},{1... | collective-permute-start | bytes 196616 | tf_op jit(solution)/shard_map/ppermute | solution.py:319
  93.8 7.1 %collective-permute-start.5 = (bf16[256,128]{1,0:T(8,128)(2,1)S(1)}, bf16[256,128]{1,0:T(8,128)(2,1)S(1)}, u32[]{:S(2)}, u32[]{:S(2)}) collective-permute-start(bf16[256,128]{1,0:T(8,128)(2,1)S(1)} %get-tuple-element.21.refs_4_.refs_0_), channel_id=1, source_target_pairs={{0,64},{16,80},{32,96},{48,112},{64,0},{80,16},{96,32},{112,48},{1... | collective-permute-start | bytes 196616 | tf_op jit(solution)/shard_map/ppermute | solution.py:319
  95.7 8.0 %collective-permute-start.4 = (bf16[256,128]{1,0:T(8,128)(2,1)S(1)}, bf16[256,128]{1,0:T(8,128)(2,1)S(1)}, u32[]{:S(2)}, u32[]{:S(2)}) collective-permute-start(bf16[256,128]{1,0:T(8,128)(2,1)S(1)} %get-tuple-element.21.refs_4_.refs_0_), channel_id=1, source_target_pairs={{0,32},{16,48},{32,64},{48,80},{64,96},{80,112},{96,0},{112,16},{1... | collective-permute-start | bytes 196616 | tf_op jit(solution)/shard_map/ppermute | solution.py:319
